TPU v7x, 32 devices: a whole 2x2x4 slice. The times are simulated.
32 devices in a mesh: rows: 4 (over y, x), wide: 8 (over z, core).
Axes of the slice: x: 2, y: 2, z: 4, core: 2. Of those that a mesh axis runs over, the one named last changes fastest.
Arguments:
- block_input: bfloat16 [4, 1024, 2048], P('rows', 'wide'), may hold values from -6 to 6
- out_grad: bfloat16 [4, 1024, 2048], P('rows', 'wide'), may hold values from -6 to 6
- segment_ids: int32 [4, 1024], P('rows'), may hold values from 0 to 7, as said below
- positions: int32 [4, 1024], P('rows', 'wide'), may hold values from 0 to 511, as said below
- norm_params: bfloat16 [4, 2048], P(None, ('rows', 'wide')), may hold values from -0.7 to 1.525
- w_qkv: bfloat16 [2048, 6144], P(('rows', 'wide')), may hold values from -0.125 to 0.125
- b_qkv: bfloat16 [6144], P(('rows', 'wide')), may hold values from -1.1953125 to 1.1953125
- w_out: bfloat16 [2048, 2048], P(('rows', 'wide')), may hold values from -1 to 1
- gate_up: bfloat16 [2, 2048, 5632], P(None, 'rows', 'wide'), may hold values from -0.125 to 0.125
- w_down: bfloat16 [5632, 2048], P('wide', 'rows'), may hold values from -0.078125 to 0.078125
- moment_norm: float32 [2, 4, 2048], P(None, None, ('rows', 'wide')), may hold values from -175 to 40000, as said below
- moment_qkv: float32 [2, 2048, 6144], P(None, ('rows', 'wide')), may hold values from -175 to 40000, as said below
- moment_bias: float32 [2, 6144], P(None, ('rows', 'wide')), may hold values from -175 to 40000, as said below
- moment_out: float32 [2, 2048, 2048], P(None, ('rows', 'wide')), may hold values from -175 to 40000, as said below
- moment_gate: float32 [2, 2, 2048, 5632], P(None, None, 'rows', 'wide'), may hold values from -175 to 40000, as said below
- moment_down: float32 [2, 5632, 2048], P(None, 'wide', 'rows'), may hold values from -175 to 40000, as said below
Outputs:
- block_output: bfloat16 [4, 1024, 2048], P('rows', 'wide')
- input_grad: float32 [4, 1024, 2048], P('rows', 'wide')
- grad_norms: float32 [4, 2048], P(None, ('rows', 'wide'))
- grad_qkv: float32 [2048, 6144], P(('rows', 'wide'))
- grad_bias: float32 [6144], P(('rows', 'wide'))
- grad_out: float32 [2048, 2048], P(('rows', 'wide'))
- grad_gate: float32 [2, 2048, 5632], P(None, 'rows', 'wide')
- grad_down: float32 [5632, 2048], P('wide', 'rows')
- step_norms: float32 [4, 2048], P(None, ('rows', 'wide'))
- step_qkv: float32 [2048, 6144], P(('rows', 'wide'))
- step_bias: float32 [6144], P(('rows', 'wide'))
- step_out: float32 [2048, 2048], P(('rows', 'wide'))
- step_gate: float32 [2, 2048, 5632], P(None, 'rows', 'wide')
- step_down: float32 [5632, 2048], P('wide', 'rows')
Inputs may be any that keep to these rules, and one draw needn't show every extreme that they name: `segment_ids`: within a row segment ids never fall, and every one of 0 to 7 occurs. positions[b, i] is i minus the index of the first token of the document of token i in row b. `moment_norm`: index 1 of the first dimension holds second moments, from 625 to 40000. `moment_qkv`: index 1 of the first dimension holds second moments, from 625 to 40000. `moment_bias`: index 1 of the first dimension holds second moments, from 625 to 40000. `moment_out`: index 1 of the first dimension holds second moments, from 625 to 40000. `moment_gate`: index 1 of the first dimension holds second moments, from 625 to 40000. `moment_down`: index 1 of the first dimension holds second moments, from 625 to 40000.
All inputs are finite; a program needn't handle non-finite values.
Results may differ from a plain program's by a relative error of at most 0.014.
Values may be sent and summed in bfloat16 or wider, within the bound.
No kernel may reach another device: no remote copies, remote signals or barrier semaphores. Data moves between devices by JAX's collectives and lax.ppermute only.
A program may use at most 256 MiB of HBM per device.

v0:
```python
import jax
import jax.numpy as jnp
from jax import lax
from jax.sharding import PartitionSpec as P

HEADS = 32
HEAD_DIM = 64
ROT_DIMS = 16


NORM_EPS = 1e-05
NEG_LARGE = -1e30
SCORE_SCALE = 0.125
ROPE_BASE = 10000.0
BETA_ONE = 0.9
BETA_TWO = 0.95
BIAS_FIRST = 0.999973438601112
BIAS_SECOND = 0.994079470779667
ADAM_EPS = 1e-08
DECAY_RATE = 0.1


def rotary_tables(positions):
    half_dims = ROT_DIMS // 2
    frequency = jnp.exp(
        jnp.arange(half_dims, dtype=jnp.float32) * (-2.0 * jnp.log(ROPE_BASE) / ROT_DIMS)
    )
    angles = positions.astype(jnp.float32)[:, None] * frequency[None, :]
    return (jnp.cos(angles)[:, None, :], jnp.sin(angles)[:, None, :])


def rotate(tensor, cosine, sine_part):
    half_dims = ROT_DIMS // 2
    leading = tensor[..., :half_dims]
    trailing = tensor[..., half_dims:ROT_DIMS]
    return jnp.concatenate(
        [
            leading * cosine - trailing * sine_part,
            trailing * cosine + leading * sine_part,
            tensor[..., ROT_DIMS:],
        ],
        axis=-1,
    )


def unrotate(tensor, cosine, sine_part):
    half_dims = ROT_DIMS // 2
    leading = tensor[..., :half_dims]
    trailing = tensor[..., half_dims:ROT_DIMS]
    return jnp.concatenate(
        [
            leading * cosine + trailing * sine_part,
            trailing * cosine - leading * sine_part,
            tensor[..., ROT_DIMS:],
        ],
        axis=-1,
    )


def layer_norm(tensor, norm_gain, norm_shift):
    center = tensor - jnp.mean(tensor, axis=-1, keepdims=True)
    inverse = lax.rsqrt(jnp.mean(center * center, axis=-1, keepdims=True) + NORM_EPS)
    normed = center * inverse
    return (normed * norm_gain + norm_shift, normed, inverse)


def norm_back(upstream_grad, normed, inverse, norm_gain):
    scaled = upstream_grad * norm_gain
    mean_grad = jnp.mean(scaled, axis=-1, keepdims=True)
    mean_proj = jnp.mean(scaled * normed, axis=-1, keepdims=True)
    grad_input = inverse * (scaled - mean_grad - normed * mean_proj)
    return (grad_input, jnp.sum(upstream_grad * normed, axis=0), jnp.sum(upstream_grad, axis=0))


def visible(segment_row, query_first, query_amount, key_first, key_amount):
    query_seg = lax.dynamic_slice_in_dim(segment_row, query_first, query_amount)
    key_seg = lax.dynamic_slice_in_dim(segment_row, key_first, key_amount)
    query_pos = query_first + jnp.arange(query_amount, dtype=jnp.int32)
    key_pos = key_first + jnp.arange(key_amount, dtype=jnp.int32)
    return (query_seg[:, None] == key_seg[None, :]) & (key_pos[None, :] <= query_pos[:, None])


def block_scores(queries, keys_blk, allowed):
    scores = (
        jnp.einsum("qhe,khe->hqk", queries, keys_blk, preferred_element_type=jnp.float32)
        * SCORE_SCALE
    )
    return jnp.where(allowed[None], scores, NEG_LARGE)


def key_slice(tensor, key_first, key_len):
    return lax.dynamic_slice_in_dim(tensor, key_first, key_len, 0)


def log_norms(queries, keys_all, segment_row, query_first):
    amount = queries.shape[0]
    key_len = min(512, keys_all.shape[0])

    def log_advance(running, block_no):
        key_first = block_no * key_len
        maxima, totals = running
        allowed = visible(segment_row, query_first, amount, key_first, key_len)
        scores = block_scores(queries, key_slice(keys_all, key_first, key_len), allowed)
        new_max = jnp.maximum(maxima, jnp.max(scores, axis=-1))
        weights = jnp.where(allowed[None], jnp.exp(scores - new_max[..., None]), 0.0)
        return ((new_max, totals * jnp.exp(maxima - new_max) + jnp.sum(weights, axis=-1)), None)

    start_state = (
        jnp.full((queries.shape[1], amount), NEG_LARGE, jnp.float32),
        jnp.zeros((queries.shape[1], amount), jnp.float32),
    )
    (maxima, totals), unused = lax.scan(
        log_advance, start_state, jnp.arange(keys_all.shape[0] // key_len, dtype=jnp.int32)
    )
    return maxima + jnp.log(totals)


def attend(queries, keys_all, values_all, segment_row, query_first, log_norm):
    amount = queries.shape[0]
    key_len = min(512, keys_all.shape[0])

    def attend_advance(running, block_no):
        key_first = block_no * key_len
        allowed = visible(segment_row, query_first, amount, key_first, key_len)
        scores = block_scores(queries, key_slice(keys_all, key_first, key_len), allowed)
        attn_probs = jnp.where(allowed[None], jnp.exp(scores - log_norm[..., None]), 0.0).astype(
            jnp.bfloat16
        )
        return (
            running
            + jnp.einsum(
                "hqk,khe->qhe",
                attn_probs,
                key_slice(values_all, key_first, key_len),
                preferred_element_type=jnp.float32,
            ),
            None,
        )

    result, unused = lax.scan(
        attend_advance,
        jnp.zeros(queries.shape, jnp.float32),
        jnp.arange(keys_all.shape[0] // key_len, dtype=jnp.int32),
    )
    return result


def back_pass(queries, grad_o, keys_all, values_all, segment_row, query_first, log_norm, row_delta):
    amount = queries.shape[0]
    key_len = min(512, keys_all.shape[0])

    def back_advance(running, block_no):
        key_first = block_no * key_len
        keys_blk = key_slice(keys_all, key_first, key_len)
        values_blk = key_slice(values_all, key_first, key_len)
        allowed = visible(segment_row, query_first, amount, key_first, key_len)
        scores = block_scores(queries, keys_blk, allowed)
        attn_probs = jnp.where(allowed[None], jnp.exp(scores - log_norm[..., None]), 0.0)
        grad_probs = jnp.einsum(
            "qhe,khe->hqk", grad_o, values_blk, preferred_element_type=jnp.float32
        )
        grad_scores = (attn_probs * (grad_probs - row_delta[..., None])).astype(jnp.bfloat16)
        updated = (
            running[0]
            + jnp.einsum("hqk,khe->qhe", grad_scores, keys_blk, preferred_element_type=jnp.float32)
            * SCORE_SCALE
        )
        key_acc, value_acc = running[1]
        key_piece = (
            jnp.einsum("hqk,qhe->khe", grad_scores, queries, preferred_element_type=jnp.float32)
            * SCORE_SCALE
        )
        value_piece = jnp.einsum(
            "hqk,qhe->khe",
            attn_probs.astype(jnp.bfloat16),
            grad_o,
            preferred_element_type=jnp.float32,
        )
        key_acc = lax.dynamic_update_slice_in_dim(
            key_acc, key_slice(key_acc, key_first, key_len) + key_piece, key_first, 0
        )
        value_acc = lax.dynamic_update_slice_in_dim(
            value_acc, key_slice(value_acc, key_first, key_len) + value_piece, key_first, 0
        )
        return ((updated, (key_acc, value_acc)), None)

    start_state = (
        jnp.zeros(queries.shape, jnp.float32),
        (jnp.zeros(keys_all.shape, jnp.float32), jnp.zeros(keys_all.shape, jnp.float32)),
    )
    result, unused = lax.scan(
        back_advance, start_state, jnp.arange(keys_all.shape[0] // key_len, dtype=jnp.int32)
    )
    return result


def adam_step(parameter, gradient, moments):
    first_moment = BETA_ONE * moments[0] + (1.0 - BETA_ONE) * gradient
    second_moment = BETA_TWO * moments[1] + (1.0 - BETA_TWO) * gradient * gradient
    return first_moment / BIAS_FIRST / (
        jnp.sqrt(second_moment / BIAS_SECOND) + ADAM_EPS
    ) + DECAY_RATE * parameter.astype(jnp.float32)


def shards(
    block_input,
    out_grad,
    segment_ids,
    positions,
    norm_params,
    w_qkv,
    b_qkv,
    w_out,
    gate_up,
    w_down,
    moment_norm,
    moment_qkv,
    moment_bias,
    moment_out,
    moment_gate,
    moment_down,
):
    residual = block_input[0].astype(jnp.float32)
    local_len = residual.shape[0]
    model_width = residual.shape[1]
    seq_len = local_len * lax.axis_size("wide")
    query_first = lax.axis_index("wide") * local_len
    segment_row = segment_ids[0]
    shaped = (local_len, HEADS, HEAD_DIM)
    norms_all, qkv_all, bias_all, out_all = (
        lax.all_gather(norm_params, ("rows", "wide"), axis=1, tiled=True),
        lax.all_gather(w_qkv, ("rows", "wide"), axis=0, tiled=True),
        lax.all_gather(b_qkv, ("rows", "wide"), axis=0, tiled=True),
        lax.all_gather(w_out, ("rows", "wide"), axis=0, tiled=True),
    )
    norm_vals = norms_all.astype(jnp.float32)
    normed_one, hat_one, inv_one = layer_norm(residual, norm_vals[0], norm_vals[1])
    normed_one_b = normed_one.astype(jnp.bfloat16)
    projected = jnp.dot(
        normed_one_b, qkv_all, preferred_element_type=jnp.float32
    ) + bias_all.astype(jnp.float32)
    cosine, sine_part = rotary_tables(positions[0])
    queries = rotate(projected[:, :model_width].reshape(shaped), cosine, sine_part).astype(
        jnp.bfloat16
    )
    keys_mine = rotate(
        projected[:, model_width : 2 * model_width].reshape(shaped), cosine, sine_part
    ).astype(jnp.bfloat16)
    values_mine = projected[:, 2 * model_width :].reshape(shaped).astype(jnp.bfloat16)
    keys_flat, values_flat = (
        lax.all_gather(keys_mine.reshape(local_len, model_width), "wide", axis=0, tiled=True),
        lax.all_gather(values_mine.reshape(local_len, model_width), "wide", axis=0, tiled=True),
    )
    keys_all = keys_flat.reshape(seq_len, HEADS, HEAD_DIM)
    values_all = values_flat.reshape(seq_len, HEADS, HEAD_DIM)
    log_norm = log_norms(queries, keys_all, segment_row, query_first)
    attended_f = attend(queries, keys_all, values_all, segment_row, query_first, log_norm)
    attended_b = attended_f.reshape(local_len, model_width).astype(jnp.bfloat16)
    after_attn = residual + jnp.dot(attended_b, out_all, preferred_element_type=jnp.float32)
    normed_two, hat_two, inv_two = layer_norm(after_attn, norm_vals[2], norm_vals[3])
    normed_two_b = normed_two.astype(jnp.bfloat16)
    gate_rows, down_rows = (
        lax.all_gather(gate_up, "rows", axis=1, tiled=True),
        lax.all_gather(w_down, "rows", axis=1, tiled=True),
    )
    tokens_all = lax.all_gather(normed_two_b, "wide", axis=0, tiled=True)
    gate_vals = jnp.einsum("td,gdf->gtf", tokens_all, gate_rows, preferred_element_type=jnp.float32)
    gate_part = gate_vals[0]
    up_part = gate_vals[1]
    sigmoid_g = jax.nn.sigmoid(gate_part)
    activated = gate_part * sigmoid_g
    hidden_b = (activated * up_part).astype(jnp.bfloat16)
    mlp_out = lax.psum_scatter(
        jnp.dot(hidden_b, down_rows, preferred_element_type=jnp.float32).astype(jnp.bfloat16),
        "wide",
        scatter_dimension=0,
        tiled=True,
    ).astype(jnp.float32)
    block_out = (after_attn + mlp_out).astype(jnp.bfloat16)
    upstream = out_grad[0].astype(jnp.float32)
    grads_all = lax.all_gather(out_grad[0], "wide", axis=0, tiled=True)
    grad_hidden = jnp.einsum("td,fd->tf", grads_all, down_rows, preferred_element_type=jnp.float32)
    down_grad = jnp.einsum("tf,td->fd", hidden_b, grads_all, preferred_element_type=jnp.float32)
    grad_gate_part = grad_hidden * up_part * sigmoid_g * (1.0 + gate_part * (1.0 - sigmoid_g))
    grad_up_part = grad_hidden * activated
    gate_grads_b = jnp.stack([grad_gate_part, grad_up_part]).astype(jnp.bfloat16)
    gate_grad = jnp.einsum(
        "td,gtf->gdf", tokens_all, gate_grads_b, preferred_element_type=jnp.float32
    )
    grad_normed_two = lax.psum_scatter(
        jnp.einsum(
            "gtf,gdf->td", gate_grads_b, gate_rows, preferred_element_type=jnp.float32
        ).astype(jnp.bfloat16),
        "wide",
        scatter_dimension=0,
        tiled=True,
    ).astype(jnp.float32)
    grad_after, gain_two, shift_two = norm_back(grad_normed_two, hat_two, inv_two, norm_vals[2])
    grad_after = grad_after + upstream
    grad_branch_b = grad_after.astype(jnp.bfloat16)
    out_grad_w = jnp.einsum(
        "tc,td->cd", attended_b, grad_branch_b, preferred_element_type=jnp.float32
    )
    grad_attended = (
        jnp.einsum("td,cd->tc", grad_branch_b, out_all, preferred_element_type=jnp.float32)
        .astype(jnp.bfloat16)
        .reshape(shaped)
    )
    row_delta = jnp.einsum("qhe,qhe->hq", grad_attended.astype(jnp.float32), attended_f)
    grad_queries, key_parts = back_pass(
        queries, grad_attended, keys_all, values_all, segment_row, query_first, log_norm, row_delta
    )
    grad_keys_flat, grad_values_flat = (
        lax.psum_scatter(
            key_parts[0].reshape(seq_len, model_width).astype(jnp.bfloat16),
            "wide",
            scatter_dimension=0,
            tiled=True,
        ).astype(jnp.float32),
        lax.psum_scatter(
            key_parts[1].reshape(seq_len, model_width).astype(jnp.bfloat16),
            "wide",
            scatter_dimension=0,
            tiled=True,
        ).astype(jnp.float32),
    )
    grad_keys = grad_keys_flat.reshape(shaped)
    grad_query_raw = unrotate(grad_queries, cosine, sine_part).reshape(local_len, model_width)
    grad_key_raw = unrotate(grad_keys, cosine, sine_part).reshape(local_len, model_width)
    grad_proj_b = jnp.concatenate([grad_query_raw, grad_key_raw, grad_values_flat], axis=1).astype(
        jnp.bfloat16
    )
    bias_grad = jnp.sum(grad_proj_b.astype(jnp.float32), axis=0)
    qkv_grad = jnp.einsum(
        "tc,tp->cp", normed_one_b, grad_proj_b, preferred_element_type=jnp.float32
    )
    grad_normed_one = jnp.einsum(
        "tp,cp->tc", grad_proj_b, qkv_all, preferred_element_type=jnp.float32
    )
    grad_input, gain_one, shift_one = norm_back(grad_normed_one, hat_one, inv_one, norm_vals[0])
    grad_input = grad_input + grad_after
    norm_grad = jnp.stack([gain_one, shift_one, gain_two, shift_two])
    grad_gate_s, grad_down_s = (
        lax.psum_scatter(
            gate_grad.astype(jnp.bfloat16), "rows", scatter_dimension=1, tiled=True
        ).astype(jnp.float32),
        lax.psum_scatter(
            down_grad.astype(jnp.bfloat16), "rows", scatter_dimension=1, tiled=True
        ).astype(jnp.float32),
    )
    grad_norms_s, grad_qkv_s, grad_bias_s, grad_out_s = (
        lax.psum_scatter(norm_grad, ("rows", "wide"), scatter_dimension=1, tiled=True),
        lax.psum_scatter(qkv_grad, ("rows", "wide"), scatter_dimension=0, tiled=True),
        lax.psum_scatter(bias_grad, ("rows", "wide"), scatter_dimension=0, tiled=True),
        lax.psum_scatter(out_grad_w, ("rows", "wide"), scatter_dimension=0, tiled=True),
    )
    step_norms = adam_step(norm_params, grad_norms_s, moment_norm)
    step_qkv = adam_step(w_qkv, grad_qkv_s, moment_qkv)
    step_bias = adam_step(b_qkv, grad_bias_s, moment_bias)
    step_out = adam_step(w_out, grad_out_s, moment_out)
    step_gate = adam_step(gate_up, grad_gate_s, moment_gate)
    step_down = adam_step(w_down, grad_down_s, moment_down)
    return (
        block_out[None],
        grad_input[None],
        grad_norms_s,
        grad_qkv_s,
        grad_bias_s,
        grad_out_s,
        grad_gate_s,
        grad_down_s,
        step_norms,
        step_qkv,
        step_bias,
        step_out,
        step_gate,
        step_down,
    )


def solution(mesh):
    placed = (
        P("rows", "wide", None),
        P("rows", "wide", None),
        P("rows", None),
        P("rows", "wide"),
        P(None, ("rows", "wide")),
        P(("rows", "wide"), None),
        P(("rows", "wide")),
        P(("rows", "wide"), None),
        P(None, "rows", "wide"),
        P("wide", "rows"),
        P(None, None, ("rows", "wide")),
        P(None, ("rows", "wide"), None),
        P(None, ("rows", "wide")),
        P(None, ("rows", "wide"), None),
        P(None, None, "rows", "wide"),
        P(None, "wide", "rows"),
    )
    return jax.shard_map(
        shards,
        mesh=mesh,
        in_specs=placed,
        out_specs=(
            P("rows", "wide", None),
            P("rows", "wide", None),
            P(None, ("rows", "wide")),
            P(("rows", "wide"), None),
            P(("rows", "wide")),
            P(("rows", "wide"), None),
            P(None, "rows", "wide"),
            P("wide", "rows"),
            P(None, ("rows", "wide")),
            P(("rows", "wide"), None),
            P(("rows", "wide")),
            P(("rows", "wide"), None),
            P(None, "rows", "wide"),
            P("wide", "rows"),
        ),
        check_vma=False,
    )
```

profile of v0, /device:TPU:9, one launch (start us, length us, event | category | flops | bytes accessed | tf_op | source)
XLA Modules:
  0.0 1738.5 jit_solution(9257747985766800197)
XLA Ops:
  8.8 41.4 %all-reduce = bf16[6144]{0:T(1024)(128)(2,1)S(1)} all-reduce(bf16[6144]{0:T(1024)(128)(2,1)S(1)} %dynamic-update-slice), channel_id=1, replica_groups=mesh['rows'=4,'wide'=8] {'rows','wide'}, use_global_device_ids=true, to_apply=%add | all-reduce | flops 6144 | bytes 24576
  50.3 38.8 %all-gather.1 = bf16[32,64,4]{1,2,0:T(4,128)(2,1)S(1)} all-gather(bf16[1,64,4]{1,2,0:T(4,128)(2,1)} %bitcast.338), channel_id=1, replica_groups=mesh['rows'=4,'wide'=8] {'rows','wide'}, dimensions={0}, use_global_device_ids=true | all-gather | bytes 16896 | tf_op jit(solution)/shard_map/all_gather | solution.py:231
  91.7 75.2 %all-gather.11.cloned.1.call-done = bf16[2048,6144]{1,0:T(8,128)(2,1)} async-done(((bf16[64,6144]{1,0:T(8,128)(2,1)}), bf16[2048,6144]{1,0:T(8,128)(2,1)}) %all-gather.11.cloned.1.call-update) | async-done | bytes 25165840 | tf_op jit(solution)/shard_map/all_gather | solution.py:232
  167.0 10.3 convolution_add_fusion
  185.7 38.3 %all-gather.13.cloned.1.call-done = bf16[1024,2048]{1,0:T(8,128)(2,1)} async-done(((bf16[128,2048]{1,0:T(8,128)(2,1)}), bf16[1024,2048]{1,0:T(8,128)(2,1)}) %all-gather.13.cloned.1.call-update) | async-done | bytes 4194320 | tf_op jit(solution)/shard_map/all_gather | solution.py:252
  230.4 42.6 %all-gather.15.cloned.1.call-done = bf16[1024,2048]{0,1:T(8,128)(2,1)} async-done(((bf16[128,2048]{0,1:T(8,128)(2,1)}), bf16[1024,2048]{0,1:T(8,128)(2,1)}) %all-gather.15.cloned.1.call-update) | async-done | bytes 4194320 | tf_op jit(solution)/shard_map/all_gather | solution.py:251
  273.0 14.3 while.45
  287.3 14.0 while.46
  301.4 51.4 %all-gather.17.cloned.1.call-done = bf16[2048,2048]{1,0:T(8,128)(2,1)} async-done(((bf16[64,2048]{1,0:T(8,128)(2,1)}), bf16[2048,2048]{1,0:T(8,128)(2,1)}) %all-gather.17.cloned.1.call-update) | async-done | bytes 8388624 | tf_op jit(solution)/shard_map/all_gather | solution.py:234
  360.7 57.6 %all-gather.21.cloned.1.call-done = bf16[2,2048,704]{1,2,0:T(8,128)(2,1)} async-done(((bf16[2,512,704]{1,2,0:T(8,128)(2,1)}), bf16[2,2048,704]{1,2,0:T(8,128)(2,1)}) %all-gather.21.cloned.1.call-update) | async-done | bytes 5767184 | tf_op jit(solution)/shard_map/all_gather | solution.py:263
  418.3 48.1 %all-gather.19.cloned.1.call-done = bf16[1024,2048]{1,0:T(8,128)(2,1)} async-done(((bf16[128,2048]{1,0:T(8,128)(2,1)}), bf16[1024,2048]{1,0:T(8,128)(2,1)}) %all-gather.19.cloned.1.call-update) | async-done | bytes 4194320 | tf_op jit(solution)/shard_map/all_gather | solution.py:266
  466.4 11.1 fusion.90
  477.5 32.3 %all-gather.23.cloned.1.call-done = bf16[704,2048]{1,0:T(8,128)(2,1)} async-done(((bf16[704,512]{1,0:T(8,128)(2,1)}), bf16[704,2048]{1,0:T(8,128)(2,1)}) %all-gather.23.cloned.1.call-update) | async-done | bytes 2883600 | tf_op jit(solution)/shard_map/all_gather | solution.py:264
  509.8 47.7 %all-gather.25.cloned.1.call-done = bf16[1,1024,2048]{2,1,0:T(8,128)(2,1)} async-done(((bf16[1,128,2048]{2,1,0:T(8,128)(2,1)}), bf16[1,1024,2048]{2,1,0:T(8,128)(2,1)}) %all-gather.25.cloned.1.call-update) | async-done | bytes 4194320 | tf_op jit(solution)/shard_map/all_gather | solution.py:281
  557.4 10.2 fusion.111
  569.2 8.6 bitcast_convert_fusion
  578.3 7.8 convolution_convert_fusion
  586.2 40.1 %reduce-scatter.18.cloned.1.call-done = bf16[128,2048]{1,0:T(8,128)(2,1)} async-done(((bf16[1024,2048]{1,0:T(8,128)(2,1)}), bf16[128,2048]{1,0:T(8,128)(2,1)}) %reduce-scatter.18.cloned.1.call-update) | async-done | bytes 524304 | tf_op jit(solution)/shard_map/reduce_scatter | solution.py:290
  628.4 48.2 %reduce-scatter.16.cloned.1.call-done = bf16[128,2048]{1,0:T(8,128)(2,1)} async-done(((bf16[1024,2048]{1,0:T(8,128)(2,1)}), bf16[128,2048]{1,0:T(8,128)(2,1)}) %reduce-scatter.16.cloned.1.call-update) | async-done | bytes 524304 | tf_op jit(solution)/shard_map/reduce_scatter | solution.py:273
  697.5 45.6 %while.47 = (s32[]{:T(128)}, f32[128,32,64]{0,2,1:T(8,128)S(1)}, f32[1024,32,64]{0,2,1:T(8,128)}, f32[1024,32,64]{0,2,1:T(8,128)}, s32[2]{0:T(128)S(1)}, /*index...) while((s32[]{:T(128)}, f32[128,32,64]{0,2,1:T(8,128)S(1)}, ...), condition=%wide.region_15.16_spmd.clone, body=%wide.region_14.15_spmd.clone.sunk | while | flops 1371472512 | bytes 98824008 | solution.py:191
  776.0 10.6 convert_bitcast_fusion
  786.7 17.2 reduce-scatter.28.cloned.1.call-done
  807.2 47.1 %reduce-scatter.30.cloned.1.call-done = bf16[128,2048]{1,0:T(8,128)(2,1)} async-done(((bf16[1024,2048]{1,0:T(8,128)(2,1)}), bf16[128,2048]{1,0:T(8,128)(2,1)}) %reduce-scatter.30.cloned.1.call-update) | async-done | bytes 524304
  857.8 14.8 fusion.126
  874.0 8.1 fusion.142
  883.2 21.6 %fusion.156 = f32[2048,6144]{1,0:T(8,128)} fusion(bf16[1,128,2048]{2,1,0:T(8,128)(2,1)S(1)} %copy-done.2, f32[2048]{0:T(1024)S(1)} %bitcast.326, f32[2048]{0:T(1024)S(1)} %bitcast.323, f32[128]{0:T(128)S(1)} %copy-done.33, f32[128]{0:T(128)S(1)} %copy-done.29, bf16[128,2048]{0,1:T(8,128)(2,1)S(1)} %copy.89, bf16[128,2048]{0,1:T(8,128)(2,1)S(1)} %bitcast.309, ...), kind=kOutput, calls=%fused_computation.218 | convolution fusion | flops 3227516928 | bytes 52446208 | tf_op jit(solution)/shard_map/tc,tp->cp/dot_general | solution.py:334
  911.0 57.1 %reduce-scatter.24.cloned.1.call-done = bf16[2,512,704]{1,2,0:T(8,128)(2,1)} async-done(((bf16[2,2048,704]{1,2,0:T(8,128)(2,1)}), bf16[2,512,704]{1,2,0:T(8,128)(2,1)}) %reduce-scatter.24.cloned.1.call-update) | async-done | bytes 1441808 | tf_op jit(solution)/shard_map/reduce_scatter | solution.py:344
  968.1 7.8 fusion.87
  976.4 39.1 %all-reduce.1 = f32[6144]{0:T(1024)S(1)} all-reduce(f32[6144]{0:T(1024)S(1)} %convert_reduce_fusion), channel_id=9, replica_groups=mesh['rows'=4,'wide'=8] {'rows','wide'}, use_global_device_ids=true, to_apply=%region_27.28.clone | all-reduce | flops 6144 | bytes 49152
  1020.9 73.6 %reduce-scatter.32.cloned.1.call-done = f32[64,4]{1,0:T(8,128)} async-done(((f32[2048,4]{1,0:T(8,128)}), f32[64,4]{1,0:T(8,128)}) %reduce-scatter.32.cloned.1.call-update) | async-done | bytes 1040
  1095.9 191.7 %reduce-scatter.22.cloned.1.call-done = f32[64,2048]{1,0:T(8,128)} async-done(((f32[2048,2048]{1,0:T(8,128)}), f32[64,2048]{1,0:T(8,128)}) %reduce-scatter.22.cloned.1.call-update) | async-done | bytes 524304 | tf_op jit(solution)/shard_map/reduce_scatter | solution.py:355
  1290.2 436.6 %reduce-scatter.20.cloned.1.call-done = f32[64,6144]{1,0:T(8,128)} async-done(((f32[2048,6144]{1,0:T(8,128)}), f32[64,6144]{1,0:T(8,128)}) %reduce-scatter.20.cloned.1.call-update) | async-done | bytes 1572880 | tf_op jit(solution)/shard_map/reduce_scatter | solution.py:353
  (249 shorter events, 184.0 us)
Async XLA Ops:
  7.2 159.8 %all-gather.11.cloned.1.call-start = ((), (), s32[]{:S(2)}) async-start(), calls=%async_computation.9 | async-start | bytes 25952256 | tf_op jit(solution)/shard_map/all_gather | solution.py:232
  7.9 216.1 %all-gather.13.cloned.1.call-start = ((), (), s32[]{:S(2)}) async-start(), calls=%async_computation.10 | async-start | bytes 4718592 | tf_op jit(solution)/shard_map/all_gather | solution.py:252
  90.3 87.0 %copy-start.28 = (f32[128]{0:T(128)}, f32[128]{0:T(128)S(1)}, u32[]{:S(2)}) copy-start(f32[128]{0:T(128)S(1)} %broadcast_multiply_fusion.5) | copy-start | bytes 1540
  91.7 85.6 %copy-start.32 = (f32[128]{0:T(128)}, f32[128]{0:T(128)S(1)}, u32[]{:S(2)}) copy-start(f32[128]{0:T(128)S(1)} %add_rsqrt_fusion.1) | copy-start | bytes 1540
  91.7 85.6 %copy-start.19 = (f32[1,2048]{1,0:T(1,128)}, f32[1,2048]{1,0:T(1,128)S(1)}, u32[]{:S(2)}) copy-start(f32[1,2048]{1,0:T(1,128)S(1)} %get-tuple-element.637) | copy-start | bytes 24580
  91.7 85.6 %copy-start.21 = (f32[1,2048]{1,0:T(1,128)}, f32[1,2048]{1,0:T(1,128)S(1)}, u32[]{:S(2)}) copy-start(f32[1,2048]{1,0:T(1,128)S(1)} %get-tuple-element.636) | copy-start | bytes 24580
  178.2 94.8 %all-gather.15.cloned.1.call-start = ((), (), s32[]{:S(2)}) async-start(), calls=%async_computation.11 | async-start | bytes 4718592 | tf_op jit(solution)/shard_map/all_gather | solution.py:251
  184.1 168.7 %all-gather.17.cloned.1.call-start = ((), (), s32[]{:S(2)}) async-start(), calls=%async_computation.12 | async-start | bytes 8650752 | tf_op jit(solution)/shard_map/all_gather | solution.py:234
  184.7 233.7 %all-gather.21.cloned.1.call-start = ((), (), s32[]{:S(2)}) async-start(), calls=%async_computation.14 | async-start | bytes 7208960 | tf_op jit(solution)/shard_map/all_gather | solution.py:263
  185.3 281.2 %all-gather.19.cloned.1.call-start = ((), (), s32[]{:S(2)}) async-start(), calls=%async_computation.13 | async-start | bytes 4718592 | tf_op jit(solution)/shard_map/all_gather | solution.py:266
  287.3 65.5 %copy-start.1 = (bf16[1,128,2048]{2,1,0:T(8,128)(2,1)S(1)}, bf16[1,128,2048]{2,1,0:T(8,128)(2,1)}, u32[]{:S(2)}) copy-start(bf16[1,128,2048]{2,1,0:T(8,128)(2,1)} %param.22) | copy-start | bytes 1572868
  301.4 56.1 %copy-start.5 = (bf16[128,32,64]{0,2,1:T(8,128)(2,1)}, bf16[128,32,64]{0,2,1:T(8,128)(2,1)S(1)}, u32[]{:S(2)}) copy-start(bf16[128,32,64]{0,2,1:T(8,128)(2,1)S(1)} %convert_element_type.145) | copy-start | bytes 1572868
  358.9 150.8 %all-gather.23.cloned.1.call-start = ((), (), s32[]{:S(2)}) async-start(), calls=%async_computation.15 | async-start | bytes 3604480 | tf_op jit(solution)/shard_map/all_gather | solution.py:264
  359.7 197.8 %all-gather.25.cloned.1.call-start = ((), (), s32[]{:S(2)}) async-start(), calls=%async_computation.22 | async-start | bytes 4718592 | tf_op jit(solution)/shard_map/all_gather | solution.py:281
  360.4 265.9 %reduce-scatter.18.cloned.1.call-start = ((), (), s32[]{:S(2)}) async-start(), calls=%async_computation.17 | async-start | bytes 4718592 | tf_op jit(solution)/shard_map/reduce_scatter | solution.py:290
  577.8 98.8 %reduce-scatter.16.cloned.1.call-start = ((), (), s32[]{:S(2)}) async-start(), calls=%async_computation.16 | async-start | bytes 4718592 | tf_op jit(solution)/shard_map/reduce_scatter | solution.py:273
  586.1 90.5 %copy-start.16 = (bf16[1,128,2048]{2,1,0:T(8,128)(2,1)S(1)}, bf16[1,128,2048]{2,1,0:T(8,128)(2,1)}, u32[]{:S(2)}) copy-start(bf16[1,128,2048]{2,1,0:T(8,128)(2,1)} %param.23) | copy-start | bytes 1572868
  586.2 217.8 %reduce-scatter.28.cloned.1.call-start = ((), (), s32[]{:S(2)}) async-start(), calls=%async_computation.23 | async-start | bytes 4718592
  755.6 98.7 %reduce-scatter.30.cloned.1.call-start = ((), (), s32[]{:S(2)}) async-start(), calls=%async_computation.24 | async-start | bytes 4718592
  768.3 137.7 %reduce-scatter.26.cloned.1.call-start = ((), (), s32[]{:S(2)}) async-start(), calls=%async_computation.21 | async-start | bytes 3604480 | tf_op jit(solution)/shard_map/reduce_scatter | solution.py:347
  775.9 192.2 %reduce-scatter.24.cloned.1.call-start = ((), (), s32[]{:S(2)}) async-start(), calls=%async_computation.20 | async-start | bytes 7208960 | tf_op jit(solution)/shard_map/reduce_scatter | solution.py:344
  786.6 69.0 %copy-start.25 = (f32[128,8]{0,1:T(8,128)S(1)}, f32[128,8]{0,1:T(8,128)}, u32[]{:S(2)}) copy-start(f32[128,8]{0,1:T(8,128)} %copy-done.24) | copy-start | bytes 12292
  786.6 69.0 %copy-start.27 = (f32[128,8]{0,1:T(8,128)S(1)}, f32[128,8]{0,1:T(8,128)}, u32[]{:S(2)}) copy-start(f32[128,8]{0,1:T(8,128)} %copy-done.26) | copy-start | bytes 12292
  786.6 307.9 %reduce-scatter.32.cloned.1.call-start = ((), (), s32[]{:S(2)}) async-start(), calls=%async_computation.25 | async-start | bytes 1081344
  874.0 413.7 %reduce-scatter.22.cloned.1.call-start = ((), (), s32[]{:S(2)}) async-start(), calls=%async_computation.19 | async-start | bytes 17301504 | tf_op jit(solution)/shard_map/reduce_scatter | solution.py:355
  882.1 844.7 %reduce-scatter.20.cloned.1.call-start = ((), (), s32[]{:S(2)}) async-start(), calls=%async_computation.18 | async-start | bytes 51904512 | tf_op jit(solution)/shard_map/reduce_scatter | solution.py:353
  906.0 62.0 %copy-start.7 = (bf16[2,512,704]{1,2,0:T(8,128)(2,1)S(1)}, bf16[2,512,704]{1,2,0:T(8,128)(2,1)}, u32[]{:S(2)}) copy-start(bf16[2,512,704]{1,2,0:T(8,128)(2,1)} %param.30) | copy-start | bytes 4325380
  975.9 119.4 %copy-start.35 = (bf16[4,64]{1,0:T(4,128)(2,1)S(1)}, bf16[4,64]{1,0:T(4,128)(2,1)}, u32[]{:S(2)}) copy-start(bf16[4,64]{1,0:T(4,128)(2,1)} %param.26) | copy-start | bytes 1540
  975.9 119.4 %copy-start.36 = (f32[2,4,64]{2,1,0:T(4,128)S(1)}, f32[2,4,64]{2,1,0:T(4,128)}, u32[]{:S(2)}) copy-start(f32[2,4,64]{2,1,0:T(4,128)} %param.32) | copy-start | bytes 6148
  975.9 311.8 %copy-start.18 = (bf16[64,2048]{1,0:T(8,128)(2,1)S(1)}, bf16[64,2048]{1,0:T(8,128)(2,1)}, u32[]{:S(2)}) copy-start(bf16[64,2048]{1,0:T(8,128)(2,1)} %param.29) | copy-start | bytes 786436
  976.4 750.4 %copy-start.15 = (bf16[64,6144]{1,0:T(8,128)(2,1)S(1)}, bf16[64,6144]{1,0:T(8,128)(2,1)}, u32[]{:S(2)}) copy-start(bf16[64,6144]{1,0:T(8,128)(2,1)} %param.27) | copy-start | bytes 2359300
  1095.3 636.1 %copy-start.34 = (f32[4,64]{1,0:T(4,128)}, f32[4,64]{1,0:T(4,128)S(1)}, u32[]{:S(2)}) copy-start(f32[4,64]{1,0:T(4,128)S(1)} %copy.91) | copy-start | bytes 3076
  (30 other events, 493.7 us)
Sparse Core Ops, SparseCore 0:
  11.0 155.9 all-gather.10
  178.3 45.6 all-gather.12
  226.2 46.7 all-gather.14
  275.8 76.9 all-gather.16
  354.5 63.7 all-gather.20
  420.3 46.0 all-gather.18
  468.2 41.4 all-gather.22
  511.4 46.0 all-gather.24
  577.9 48.3 reduce-scatter.17
  628.5 48.1 reduce-scatter.15
  755.7 48.1 reduce-scatter.27
  806.1 48.1 reduce-scatter.29
  857.9 41.4 reduce-scatter.25
  902.2 65.8 reduce-scatter.23
  970.2 124.2 reduce-scatter.31
  1097.3 190.2 reduce-scatter.21
  1295.6 431.1 reduce-scatter.19
where the time goes:
time: 1750 us; the launch traced here: 1740 us
  waiting for transfers between devices  1310 us (75%)
  matrix products  182 us (10%)
  blocking collectives  119 us (7%)
  other arithmetic  57.6 us (3%)
  local copies, waits for them, and re-layouts  50 us (3%)
    reduce_scatter x1, waiting for transfers between devices, shards(): lax.psum_scatter(qkv_grad, ('rows', 'wide'), scatter_dimension=0, tiled=T...  437 us
    reduce_scatter x1, waiting for transfers between devices, shards(): lax.psum_scatter(out_grad_w, ('rows', 'wide'), scatter_dimension=0, tiled...  192 us
    unnamed x20, waiting for transfers between devices  141 us
    unnamed x2, blocking collectives  80.5 us
    all_gather x1, waiting for transfers between devices, shards(): lax.all_gather(w_qkv, ('rows', 'wide'), axis=0, tiled=True)  75.2 us
    all_gather x1, waiting for transfers between devices, shards(): lax.all_gather(gate_up, 'rows', axis=1, tiled=True)  57.6 us
    reduce_scatter x1, waiting for transfers between devices, shards(): lax.psum_scatter(gate_grad.astype(jnp.bfloat16), 'rows', scatter_dimensio...  57.1 us
    all_gather x1, waiting for transfers between devices, shards(): lax.all_gather(w_out, ('rows', 'wide'), axis=0, tiled=True)  51.4 us
  transfers between devices with their start and end apart: 17, of which 16 were waited for; matrix products, arithmetic and copies ran while one was open for 10% of the time, Pallas kernels for 0%

commit v1 on v0

v1 whole, which is shorter than its diff:
```python
import functools

import jax
import jax.numpy as jnp
from jax import lax
from jax.experimental import pallas as pl
from jax.experimental.pallas import tpu as pltpu
from jax.sharding import PartitionSpec as P

F = jnp.float32
B = jnp.bfloat16
HEADS = 32
HEAD_DIM = 64
ROT_DIMS = 16
HALF_ROT = ROT_DIMS // 2
NORM_EPS = 1e-05
NEG_LARGE = -1e30
SCORE_SCALE = 0.125
ROPE_BASE = 10000.0
BETA_ONE = 0.9
BETA_TWO = 0.95
BIAS_FIRST = 0.999973438601112
BIAS_SECOND = 0.994079470779667
ADAM_EPS = 1e-08
DECAY_RATE = 0.1
TOKEN_BLOCK = 256
EXTRA_ROWS = 8
NT = (((1,), (1,)), ((), ()))
TN = (((0,), (0,)), ((), ()))


def dotg(left, right, dims):
    return lax.dot_general(left, right, dims, preferred_element_type=F)


def plus(left, right):
    return (left.astype(F) + right.astype(F)).astype(B)


def rows_swap(value, bits):
    return lax.ppermute(value, "rows", [(i, i ^ bits) for i in range(4)])


def rows_gather(shard, axis):
    if lax.axis_size("rows") != 4:
        return lax.all_gather(shard, "rows", axis=axis, tiled=True)
    me = lax.axis_index("rows")
    half = shard.shape[0] // 2
    near = rows_swap(shard, 1)
    far = rows_swap(shard, 2)
    diagonal = (rows_swap(near[:half], 2), rows_swap(far[half:], 1))
    shape = list(shard.shape)
    size = shape[axis]
    shape[axis] = 4 * size
    whole = jnp.zeros(shape, shard.dtype)
    for piece, bits, first in ((shard, 0, 0), (near, 1, 0), (far, 2, 0), (diagonal[0], 3, 0), (diagonal[1], 3, half)):
        start = [0] * len(shape)
        start[0] = first
        start[axis] = start[axis] + (me ^ bits) * size
        whole = lax.dynamic_update_slice(whole, piece, start)
    return whole


def rows_scatter(whole, axis):
    if lax.axis_size("rows") != 4:
        return lax.psum_scatter(whole, "rows", scatter_dimension=axis, tiled=True).astype(F)
    me = lax.axis_index("rows")
    size = whole.shape[axis] // 4
    part = lambda bits: lax.dynamic_slice_in_dim(whole, (me ^ bits) * size, size, axis)
    diagonal = part(3)
    half = diagonal.shape[0] // 2
    from_near = rows_swap(diagonal[:half], 1)
    from_far = rows_swap(diagonal[half:], 2)
    far = part(2)
    near = part(1)
    far = rows_swap(jnp.concatenate([plus(far[:half], from_near), far[half:]], 0), 2)
    near = rows_swap(jnp.concatenate([near[:half], plus(near[half:], from_far)], 0), 1)
    return part(0).astype(F) + far.astype(F) + near.astype(F)


def wide_exchange(blocks):
    count = lax.axis_size("wide")
    me = lax.axis_index("wide")
    whole = jnp.zeros(blocks.shape, blocks.dtype)
    for step in range(count):
        block = lax.dynamic_slice_in_dim(blocks, (me + step) % count, 1, 0)
        if step:
            block = lax.ppermute(block, "wide", [(i, (i + step) % count) for i in range(count)])
        whole = lax.dynamic_update_slice_in_dim(whole, block, (me - step) % count, 0)
    return whole


def wide_gather(shard):
    return lax.all_gather(shard, "wide", axis=0, tiled=True)


def wide_scatter(whole):
    return lax.psum_scatter(whole, "wide", scatter_dimension=0, tiled=True).astype(F)


def rotated(value, same, ahead, behind):
    width = value.shape[1]
    return (
        value * same
        + pltpu.roll(value, width - HALF_ROT, 1) * ahead
        + pltpu.roll(value, HALF_ROT, 1) * behind
    )


def unrotated(value, same, ahead, behind):
    width = value.shape[1]
    return value * same - (
        pltpu.roll(value, width - HALF_ROT, 1) * ahead
        + pltpu.roll(value, HALF_ROT, 1) * behind
    )


def unit_rows(tensor):
    center = tensor - jnp.mean(tensor, axis=-1, keepdims=True)
    inverse = lax.rsqrt(jnp.mean(center * center, axis=-1, keepdims=True) + NORM_EPS)
    return center * inverse, inverse


def project_body(
    x_ref, norm_ref, w_ref, bias_ref, same_ref, ahead_ref, behind_ref, q_ref, k_ref, v_ref, normed_ref
):
    hat, _ = unit_rows(x_ref[...].astype(F))
    normed = (hat * norm_ref[0:1, :] + norm_ref[1:2, :]).astype(B)
    normed_ref[...] = normed
    out = jnp.dot(normed, w_ref[...], preferred_element_type=F) + bias_ref[...]
    width = q_ref.shape[1]
    tables = (same_ref[...], ahead_ref[...], behind_ref[...])
    q_ref[...] = rotated(out[:, :width], *tables).astype(B)
    k_ref[...] = rotated(out[:, width : 2 * width], *tables).astype(B)
    v_ref[...] = out[:, 2 * width :].astype(B)


def row_spec(width, block):
    return pl.BlockSpec((block, width), lambda i: (i, 0))


def whole_spec(array):
    return pl.BlockSpec(array.shape, lambda i: (0, 0))


def project(x_all, norm_one, w_mine, bias_mine, tables):
    tokens, features = x_all.shape
    width = w_mine.shape[1] // 3
    block = min(TOKEN_BLOCK, tokens)
    return pl.pallas_call(
        project_body,
        grid=(tokens // block,),
        in_specs=[
            row_spec(features, block),
            whole_spec(norm_one),
            whole_spec(w_mine),
            whole_spec(bias_mine),
        ]
        + [row_spec(width, block)] * 3,
        out_specs=[row_spec(width, block)] * 3 + [row_spec(features, block)],
        out_shape=[jax.ShapeDtypeStruct((tokens, width), B)] * 3
        + [jax.ShapeDtypeStruct((tokens, features), B)],
        name="project",
    )(x_all, norm_one, w_mine, bias_mine, *tables)


def pair_bias(seg_col, seg_row, first, size, keys):
    same = seg_col[first : first + size, :] == seg_row[:, :keys]
    key_pos = lax.broadcasted_iota(jnp.int32, (size, keys), 1)
    query_pos = first + lax.broadcasted_iota(jnp.int32, (size, keys), 0)
    return jnp.where(same & (key_pos <= query_pos), 0.0, NEG_LARGE)


def head_masks(heads, width):
    lane = lax.broadcasted_iota(jnp.int32, (1, width), 1) // HEAD_DIM
    return [jnp.where(lane == head, 1.0, 0.0).astype(B) for head in range(heads)]


def attend_body(heads, q_ref, k_ref, v_ref, seg_col, seg_row, out_ref, lse_ref):
    tokens, width = q_ref.shape
    block = min(TOKEN_BLOCK, tokens)
    masks = head_masks(heads, width)
    for first in range(0, tokens, block):
        keys = first + block
        bias = pair_bias(seg_col, seg_row, first, block, keys)
        queries = q_ref[first:keys, :]
        total = jnp.zeros((block, width), F)
        for head in range(heads):
            scores = dotg(queries * (masks[head] * SCORE_SCALE), k_ref[:keys, :], NT) + bias
            top = jnp.max(scores, axis=-1, keepdims=True)
            weights = jnp.exp(scores - top)
            norm = jnp.sum(weights, axis=-1, keepdims=True)
            probs = (weights * (1.0 / norm)).astype(B)
            total += jnp.dot(probs, v_ref[:keys, :] * masks[head], preferred_element_type=F)
            lse_ref[first:keys, head : head + 1] = top + jnp.log(norm)
        out_ref[first:keys, :] = total.astype(B)


def attend(q, k, v, seg_col, seg_row, heads):
    tokens, width = q.shape
    return pl.pallas_call(
        functools.partial(attend_body, heads),
        out_shape=[
            jax.ShapeDtypeStruct((tokens, width), B),
            jax.ShapeDtypeStruct((tokens, 128), F),
        ],
        name="attend",
    )(q, k, v, seg_col, seg_row)


def attend_back_body(
    heads, q_ref, k_ref, v_ref, g_ref, lse_ref, seg_col, seg_row, same_ref, ahead_ref, behind_ref,
    out_ref, bias_ref, dq_ref, dk_ref, dv_ref,
):
    tokens, width = q_ref.shape
    block = min(TOKEN_BLOCK, tokens)
    masks = head_masks(heads, width)
    for first in reversed(range(0, tokens, block)):
        keys = first + block
        bias = pair_bias(seg_col, seg_row, first, block, keys)
        queries = q_ref[first:keys, :]
        grads = g_ref[first:keys, :]
        dq = jnp.zeros((block, width), F)
        stacks = ([], [], [], [])
        for head in range(heads):
            q_head = queries * (masks[head] * SCORE_SCALE)
            g_head = grads * masks[head]
            scores = dotg(q_head, k_ref[:keys, :], NT) + bias
            probs = jnp.exp(scores - lse_ref[first:keys, head : head + 1])
            weighted = probs * dotg(g_head, v_ref[:keys, :], NT)
            delta = jnp.sum(weighted, axis=-1, keepdims=True)
            grad_scores = (weighted - probs * delta).astype(B)
            dq += jnp.dot(grad_scores, k_ref[:keys, :] * masks[head], preferred_element_type=F)
            for stack, value in zip(stacks, (grad_scores, q_head, probs.astype(B), g_head)):
                stack.append(value)
        joined = [jnp.concatenate(stack, 0) for stack in stacks]
        dk = dotg(joined[0], joined[1], TN)
        dv = dotg(joined[2], joined[3], TN)
        if keys == tokens:
            dk_ref[...] = dk
            dv_ref[...] = dv
        else:
            dk_ref[:keys, :] += dk
            dv_ref[:keys, :] += dv
        dq_ref[first:keys, :] = dq * SCORE_SCALE
    tables = (same_ref[...], ahead_ref[...], behind_ref[...])
    pieces = (unrotated(dq_ref[...], *tables), unrotated(dk_ref[...], *tables), dv_ref[...])
    for at, piece in enumerate(pieces):
        rounded = piece.astype(B)
        out_ref[:, at * width : (at + 1) * width] = rounded
        bias_ref[:, at * width : (at + 1) * width] = jnp.sum(
            rounded.astype(F), axis=0, keepdims=True
        )


def attend_back(q, k, v, grads, lse, seg_col, seg_row, tables, heads):
    tokens, width = q.shape
    return pl.pallas_call(
        functools.partial(attend_back_body, heads),
        out_shape=[
            jax.ShapeDtypeStruct((tokens, 3 * width), B),
            jax.ShapeDtypeStruct((1, 3 * width), F),
        ],
        scratch_shapes=[pltpu.VMEM((tokens, width), F)] * 3,
        name="attend_back",
    )(q, k, v, grads, lse, seg_col, seg_row, *tables)


def project_back_body(grad_ref, w_ref, x_ref, e_ref, sums_ref):
    hat, _ = unit_rows(x_ref[...].astype(F))
    e = dotg(grad_ref[...], w_ref[...], NT)
    e_ref[...] = e.astype(B)
    sums = jnp.concatenate(
        [jnp.sum(e * hat, axis=0, keepdims=True), jnp.sum(e, axis=0, keepdims=True)], 0
    )

    @pl.when(pl.program_id(0) == 0)
    def _():
        sums_ref[...] = sums

    @pl.when(pl.program_id(0) != 0)
    def _():
        sums_ref[...] += sums


def project_back(grad_proj, w_mine, x_all):
    tokens, features = x_all.shape
    block = min(TOKEN_BLOCK, tokens)
    return pl.pallas_call(
        project_back_body,
        grid=(tokens // block,),
        in_specs=[
            row_spec(grad_proj.shape[1], block),
            whole_spec(w_mine),
            row_spec(features, block),
        ],
        out_specs=[
            row_spec(features, block),
            pl.BlockSpec((2, features), lambda i: (0, 0)),
        ],
        out_shape=[
            jax.ShapeDtypeStruct((tokens, features), B),
            jax.ShapeDtypeStruct((2, features), F),
        ],
        name="project_back",
    )(grad_proj, w_mine, x_all)


def adam_step(parameter, gradient, moments):
    first_moment = BETA_ONE * moments[0] + (1.0 - BETA_ONE) * gradient
    second_moment = BETA_TWO * moments[1] + (1.0 - BETA_TWO) * gradient * gradient
    return first_moment / BIAS_FIRST / (
        jnp.sqrt(second_moment / BIAS_SECOND) + ADAM_EPS
    ) + DECAY_RATE * parameter.astype(F)


def rotary_tables(segment_row, width):
    tokens = segment_row.shape[0]
    before = jnp.sum((segment_row[None, :] < segment_row[:, None]).astype(jnp.int32), axis=1)
    positions = jnp.arange(tokens, dtype=jnp.int32) - before
    frequency = jnp.exp(
        jnp.arange(HALF_ROT, dtype=F) * (-2.0 * jnp.log(ROPE_BASE) / ROT_DIMS)
    )
    angles = positions.astype(F)[:, None] * frequency[None, :]
    cosine = jnp.cos(angles)
    sine = jnp.sin(angles)
    none = jnp.zeros((tokens, HALF_ROT), F)
    rest = jnp.zeros((tokens, HEAD_DIM - ROT_DIMS), F)
    heads = width // HEAD_DIM
    tile = lambda *parts: jnp.tile(jnp.concatenate(parts, 1), (1, heads))
    return (
        tile(cosine, cosine, rest + 1.0),
        tile(-sine, none, rest),
        tile(none, sine, rest),
    )


def packed_rows(parts, rows, columns):
    flat = jnp.concatenate(parts, -1)
    room = rows * columns - flat.shape[-1]
    flat = jnp.concatenate([flat, jnp.zeros(flat.shape[:-1] + (room,), flat.dtype)], -1)
    return flat.reshape(flat.shape[:-1] + (rows, columns))


def shards(
    block_input, out_grad, segment_ids, positions, norm_params, w_qkv, b_qkv, w_out, gate_up, w_down,
    moment_norm, moment_qkv, moment_bias, moment_out, moment_gate, moment_down,
):
    x_own = block_input[0]
    local_len, features = x_own.shape
    rows = lax.axis_size("rows")
    wide = lax.axis_size("wide")
    my_row = lax.axis_index("rows")
    my_wide = lax.axis_index("wide")
    segment_row = segment_ids[0]
    heads = HEADS // wide
    width = heads * HEAD_DIM
    depth = w_qkv.shape[0]
    norm_size = norm_params.shape[1]
    strided = depth % HEAD_DIM == 0

    def by_head(array, axis):
        shape = array.shape
        if strided:
            array = array.reshape(shape[:axis] + (heads, wide, HEAD_DIM) + shape[axis + 1 :])
            return jnp.moveaxis(array, axis + 1, 0)
        array = array.reshape(shape[:axis] + (wide, heads, HEAD_DIM) + shape[axis + 1 :])
        return jnp.moveaxis(array, axis, 0)

    def from_heads(array, axis):
        array = jnp.moveaxis(array, 0, axis + 1 if strided else axis)
        shape = array.shape
        return array.reshape(shape[:axis] + (HEADS * HEAD_DIM,) + shape[axis + 3 :])

    w_blocks = by_head(w_qkv.reshape(depth, 3, features), 2).reshape(wide, depth, 3 * width)
    extra = packed_rows([norm_params.reshape(-1), b_qkv], EXTRA_ROWS, 3 * width)
    w_blocks = jnp.concatenate(
        [w_blocks, jnp.broadcast_to(extra[None], (wide,) + extra.shape)], 1
    )
    w_packed = rows_gather(wide_exchange(w_blocks), 0)
    w_mine = w_packed[:, :depth].reshape(features, 3 * width)
    extra = w_packed[:, depth:].reshape(rows * wide, -1)
    norms = extra[:, : 4 * norm_size].reshape(rows * wide, 4, norm_size)
    norms = norms.transpose(1, 0, 2).reshape(4, features).astype(F)
    bias = extra[:, 4 * norm_size : 4 * norm_size + b_qkv.shape[0]].reshape(3, features)
    bias_mine = lax.dynamic_index_in_dim(by_head(bias, 1), my_wide, 0, False)
    bias_mine = bias_mine.reshape(1, 3 * width).astype(F)
    if strided:
        out_mine = rows_gather(w_out, 0)
    else:
        out_mine = lax.all_gather(w_out, ("rows", "wide"), axis=0, tiled=True)
        out_mine = lax.dynamic_slice_in_dim(out_mine, my_wide * width, width, 0)

    x_all = wide_gather(x_own)
    tables = rotary_tables(segment_row, width)
    seg_col = segment_row[:, None]
    seg_line = segment_row[None, :]
    q, k, v, normed_all = project(x_all, norms[:2], w_mine, bias_mine, tables)
    attended, lse = attend(q, k, v, seg_col, seg_line, heads)
    branch = jnp.dot(attended, out_mine, preferred_element_type=F).astype(B)
    after_attn = x_own.astype(F) + wide_scatter(branch)
    hat_two, inv_two = unit_rows(after_attn)
    normed_two = (hat_two * norms[2] + norms[3]).astype(B)
    tokens_all = wide_gather(normed_two)
    gate_rows = rows_gather(gate_up, 1)
    down_rows = rows_gather(w_down, 1)
    gate_vals = jnp.einsum("td,gdf->gtf", tokens_all, gate_rows, preferred_element_type=F)
    gate_part, up_part = gate_vals[0], gate_vals[1]
    sigmoid_g = jax.nn.sigmoid(gate_part)
    activated = gate_part * sigmoid_g
    hidden = (activated * up_part).astype(B)
    mlp_out = wide_scatter(jnp.dot(hidden, down_rows, preferred_element_type=F).astype(B))
    block_out = (after_attn + mlp_out).astype(B)

    grads_all = wide_gather(out_grad[0])
    grad_hidden = jnp.einsum("td,fd->tf", grads_all, down_rows, preferred_element_type=F)
    down_grad = jnp.einsum("tf,td->fd", hidden, grads_all, preferred_element_type=F).astype(B)
    grad_gate_part = grad_hidden * up_part * sigmoid_g * (1.0 + gate_part * (1.0 - sigmoid_g))
    gate_grads = jnp.stack([grad_gate_part, grad_hidden * activated]).astype(B)
    grad_normed_two = wide_scatter(
        jnp.einsum("gtf,gdf->td", gate_grads, gate_rows, preferred_element_type=F).astype(B)
    )
    gate_grad = jnp.einsum("td,gtf->gdf", tokens_all, gate_grads, preferred_element_type=F).astype(B)
    grad_gate = rows_scatter(gate_grad, 1)
    grad_down = rows_scatter(down_grad, 1)

    def norm_back(upstream, hat, inverse, gain):
        scaled = upstream * gain
        mean_grad = jnp.mean(scaled, axis=-1, keepdims=True)
        mean_proj = jnp.mean(scaled * hat, axis=-1, keepdims=True)
        return inverse * (scaled - mean_grad - hat * mean_proj)

    grad_after = out_grad[0].astype(F) + norm_back(grad_normed_two, hat_two, inv_two, norms[2])
    gain_two = jnp.sum(grad_normed_two * hat_two, axis=0)
    shift_two = jnp.sum(grad_normed_two, axis=0)
    branch_all = wide_gather(grad_after.astype(B))
    grad_attended = dotg(branch_all, out_mine, NT).astype(B)
    out_part = dotg(attended, branch_all, TN).astype(B)
    if strided:
        grad_out = rows_scatter(out_part, 0)
    else:
        grad_out = rows_scatter(out_part, 0)
        moves = [
            (r * wide + w, w * rows + r) for r in range(rows) for w in range(wide)
        ]
        grad_out = lax.ppermute(grad_out, ("rows", "wide"), moves)
    grad_proj, bias_grad = attend_back(
        q, k, v, grad_attended, lse, seg_col, seg_line, tables, heads
    )
    e_one, sums_one = project_back(grad_proj, w_mine, x_all)
    grad_normed_one = wide_scatter(e_one)
    qkv_part = dotg(normed_all, grad_proj, TN).astype(B)
    hat_one, inv_one = unit_rows(x_own.astype(F))
    input_grad = grad_after + norm_back(grad_normed_one, hat_one, inv_one, norms[0])

    norm_parts = jnp.concatenate([sums_one, gain_two[None], shift_two[None]], 0)
    norm_parts = norm_parts.reshape(4, rows * wide, norm_size).transpose(1, 0, 2)
    extra = packed_rows(
        [
            norm_parts.reshape(rows * wide, -1),
            jnp.broadcast_to(bias_grad, (rows * wide, 3 * width)),
        ],
        EXTRA_ROWS,
        3 * width,
    ).astype(B)
    packed = jnp.concatenate([qkv_part.reshape(rows * wide, depth, 3 * width), extra], 1)
    received = wide_exchange(rows_scatter(packed, 0).astype(B)).astype(F)
    grad_qkv = received[:, :depth].reshape(wide, depth, 3, heads, HEAD_DIM)
    grad_qkv = from_heads(grad_qkv, 2).reshape(depth, 3 * features)
    extra = received[:, depth:].reshape(wide, -1)
    grad_norms = jnp.sum(extra[:, : 4 * norm_size], axis=0).reshape(4, norm_size)
    bias_all = extra[:, 4 * norm_size : 4 * norm_size + 3 * width]
    bias_all = from_heads(bias_all.reshape(wide, 3, heads, HEAD_DIM), 1).reshape(-1)
    size = b_qkv.shape[0]
    grad_bias = lax.dynamic_slice_in_dim(bias_all, (my_row * wide + my_wide) * size, size, 0)

    return (
        block_out[None],
        input_grad[None],
        grad_norms,
        grad_qkv,
        grad_bias,
        grad_out,
        grad_gate,
        grad_down,
        adam_step(norm_params, grad_norms, moment_norm),
        adam_step(w_qkv, grad_qkv, moment_qkv),
        adam_step(b_qkv, grad_bias, moment_bias),
        adam_step(w_out, grad_out, moment_out),
        adam_step(gate_up, grad_gate, moment_gate),
        adam_step(w_down, grad_down, moment_down),
    )


def solution(mesh):
    both = ("rows", "wide")
    tokens = P("rows", "wide", None)
    weights = (P(None, both), P(both, None), P(both), P(both, None), P(None, "rows", "wide"), P("wide", "rows"))
    moments = tuple(P(None, *spec) for spec in weights)
    return jax.shard_map(
        shards,
        mesh=mesh,
        in_specs=(tokens, tokens, P("rows", None), P("rows", "wide")) + weights + moments,
        out_specs=(tokens, tokens) + weights + weights,
        check_vma=False,
    )
```

time: 1750 us -> 644 us (0.37)
  waiting for transfers between devices: 1310 us -> 344 us
  blocking collectives: 119 us -> 0 us
  matrix products: 182 us -> 65.1 us
  starting transfers between devices: 1.62 us -> 51.1 us
  Pallas kernels: 0 us -> 43.3 us
  local copies, waits for them, and re-layouts: 50 us -> 71.1 us
    reduce_scatter x6 -> x4, waiting for transfers between devices: 774 us -> 98.6 us  [wide_scatter(): lax.psum_scatter(whole, 'wide', scatter_dimension=0, tiled=True).astype(F)]
    all_gather x8 -> x4, waiting for transfers between devices: 393 us -> 47.5 us  [wide_gather(): return lax.all_gather(shard, 'wide', axis=0, tiled=True)]
    ppermute x0 -> x46, waiting for transfers between devices: none -> 196 us  [the longest x32 137 us: rows_swap(): return lax.ppermute(value, 'rows', [(i, i ^ bits) for i in range(4)])]
    unnamed x20 -> x8, waiting for transfers between devices: 141 us -> 1.3 us
    dot_general x26 -> x10, matrix products: 182 us -> 65.1 us  [the longest x1 11.4 us: shards(): jnp.einsum('td,gdf->gtf', tokens_all, gate_rows, preferred_element_type=F)]
    unnamed x2 -> x0, blocking collectives: 80.5 us -> none
    ppermute x0 -> x46, starting transfers between devices: none -> 50.2 us  [the longest x32 30.6 us: rows_swap(): return lax.ppermute(value, 'rows', [(i, i ^ bits) for i in range(4)])]
    pallas_call x0 -> x4, Pallas kernels: none -> 43.3 us  [the longest x1 15.5 us: attend_back(): pl.pallas_call(functools.partial(attend_back_body, heads), out_shape=[jax...]
  transfers between devices with their start and end apart: 17 -> 54, of which waited for: 16 -> 30; matrix products, arithmetic and copies ran while one was open for 10% -> 21% of each run, Pallas kernels for 0% -> 0%
where the time goes in v1:
time: 644 us; the launch traced here: 635 us
  waiting for transfers between devices  344 us (53%)
  local copies, waits for them, and re-layouts  71.1 us (11%)
  matrix products  65.1 us (10%)
  starting transfers between devices  51.1 us (8%)
  other arithmetic  45.2 us (7%)
  Pallas kernels  43.3 us (7%)
  between operations  15.4 us (2%)
    ppermute x32, waiting for transfers between devices, rows_swap(): return lax.ppermute(value, 'rows', [(i, i ^ bits) for i in range(4)])  137 us
    reduce_scatter x4, waiting for transfers between devices, wide_scatter(): lax.psum_scatter(whole, 'wide', scatter_dimension=0, tiled=True).astype(F)  98.6 us
    ppermute x14, waiting for transfers between devices, wide_exchange(): lax.ppermute(block, 'wide', [(i, (i + step) % count) for i in range(count)])  59.6 us
    all_gather x4, waiting for transfers between devices, wide_gather(): return lax.all_gather(shard, 'wide', axis=0, tiled=True)  47.5 us
    ppermute x32, starting transfers between devices, rows_swap(): return lax.ppermute(value, 'rows', [(i, i ^ bits) for i in range(4)])  30.6 us
    add x6, other arithmetic, adam_step(): first_moment / BIAS_FIRST  19.6 us
    ppermute x14, starting transfers between devices, wide_exchange(): lax.ppermute(block, 'wide', [(i, (i + step) % count) for i in range(count)])  19.6 us
    dynamic_update_slice x20, local copies, waits for them, and re-layouts, rows_gather(): whole = lax.dynamic_update_slice(whole, piece, start)  16.7 us
  transfers between devices with their start and end apart: 54, of which 30 were waited for; matrix products, arithmetic and copies ran while one was open for 21% of the time, Pallas kernels for 0%

profile of v1, /device:TPU:9, one launch (start us, length us, event | category | flops | bytes accessed | tf_op | source)
XLA Modules:
  0.0 635.0 jit_solution(17971951403753996675)
XLA Ops:
  27.7 10.5 %collective-permute-done.1 = bf16[1,72,768]{2,1,0:T(8,128)(2,1)S(1)} collective-permute-done((bf16[1,72,768]{2,1,0:T(8,128)(2,1)}, bf16[1,72,768]{2,1,0:T(8,128)(2,1)S(1)}, u32[]{:S(2)}, u32[]{:S(2)}) %collective-permute-start.1) | collective-permute-done | bytes 110624 | tf_op jit(solution)/shard_map/ppermute | solution.py:88
  38.2 14.6 %collective-permute-done.2 = bf16[1,72,768]{2,1,0:T(8,128)(2,1)S(1)} collective-permute-done((bf16[1,72,768]{2,1,0:T(8,128)(2,1)}, bf16[1,72,768]{2,1,0:T(8,128)(2,1)S(1)}, u32[]{:S(2)}, u32[]{:S(2)}) %collective-permute-start.2) | collective-permute-done | bytes 110624 | tf_op jit(solution)/shard_map/ppermute | solution.py:88
  52.8 9.6 %collective-permute-done.3 = bf16[1,72,768]{2,1,0:T(8,128)(2,1)S(1)} collective-permute-done((bf16[1,72,768]{2,1,0:T(8,128)(2,1)S(1)}, bf16[1,72,768]{2,1,0:T(8,128)(2,1)S(1)}, u32[]{:S(2)}, u32[]{:S(2)}) %collective-permute-start.3) | collective-permute-done | bytes 110624 | tf_op jit(solution)/shard_map/ppermute | solution.py:88
  64.0 7.3 %collective-permute-done.6 = bf16[1,72,768]{2,1,0:T(8,128)(2,1)S(1)} collective-permute-done((bf16[1,72,768]{2,1,0:T(8,128)(2,1)S(1)}, bf16[1,72,768]{2,1,0:T(8,128)(2,1)S(1)}, u32[]{:S(2)}, u32[]{:S(2)}) %collective-permute-start.6) | collective-permute-done | bytes 110624 | tf_op jit(solution)/shard_map/ppermute | solution.py:88
  85.1 6.3 collective-permute-done.13
  104.6 10.5 %project.1 = (bf16[1024,256]{1,0:T(8,128)(2,1)}, bf16[1024,256]{1,0:T(8,128)(2,1)}, bf16[1024,256]{1,0:T(8,128)(2,1)}, bf16[1024,2048]{1,0:T(8,128)(2,1)}) custom-call(bf16[1024,2048]{1,0:T(8,128)(2,1)} %bitcast.216, f32[2,2048]{1,0:T(2,128)} %slice.186.norm_ref, bf16[2048,768]{1,0:T(8,128)(2,1)} %bitcast.214, f32[1,768]{1,0:T(1,128)} %reshape.200.bias_ref, ...), custom_call_target="tpu_custom_call" | custom-call | tf_op jit(solution)/shard_map/project/pallas_call | solution.py:150
  115.1 8.2 %attend.1 = (bf16[1024,256]{1,0:T(8,128)(2,1)}, f32[1024,128]{1,0:T(8,128)}) custom-call(bf16[1024,256]{1,0:T(8,128)(2,1)} %get-tuple-element.24.q_ref, bf16[1024,256]{1,0:T(8,128)(2,1)} %get-tuple-element.25.k_ref, bf16[1024,256]{1,0:T(8,128)(2,1)} %get-tuple-element.26.v_ref, s32[1024,1]{1,0:T(8,128)} %copy.63.seg_col, s32[1,1024]{1,0:T(1,128)} %seg_row.3), custom_call_target="tpu_custom_call" | custom-call | tf_op jit(solution)/shard_map/attend/pallas_call | solution.py:201
  127.9 50.3 %reduce-scatter.5.cloned.1.call-done = bf16[128,2048]{1,0:T(8,128)(2,1)} async-done(((bf16[1024,2048]{1,0:T(8,128)(2,1)}), bf16[128,2048]{1,0:T(8,128)(2,1)}) %reduce-scatter.5.cloned.1.call-update) | async-done | bytes 524304 | tf_op jit(solution)/shard_map/reduce_scatter | solution.py:98
  191.4 40.6 %collective-permute-done.19 = bf16[704,512]{1,0:T(8,128)(2,1)} collective-permute-done((bf16[704,512]{1,0:T(8,128)(2,1)}, bf16[704,512]{1,0:T(8,128)(2,1)}, u32[]{:S(2)}, u32[]{:S(2)}) %collective-permute-start.19) | collective-permute-done | bytes 720928 | tf_op jit(solution)/shard_map/ppermute | solution.py:41
  252.7 6.4 %collective-permute-done.17 = bf16[1,512,704]{1,2,0:T(8,128)(2,1)S(1)} collective-permute-done((bf16[1,512,704]{1,2,0:T(8,128)(2,1)S(1)}, bf16[1,512,704]{1,2,0:T(8,128)(2,1)S(1)}, u32[]{:S(2)}, u32[]{:S(2)}) %collective-permute-start.17) | collective-permute-done | bytes 720928 | tf_op jit(solution)/shard_map/ppermute | solution.py:41
  262.8 11.4 %fusion.23 = f32[2,1024,704]{1,2,0:T(8,128)} fusion(bf16[2,2048,704]{1,2,0:T(8,128)(2,1)} %constant_dynamic-update-slice_fusion.11, bf16[1024,2048]{1,0:T(8,128)(2,1)} %all-gather.7.cloned.1.call-done), kind=kOutput, calls=%fused_computation.55 | convolution fusion | flops 5905580032 | bytes 15728640 | tf_op jit(solution)/shard_map/td,gdf->gtf/dot_general | solution.py:407
  276.1 10.1 %fusion.41 = (bf16[1,1024,704]{1,2,0:T(8,128)(2,1)S(1)}, bf16[1,1024,704]{1,2,0:T(8,128)(2,1)S(1)}, bf16[1024,704]{0,1:T(8,128)(2,1)}) fusion(f32[2,1024,704]{1,2,0:T(8,128)} %fusion.23, bf16[704,2048]{1,0:T(8,128)(2,1)} %copy-done.10, bf16[1,1024,2048]{2,1,0:T(8,128)(2,1)} %all-gather.13.cloned.1.call-done), kind=kOutput, calls=%fused_computation.84 | convolution fusion | flops 2963603456 | bytes 17170432 | tf_op jit(solution)/shard_map/td,fd->tf/dot_general | solution.py:416
  287.7 11.0 %bitcast_convert_fusion = bf16[1024,2048]{1,0:T(8,128)(2,1)} fusion(bf16[2,2048,704]{1,2,0:T(8,128)(2,1)} %constant_dynamic-update-slice_fusion.11, bf16[1,1024,704]{1,2,0:T(8,128)(2,1)S(1)} %get-tuple-element.52, bf16[1,1024,704]{1,2,0:T(8,128)(2,1)S(1)} %get-tuple-element.51), kind=kOutput, calls=%fused_computation | convolution fusion | flops 5909118976 | bytes 12845056 | tf_op jit(solution)/shard_map/gtf,gdf->td/dot_general | solution.py:421
  298.9 48.3 %reduce-scatter.9.cloned.1.call-done = bf16[128,2048]{1,0:T(8,128)(2,1)} async-done(((bf16[1024,2048]{1,0:T(8,128)(2,1)}), bf16[128,2048]{1,0:T(8,128)(2,1)}) %reduce-scatter.9.cloned.1.call-update) | async-done | bytes 524304 | tf_op jit(solution)/shard_map/reduce_scatter | solution.py:98
  351.8 45.6 %all-gather.9.cloned.1.call-done = bf16[1024,2048]{1,0:T(8,128)(2,1)} async-done(((bf16[128,2048]{1,0:T(8,128)(2,1)}), bf16[1024,2048]{1,0:T(8,128)(2,1)}) %all-gather.9.cloned.1.call-update) | async-done | bytes 4194320 | tf_op jit(solution)/shard_map/all_gather | solution.py:94
  397.4 4.3 convolution_convert_fusion.5.g_ref
  401.7 15.5 %attend_back.1 = (bf16[1024,768]{1,0:T(8,128)(2,1)}, f32[1,768]{1,0:T(1,128)}) custom-call(bf16[1024,256]{1,0:T(8,128)(2,1)} %get-tuple-element.24.q_ref, bf16[1024,256]{1,0:T(8,128)(2,1)} %get-tuple-element.25.k_ref, bf16[1024,256]{1,0:T(8,128)(2,1)} %get-tuple-element.26.v_ref, bf16[1024,256]{1,0:T(8,128)(2,1)} %convolution_convert_fusion.5.g_ref, ...), custom_call_target="tpu_custom_call" | custom-call | tf_op jit(solution)/shard_map/attend_back/pallas_call | solution.py:258
  417.2 9.1 %project_back.1 = (bf16[1024,2048]{1,0:T(8,128)(2,1)}, f32[2,2048]{1,0:T(2,128)}) custom-call(bf16[1024,768]{1,0:T(8,128)(2,1)} %get-tuple-element.29.grad_ref, bf16[2048,768]{1,0:T(8,128)(2,1)} %bitcast.215, bf16[1024,2048]{1,0:T(8,128)(2,1)} %bitcast.217), custom_call_target="tpu_custom_call" | custom-call | tf_op jit(solution)/shard_map/project_back/pallas_call | solution.py:289
  427.7 8.7 %convolution_convert_fusion = bf16[2,704,2048]{2,1,0:T(8,128)(2,1)S(1)} fusion(bf16[1024,2048]{1,0:T(8,128)(2,1)} %all-gather.7.cloned.1.call-done, bf16[1,1024,704]{1,2,0:T(8,128)(2,1)} %copy-done.31, bf16[1,1024,704]{1,2,0:T(8,128)(2,1)S(1)} %copy-done.30), kind=kOutput, calls=%fused_computation.5 | convolution fusion | flops 5909905408 | bytes 12845056 | tf_op jit(solution)/shard_map/td,gtf->gdf/dot_general | solution.py:423
  452.5 5.7 collective-permute-done.42
  458.2 8.6 %collective-permute-done.44 = bf16[352,512]{1,0:T(8,128)(2,1)} collective-permute-done((bf16[352,512]{1,0:T(8,128)(2,1)}, bf16[352,512]{1,0:T(8,128)(2,1)}, u32[]{:S(2)}, u32[]{:S(2)}) %collective-permute-start.44) | collective-permute-done | bytes 360480 | tf_op jit(solution)/shard_map/ppermute | solution.py:41
  479.9 5.1 convolution_convert_fusion.1
  485.0 35.1 %collective-permute-done.45 = bf16[704,512]{1,0:T(8,128)(2,1)} collective-permute-done((bf16[704,512]{1,0:T(8,128)(2,1)S(1)}, bf16[704,512]{1,0:T(8,128)(2,1)}, u32[]{:S(2)}, u32[]{:S(2)}) %collective-permute-start.45) | collective-permute-done | bytes 720928 | tf_op jit(solution)/shard_map/ppermute | solution.py:41
  523.0 5.1 fusion.38
  528.1 7.3 %fusion.15 = (f32[2,512,704]{1,2,0:T(8,128)}, f32[2,512,704]{1,2,0:T(8,128)}) fusion(bf16[2,512,704]{1,2,0:T(8,128)(2,1)S(1)} %copy-done.7, f32[2,2,512,704]{2,3,1,0:T(8,128)} %param.29, bf16[2,512,704]{1,2,0:T(8,128)(2,1)} %collective-permute-done.41, bf16[2,512,704]{1,2,0:T(8,128)(2,1)} %collective-permute-done.39, bf16[2,704,2048]{2,1,0:T(8,128)(2,1)} %copy-done.5, ...), kind=kLoop, calls=%fused_computation.33 | loop fusion | flops 13697024 | bytes 17301508 | tf_op jit(solution)/shard_map/add | solution.py:312
  536.2 5.7 convolution_convert_fusion.3
  557.3 17.3 %collective-permute-done.26 = bf16[8,72,768]{2,1,0:T(8,128)(2,1)S(1)} collective-permute-done((bf16[8,72,768]{2,1,0:T(8,128)(2,1)S(1)}, bf16[8,72,768]{2,1,0:T(8,128)(2,1)S(1)}, u32[]{:S(2)}, u32[]{:S(2)}) %collective-permute-start.26) | collective-permute-done | bytes 884768 | tf_op jit(solution)/shard_map/ppermute | solution.py:41
  575.1 7.9 %collective-permute-start.27 = (bf16[1,72,768]{2,1,0:T(8,128)(2,1)S(1)}, bf16[1,72,768]{2,1,0:T(8,128)(2,1)S(1)}, u32[]{:S(2)}, u32[]{:S(2)}) collective-permute-start(bf16[1,72,768]{2,1,0:T(8,128)(2,1)S(1)} %get-tuple-element.82), channel_id=1, source_target_pairs={{0,1},{1,2},{2,3},{3,4},{4,5},{5,6},{6,7},{7,0},{8,9},{9,10},{10,1... | collective-permute-start | bytes 331784 | tf_op jit(solution)/shard_map/ppermute | solution.py:88
  584.8 4.7 collective-permute-start.29
  592.3 8.9 %collective-permute-done.29 = bf16[1,72,768]{2,1,0:T(8,128)(2,1)S(1)} collective-permute-done((bf16[1,72,768]{2,1,0:T(8,128)(2,1)S(1)}, bf16[1,72,768]{2,1,0:T(8,128)(2,1)S(1)}, u32[]{:S(2)}, u32[]{:S(2)}) %collective-permute-start.29) | collective-permute-done | bytes 110624 | tf_op jit(solution)/shard_map/ppermute | solution.py:88
  609.0 5.4 copy.77
  618.6 4.4 fusion.31
  (333 shorter events, 170.4 us)
Async XLA Ops:
  7.2 97.4 %all-gather.11.cloned.1.call-start = ((), (), s32[]{:S(2)}) async-start(), calls=%async_computation.10 | async-start | bytes 4718592 | tf_op jit(solution)/shard_map/all_gather | solution.py:94
  7.9 170.2 %reduce-scatter.5.cloned.1.call-start = ((), (), s32[]{:S(2)}) async-start(), calls=%async_computation.4 | async-start | bytes 4718592 | tf_op jit(solution)/shard_map/reduce_scatter | solution.py:98
  8.0 70.5 %collective-permute-start.11 = (bf16[64,2048]{1,0:T(8,128)(2,1)}, bf16[64,2048]{1,0:T(8,128)(2,1)}, u32[]{:S(2)}, u32[]{:S(2)}) collective-permute-start(bf16[64,2048]{1,0:T(8,128)(2,1)} %param.22), channel_id=1, source_target_pairs={{0,8},{8,0},{16,24},{24,16},{1,9},{9,1},{17,25},{25,17},{2,10},{10... | collective-permute-start | bytes 786440 | tf_op jit(solution)/shard_map/ppermute | solution.py:41
  9.2 71.6 %collective-permute-start.12 = (bf16[64,2048]{1,0:T(8,128)(2,1)}, bf16[64,2048]{1,0:T(8,128)(2,1)}, u32[]{:S(2)}, u32[]{:S(2)}) collective-permute-start(bf16[64,2048]{1,0:T(8,128)(2,1)} %param.22), channel_id=1, source_target_pairs={{0,16},{8,24},{16,0},{24,8},{1,17},{9,25},{17,1},{25,9},{2,18},{10... | collective-permute-start | bytes 786440 | tf_op jit(solution)/shard_map/ppermute | solution.py:41
  23.0 29.8 %collective-permute-start.2 = (bf16[1,72,768]{2,1,0:T(8,128)(2,1)}, bf16[1,72,768]{2,1,0:T(8,128)(2,1)S(1)}, u32[]{:S(2)}, u32[]{:S(2)}) collective-permute-start(bf16[1,72,768]{2,1,0:T(8,128)(2,1)} %get-tuple-element.90), channel_id=1, source_target_pairs={{0,3},{1,4},{2,5},{3,6},{4,7},{5,0},{6,1},{7,2},{8,11},{9,12},{10,... | collective-permute-start | bytes 331784 | tf_op jit(solution)/shard_map/ppermute | solution.py:88
  27.7 34.7 %collective-permute-start.3 = (bf16[1,72,768]{2,1,0:T(8,128)(2,1)S(1)}, bf16[1,72,768]{2,1,0:T(8,128)(2,1)S(1)}, u32[]{:S(2)}, u32[]{:S(2)}) collective-permute-start(bf16[1,72,768]{2,1,0:T(8,128)(2,1)S(1)} %get-tuple-element.91), channel_id=1, source_target_pairs={{0,4},{1,5},{2,6},{3,7},{4,0},{5,1},{6,2},{7,3},{8,12},{9,13},{10,... | collective-permute-start | bytes 331784 | tf_op jit(solution)/shard_map/ppermute | solution.py:88
  38.2 24.4 %collective-permute-start.4 = (bf16[1,72,768]{2,1,0:T(8,128)(2,1)S(1)}, bf16[1,72,768]{2,1,0:T(8,128)(2,1)S(1)}, u32[]{:S(2)}, u32[]{:S(2)}) collective-permute-start(bf16[1,72,768]{2,1,0:T(8,128)(2,1)S(1)} %get-tuple-element.93), channel_id=1, source_target_pairs={{0,5},{1,6},{2,7},{3,0},{4,1},{5,2},{6,3},{7,4},{8,13},{9,14},{10,... | collective-permute-start | bytes 331784 | tf_op jit(solution)/shard_map/ppermute | solution.py:88
  71.4 20.0 %collective-permute-start.7 = (bf16[8,72,768]{2,1,0:T(8,128)(2,1)S(1)}, bf16[8,72,768]{2,1,0:T(8,128)(2,1)}, u32[]{:S(2)}, u32[]{:S(2)}) collective-permute-start(bf16[8,72,768]{2,1,0:T(8,128)(2,1)S(1)} %constant_dynamic-update-slice_fusion.26), channel_id=1, source_target_pairs={{0,8},{8,0},{16,24},{24,16},{1,9},{9,1},{17,25},{25,17},{2,10},{10... | collective-permute-start | bytes 2654216 | tf_op jit(solution)/shard_map/ppermute | solution.py:41
  71.5 20.9 %collective-permute-start.8 = (bf16[8,72,768]{2,1,0:T(8,128)(2,1)S(1)}, bf16[8,72,768]{2,1,0:T(8,128)(2,1)}, u32[]{:S(2)}, u32[]{:S(2)}) collective-permute-start(bf16[8,72,768]{2,1,0:T(8,128)(2,1)S(1)} %constant_dynamic-update-slice_fusion.26), channel_id=1, source_target_pairs={{0,16},{8,24},{16,0},{24,8},{1,17},{9,25},{17,1},{25,9},{2,18},{10... | collective-permute-start | bytes 2654216 | tf_op jit(solution)/shard_map/ppermute | solution.py:41
  127.5 135.3 %all-gather.7.cloned.1.call-start = ((), (), s32[]{:S(2)}) async-start(), calls=%async_computation.5 | async-start | bytes 4718592 | tf_op jit(solution)/shard_map/all_gather | solution.py:94
  182.9 93.2 %all-gather.13.cloned.1.call-start = ((), (), s32[]{:S(2)}) async-start(), calls=%async_computation.11 | async-start | bytes 4718592 | tf_op jit(solution)/shard_map/all_gather | solution.py:94
  183.5 163.7 %reduce-scatter.9.cloned.1.call-start = ((), (), s32[]{:S(2)}) async-start(), calls=%async_computation.7 | async-start | bytes 4718592 | tf_op jit(solution)/shard_map/reduce_scatter | solution.py:98
  183.9 53.5 %collective-permute-start.15 = (bf16[2,512,704]{1,2,0:T(8,128)(2,1)S(1)}, bf16[2,512,704]{1,2,0:T(8,128)(2,1)}, u32[]{:S(2)}, u32[]{:S(2)}) collective-permute-start(bf16[2,512,704]{1,2,0:T(8,128)(2,1)S(1)} %copy-done.6), channel_id=1, source_target_pairs={{0,8},{8,0},{16,24},{24,16},{1,9},{9,1},{17,25},{25,17},{2,10},{10... | collective-permute-start | bytes 4325384 | tf_op jit(solution)/shard_map/ppermute | solution.py:41
  185.2 54.9 %collective-permute-start.16 = (bf16[2,512,704]{1,2,0:T(8,128)(2,1)S(1)}, bf16[2,512,704]{1,2,0:T(8,128)(2,1)}, u32[]{:S(2)}, u32[]{:S(2)}) collective-permute-start(bf16[2,512,704]{1,2,0:T(8,128)(2,1)S(1)} %copy-done.6), channel_id=1, source_target_pairs={{0,16},{8,24},{16,0},{24,8},{1,17},{9,25},{17,1},{25,9},{2,18},{10... | collective-permute-start | bytes 4325384 | tf_op jit(solution)/shard_map/ppermute | solution.py:41
  186.4 45.6 %collective-permute-start.19 = (bf16[704,512]{1,0:T(8,128)(2,1)}, bf16[704,512]{1,0:T(8,128)(2,1)}, u32[]{:S(2)}, u32[]{:S(2)}) collective-permute-start(bf16[704,512]{1,0:T(8,128)(2,1)} %param.24), channel_id=1, source_target_pairs={{0,8},{8,0},{16,24},{24,16},{1,9},{9,1},{17,25},{25,17},{2,10},{10... | collective-permute-start | bytes 2162696 | tf_op jit(solution)/shard_map/ppermute | solution.py:41
  186.7 48.5 %collective-permute-start.20 = (bf16[704,512]{1,0:T(8,128)(2,1)}, bf16[704,512]{1,0:T(8,128)(2,1)}, u32[]{:S(2)}, u32[]{:S(2)}) collective-permute-start(bf16[704,512]{1,0:T(8,128)(2,1)} %param.24), channel_id=1, source_target_pairs={{0,16},{8,24},{16,0},{24,8},{1,17},{9,25},{17,1},{25,9},{2,18},{10... | collective-permute-start | bytes 2162696 | tf_op jit(solution)/shard_map/ppermute | solution.py:41
  238.7 20.4 %collective-permute-start.17 = (bf16[1,512,704]{1,2,0:T(8,128)(2,1)S(1)}, bf16[1,512,704]{1,2,0:T(8,128)(2,1)S(1)}, u32[]{:S(2)}, u32[]{:S(2)}) collective-permute-start(bf16[1,512,704]{1,2,0:T(8,128)(2,1)S(1)} %slice.249), channel_id=1, source_target_pairs={{0,16},{8,24},{16,0},{24,8},{1,17},{9,25},{17,1},{25,9},{2,18},{10... | collective-permute-start | bytes 2162696 | tf_op jit(solution)/shard_map/ppermute | solution.py:41
  241.3 20.6 %collective-permute-start.18 = (bf16[1,512,704]{1,2,0:T(8,128)(2,1)S(1)}, bf16[1,512,704]{1,2,0:T(8,128)(2,1)S(1)}, u32[]{:S(2)}, u32[]{:S(2)}) collective-permute-start(bf16[1,512,704]{1,2,0:T(8,128)(2,1)S(1)} %slice.250), channel_id=1, source_target_pairs={{0,8},{8,0},{16,24},{24,16},{1,9},{9,1},{17,25},{25,17},{2,10},{10... | collective-permute-start | bytes 2162696 | tf_op jit(solution)/shard_map/ppermute | solution.py:41
  298.7 98.7 %all-gather.9.cloned.1.call-start = ((), (), s32[]{:S(2)}) async-start(), calls=%async_computation.8 | async-start | bytes 4718592 | tf_op jit(solution)/shard_map/all_gather | solution.py:94
  351.6 271.4 %reduce-scatter.11.cloned.1.call-start = ((), (), s32[]{:S(2)}) async-start(), calls=%async_computation.9 | async-start | bytes 4718592 | tf_op jit(solution)/shard_map/reduce_scatter | solution.py:98
  426.4 198.1 %reduce-scatter.7.cloned.1.call-start = ((), (), s32[]{:S(2)}) async-start(), calls=%async_computation.6 | async-start | bytes 4718592 | tf_op jit(solution)/shard_map/reduce_scatter | solution.py:98
  441.2 27.0 %collective-permute-start.40 = (bf16[1,512,704]{1,2,0:T(8,128)(2,1)}, bf16[1,512,704]{1,2,0:T(8,128)(2,1)}, u32[]{:S(2)}, u32[]{:S(2)}) collective-permute-start(bf16[1,512,704]{1,2,0:T(8,128)(2,1)} %get-tuple-element.67), channel_id=1, source_target_pairs={{0,16},{8,24},{16,0},{24,8},{1,17},{9,25},{17,1},{25,9},{2,18},{10... | collective-permute-start | bytes 2162696 | tf_op jit(solution)/shard_map/ppermute | solution.py:41
  449.6 17.2 %collective-permute-start.44 = (bf16[352,512]{1,0:T(8,128)(2,1)}, bf16[352,512]{1,0:T(8,128)(2,1)}, u32[]{:S(2)}, u32[]{:S(2)}) collective-permute-start(bf16[352,512]{1,0:T(8,128)(2,1)} %get-tuple-element.64), channel_id=1, source_target_pairs={{0,16},{8,24},{16,0},{24,8},{1,17},{9,25},{17,1},{25,9},{2,18},{10... | collective-permute-start | bytes 1081352 | tf_op jit(solution)/shard_map/ppermute | solution.py:41
  450.8 22.8 %collective-permute-start.38 = (bf16[1,512,704]{1,2,0:T(8,128)(2,1)}, bf16[1,512,704]{1,2,0:T(8,128)(2,1)}, u32[]{:S(2)}, u32[]{:S(2)}) collective-permute-start(bf16[1,512,704]{1,2,0:T(8,128)(2,1)} %get-tuple-element.66), channel_id=1, source_target_pairs={{0,8},{8,0},{16,24},{24,16},{1,9},{9,1},{17,25},{25,17},{2,10},{10... | collective-permute-start | bytes 2162696 | tf_op jit(solution)/shard_map/ppermute | solution.py:41
  470.8 57.3 %collective-permute-start.41 = (bf16[2,512,704]{1,2,0:T(8,128)(2,1)}, bf16[2,512,704]{1,2,0:T(8,128)(2,1)}, u32[]{:S(2)}, u32[]{:S(2)}) collective-permute-start(bf16[2,512,704]{1,2,0:T(8,128)(2,1)} %pad_maximum_fusion.4), channel_id=1, source_target_pairs={{0,8},{8,0},{16,24},{24,16},{1,9},{9,1},{17,25},{25,17},{2,10},{10... | collective-permute-start | bytes 4325384 | tf_op jit(solution)/shard_map/ppermute | solution.py:41
  476.2 51.9 %collective-permute-start.39 = (bf16[2,512,704]{1,2,0:T(8,128)(2,1)}, bf16[2,512,704]{1,2,0:T(8,128)(2,1)}, u32[]{:S(2)}, u32[]{:S(2)}) collective-permute-start(bf16[2,512,704]{1,2,0:T(8,128)(2,1)} %pad_maximum_fusion.3), channel_id=1, source_target_pairs={{0,16},{8,24},{16,0},{24,8},{1,17},{9,25},{17,1},{25,9},{2,18},{10... | collective-permute-start | bytes 4325384 | tf_op jit(solution)/shard_map/ppermute | solution.py:41
  477.8 42.4 %collective-permute-start.45 = (bf16[704,512]{1,0:T(8,128)(2,1)S(1)}, bf16[704,512]{1,0:T(8,128)(2,1)}, u32[]{:S(2)}, u32[]{:S(2)}) collective-permute-start(bf16[704,512]{1,0:T(8,128)(2,1)S(1)} %pad_maximum_fusion.8), channel_id=1, source_target_pairs={{0,8},{8,0},{16,24},{24,16},{1,9},{9,1},{17,25},{25,17},{2,10},{10... | collective-permute-start | bytes 2162696 | tf_op jit(solution)/shard_map/ppermute | solution.py:41
  479.9 43.1 %collective-permute-start.43 = (bf16[704,512]{1,0:T(8,128)(2,1)}, bf16[704,512]{1,0:T(8,128)(2,1)S(1)}, u32[]{:S(2)}, u32[]{:S(2)}) collective-permute-start(bf16[704,512]{1,0:T(8,128)(2,1)} %pad_maximum_fusion.7), channel_id=1, source_target_pairs={{0,16},{8,24},{16,0},{24,8},{1,17},{9,25},{17,1},{25,9},{2,18},{10... | collective-permute-start | bytes 2162696 | tf_op jit(solution)/shard_map/ppermute | solution.py:41
  551.8 22.7 %collective-permute-start.26 = (bf16[8,72,768]{2,1,0:T(8,128)(2,1)S(1)}, bf16[8,72,768]{2,1,0:T(8,128)(2,1)S(1)}, u32[]{:S(2)}, u32[]{:S(2)}) collective-permute-start(bf16[8,72,768]{2,1,0:T(8,128)(2,1)S(1)} %pad_maximum_fusion.6), channel_id=1, source_target_pairs={{0,8},{8,0},{16,24},{24,16},{1,9},{9,1},{17,25},{25,17},{2,10},{10... | collective-permute-start | bytes 2654216 | tf_op jit(solution)/shard_map/ppermute | solution.py:41
  553.2 21.3 %collective-permute-start.24 = (bf16[8,72,768]{2,1,0:T(8,128)(2,1)S(1)}, bf16[8,72,768]{2,1,0:T(8,128)(2,1)S(1)}, u32[]{:S(2)}, u32[]{:S(2)}) collective-permute-start(bf16[8,72,768]{2,1,0:T(8,128)(2,1)S(1)} %pad_maximum_fusion.5), channel_id=1, source_target_pairs={{0,16},{8,24},{16,0},{24,8},{1,17},{9,25},{17,1},{25,9},{2,18},{10... | collective-permute-start | bytes 2654216 | tf_op jit(solution)/shard_map/ppermute | solution.py:41
  555.7 27.3 %collective-permute-start.37 = (bf16[64,2048]{1,0:T(8,128)(2,1)S(1)}, bf16[64,2048]{1,0:T(8,128)(2,1)S(1)}, u32[]{:S(2)}, u32[]{:S(2)}) collective-permute-start(bf16[64,2048]{1,0:T(8,128)(2,1)S(1)} %pad_maximum_fusion.10), channel_id=1, source_target_pairs={{0,8},{8,0},{16,24},{24,16},{1,9},{9,1},{17,25},{25,17},{2,10},{10... | collective-permute-start | bytes 786440 | tf_op jit(solution)/shard_map/ppermute | solution.py:41
  557.0 26.1 %collective-permute-start.35 = (bf16[64,2048]{1,0:T(8,128)(2,1)S(1)}, bf16[64,2048]{1,0:T(8,128)(2,1)S(1)}, u32[]{:S(2)}, u32[]{:S(2)}) collective-permute-start(bf16[64,2048]{1,0:T(8,128)(2,1)S(1)} %pad_maximum_fusion.9), channel_id=1, source_target_pairs={{0,16},{8,24},{16,0},{24,8},{1,17},{9,25},{17,1},{25,9},{2,18},{10... | collective-permute-start | bytes 786440 | tf_op jit(solution)/shard_map/ppermute | solution.py:41
  (56 other events, 809.8 us)
Sparse Core Ops, SparseCore 0:
  9.6 63.3 all-gather.10
  127.6 50.4 reduce-scatter.4
  183.0 45.6 all-gather.6
  230.2 45.8 all-gather.12
  298.9 48.3 reduce-scatter.8
  351.7 45.6 all-gather.8
  426.5 48.6 reduce-scatter.10
  485.1 50.0 reduce-scatter.6

commit v2 on v1

v2 whole, which is shorter than its diff:
```python
import functools
import math

import jax
import jax.numpy as jnp
from jax import lax
from jax.experimental import pallas as pl
from jax.experimental.pallas import tpu as pltpu
from jax.sharding import PartitionSpec as P

F = jnp.float32
B = jnp.bfloat16
HEADS = 32
HEAD_DIM = 64
ROT_DIMS = 16
HALF_ROT = ROT_DIMS // 2
NORM_EPS = 1e-05
NEG_LARGE = -1e30
SCORE_SCALE = 0.125
ROPE_BASE = 10000.0
BETA_ONE = 0.9
BETA_TWO = 0.95
BIAS_FIRST = 0.999973438601112
BIAS_SECOND = 0.994079470779667
ADAM_EPS = 1e-08
DECAY_RATE = 0.1
TOKEN_BLOCK = 256
EXTRA_ROWS = 8
NT = (((1,), (1,)), ((), ()))
TN = (((0,), (0,)), ((), ()))


def dotg(left, right, dims):
    return lax.dot_general(left, right, dims, preferred_element_type=F)


def plus(left, right):
    return (left.astype(F) + right.astype(F)).astype(B)


def rows_swap(value, bits):
    return lax.ppermute(value, "rows", [(i, i ^ bits) for i in range(4)])


class RowsGather:
    def __init__(self, shard, axis):
        self.axis = axis
        self.size = shard.shape[axis]
        self.step = self.whole = None
        if lax.axis_size("rows") == 4:
            self.shard = shard
            self.step = (rows_swap(shard, 1), rows_swap(shard, 2))
        else:
            self.whole = lax.all_gather(shard, "rows", axis=axis, tiled=True)

    def before(self, *values):
        if self.step is not None:
            near, far, *values = tie(*self.step, *values)
            self.step = (near, far)
        return values if len(values) > 1 else values[0]

    def second(self):
        if self.step is not None:
            self.near, self.far = self.step
            half = self.size // 2
            first = lax.slice_in_dim(self.near, 0, half, axis=self.axis)
            last = lax.slice_in_dim(self.far, half, self.size, axis=self.axis)
            self.step = (rows_swap(first, 2), rows_swap(last, 1))
        return self

    def pieces(self):
        if self.whole is not None:
            return [self.whole], [jnp.int32(0)]
        me = lax.axis_index("rows")
        places = [(me ^ bits) * self.size for bits in range(4)]
        arrays = [self.shard, self.near, self.far, *self.step]
        return arrays, places + [places[3] + self.size // 2]

    def join(self):
        if self.whole is not None:
            return self.whole
        shape = list(self.shard.shape)
        shape[self.axis] = 4 * self.size
        whole = jnp.zeros(shape, self.shard.dtype)
        for piece, place in zip(*self.pieces()):
            whole = lax.dynamic_update_slice_in_dim(whole, piece, place, self.axis)
        return whole


class RowsSum:
    def __init__(self, whole, axis):
        self.whole, self.axis = whole, axis
        self.arrived = self.sent = None
        if lax.axis_size("rows") == 4:
            diagonal = self.part(3)
            half = diagonal.shape[0] // 2
            self.arrived = (rows_swap(diagonal[:half], 1), rows_swap(diagonal[half:], 2))

    def part(self, bits):
        size = self.whole.shape[self.axis] // 4
        start = (lax.axis_index("rows") ^ bits) * size
        return lax.dynamic_slice_in_dim(self.whole, start, size, self.axis)

    def before(self, value):
        if self.arrived is not None:
            near, far, value = tie(*self.arrived, value)
            self.arrived = (near, far)
        return value

    def result(self):
        if self.arrived is None:
            return lax.psum_scatter(
                self.whole, "rows", scatter_dimension=self.axis, tiled=True
            ).astype(F)
        if self.sent is None:
            self.second()
        far, near = self.sent
        return self.part(0).astype(F) + far.astype(F) + near.astype(F)

    def arrived_or_whole(self):
        return (self.whole,) if self.arrived is None else self.arrived

    def second(self):
        if self.arrived is None:
            return self.whole, self.whole
        near, far = self.part(1), self.part(2)
        half = near.shape[0] // 2
        far = jnp.concatenate([plus(far[:half], self.arrived[0]), far[half:]], 0)
        near = jnp.concatenate([near[:half], plus(near[half:], self.arrived[1])], 0)
        self.sent = (rows_swap(far, 2), rows_swap(near, 1))
        return far, near

    def after(self, *values):
        if self.arrived is None:
            self.whole, *values = tie(self.whole, *values)
        else:
            far, near, *values = tie(*self.sent, *values)
            self.sent = (far, near)
        return values if len(values) > 1 else values[0]


def wide_exchange(blocks, between=None):
    count = lax.axis_size("wide")
    me = lax.axis_index("wide")
    whole = jnp.zeros(blocks.shape, blocks.dtype)
    moved = []
    for step in range(count):
        block = lax.dynamic_slice_in_dim(blocks, (me + step) % count, 1, 0)
        if step:
            block = lax.ppermute(block, "wide", [(i, (i + step) % count) for i in range(count)])
        moved.append(block)
    values = ()
    if between is not None:
        half = count // 2
        moved[half:], values = split_tie(moved[half:], between(moved[:half]))
    for step, block in enumerate(moved):
        whole = lax.dynamic_update_slice_in_dim(whole, block, (me - step) % count, 0)
    return whole, values


def wide_gather(shard):
    return lax.all_gather(shard, "wide", axis=0, tiled=True)


def wide_scatter(whole):
    return lax.psum_scatter(whole, "wide", scatter_dimension=0, tiled=True)


def tie(*values):
    return lax.optimization_barrier(values)


def split_tie(first, second):
    values = list(tie(*first, *second))
    return values[: len(first)], values[len(first) :]


def chip_pairs(move):
    pairs = []
    for at in range(lax.axis_size("wide")):
        target = move(at // 2, at % 2)
        if target is not None:
            pairs.append((at, target[0] * 2 + target[1]))
    return pairs


def core_swap(value):
    return lax.ppermute(value, "wide", chip_pairs(lambda chip, core: (chip, 1 - core)))


def line_step(right, left, step, spread):
    chips = lax.axis_size("wide") // 2

    def sends(passed):
        return step <= passed if spread else passed <= step

    right = lax.ppermute(
        right,
        "wide",
        chip_pairs(
            lambda chip, core: (chip + 1, core) if chip < chips - 1 and sends(chip) else None
        ),
    )
    left = lax.ppermute(
        left,
        "wide",
        chip_pairs(
            lambda chip, core: (chip - 1, core) if 0 < chip and sends(chips - 1 - chip) else None
        ),
    )
    return right, left


class LineSum:
    def __init__(self, whole):
        self.chips = lax.axis_size("wide") // 2
        at = lax.axis_index("wide")
        self.chip, core = at // 2, at % 2
        size = whole.shape[0] // (2 * self.chips)
        parts = whole.reshape((self.chips, 2, size) + whole.shape[1:])
        mine = lax.dynamic_index_in_dim(parts, core, 1, False)
        swapped = core_swap(lax.dynamic_index_in_dim(parts, 1 - core, 1, False))
        self.parts = plus(mine, swapped)
        self.flows = None
        self.step = 0

    def part(self, chip):
        return lax.dynamic_index_in_dim(self.parts, jnp.clip(chip, 0, self.chips - 1), 0, False)

    def prepare(self):
        to_right = self.part(self.chips - 1 - self.step + self.chip)
        to_left = self.part(self.step - (self.chips - 1 - self.chip))
        if self.flows is not None:
            to_right = plus(to_right, self.flows[0])
            to_left = plus(to_left, self.flows[1])
        self.flows = (to_right, to_left)

    def advance(self):
        self.flows = line_step(*self.flows, self.step, False)
        self.step += 1

    def before(self, value):
        right, left, value = tie(*self.flows, value)
        self.flows = (right, left)
        return value

    def result(self):
        while self.step < self.chips - 1:
            self.prepare()
            self.advance()
        return self.part(self.chip).astype(F) + self.flows[0].astype(F) + self.flows[1].astype(F)


def rotated(value, same, ahead, behind):
    width = value.shape[1]
    return (
        value * same
        + pltpu.roll(value, width - HALF_ROT, 1) * ahead
        + pltpu.roll(value, HALF_ROT, 1) * behind
    )


def unrotated(value, same, ahead, behind):
    width = value.shape[1]
    return value * same - (
        pltpu.roll(value, width - HALF_ROT, 1) * ahead
        + pltpu.roll(value, HALF_ROT, 1) * behind
    )


def wide_tables(width, *refs):
    return [jnp.concatenate([ref[...]] * (width // ref.shape[1]), 1) for ref in refs]


def tables_body(col_ref, row_ref, same_ref, ahead_ref, behind_ref):
    tokens, lanes = same_ref.shape
    col = col_ref[...]
    before = jnp.zeros((tokens, 1), jnp.int32)
    for first in range(0, tokens, TOKEN_BLOCK):
        smaller = row_ref[:, first : first + TOKEN_BLOCK] < col
        before += jnp.sum(jnp.where(smaller, 1, 0), axis=1, keepdims=True)
    positions = lax.broadcasted_iota(jnp.int32, (tokens, 1), 0) - before
    dim = lax.broadcasted_iota(jnp.int32, (1, lanes), 1) % HEAD_DIM
    frequency = jnp.exp((dim % HALF_ROT).astype(F) * (-2.0 * math.log(ROPE_BASE) / ROT_DIMS))
    angles = positions.astype(F) * frequency
    cosine, sine = jnp.cos(angles), jnp.sin(angles)
    same_ref[...] = jnp.where(dim < ROT_DIMS, cosine, 1.0)
    ahead_ref[...] = jnp.where(dim < HALF_ROT, -sine, 0.0)
    behind_ref[...] = jnp.where((dim >= HALF_ROT) & (dim < ROT_DIMS), sine, 0.0)


def rotary_tables(seg_col, seg_line):
    tokens = seg_col.shape[0]
    return pl.pallas_call(
        tables_body,
        out_shape=[jax.ShapeDtypeStruct((tokens, 2 * HEAD_DIM), F)] * 3,
        name="tables",
    )(seg_col, seg_line)


def unit_rows(tensor):
    center = tensor - jnp.mean(tensor, axis=-1, keepdims=True)
    inverse = lax.rsqrt(jnp.mean(center * center, axis=-1, keepdims=True) + NORM_EPS)
    return center * inverse, inverse


def cost(products, values):
    return pl.CostEstimate(flops=2 * products, transcendentals=0, bytes_accessed=values)


def project_body(pieces, depth, norm_size, *refs):
    place_ref, x_ref, same_ref, ahead_ref, behind_ref = refs[:5]
    w_refs = refs[5 : 5 + pieces]
    q_ref, k_ref, v_ref, hat_ref, w_ref, norms_ref, bias_ref = refs[5 + pieces :]

    @pl.when(pl.program_id(0) == 0)
    def _():
        bias_ref[...] = jnp.zeros_like(bias_ref)
        for at, piece in enumerate(w_refs):
            blocks = piece.shape[0]
            rows = pl.multiple_of(place_ref[at] * depth, blocks * depth)
            columns = pl.multiple_of(place_ref[at] * norm_size, blocks * norm_size)
            for block in range(blocks):
                w_ref[pl.ds(rows + block * depth, depth), :] = piece[block, :depth]
                bias_ref[...] += piece[block, depth + 4 : depth + 5].astype(F)
            norms = [piece[block, depth : depth + 4, :norm_size].astype(F) for block in range(blocks)]
            norms_ref[:, pl.ds(columns, blocks * norm_size)] = jnp.concatenate(norms, 1)

    hat, _ = unit_rows(x_ref[...].astype(F))
    normed = (hat * norms_ref[0:1, :] + norms_ref[1:2, :]).astype(B)
    hat_ref[...] = hat.astype(B)
    out = jnp.dot(normed, w_ref[...], preferred_element_type=F) + bias_ref[...]
    width = q_ref.shape[1]
    tables = wide_tables(width, same_ref, ahead_ref, behind_ref)
    q_ref[...] = rotated(out[:, :width], *tables).astype(B)
    k_ref[...] = rotated(out[:, width : 2 * width], *tables).astype(B)
    v_ref[...] = out[:, 2 * width :].astype(B)


def row_spec(width, block):
    return pl.BlockSpec((block, width), lambda i: (i, 0))


def whole_spec(array):
    return pl.BlockSpec(array.shape, lambda i: (0, 0))


def project(x_all, gathered, tables, depth, norm_size):
    tokens, features = x_all.shape
    pieces, places = gathered.pieces()
    columns = pieces[0].shape[2]
    width = columns // 3
    block = min(TOKEN_BLOCK, tokens)
    row = lambda size: pl.BlockSpec((block, size), lambda i, place: (i, 0))
    flat = lambda *shape: pl.BlockSpec(shape, lambda i, place: (0,) * len(shape))
    return pl.pallas_call(
        functools.partial(project_body, len(pieces), depth, norm_size),
        grid_spec=pltpu.PrefetchScalarGridSpec(
            num_scalar_prefetch=1,
            grid=(tokens // block,),
            in_specs=[row(features)]
            + [row(table.shape[1]) for table in tables]
            + [flat(*piece.shape) for piece in pieces],
            out_specs=[row(width)] * 3
            + [row(features), flat(features, columns), flat(4, features), flat(1, columns)],
        ),
        out_shape=[jax.ShapeDtypeStruct((tokens, width), B)] * 3
        + [
            jax.ShapeDtypeStruct((tokens, features), B),
            jax.ShapeDtypeStruct((features, columns), B),
            jax.ShapeDtypeStruct((4, features), F),
            jax.ShapeDtypeStruct((1, columns), F),
        ],
        name="project",
        cost_estimate=cost(tokens * features * columns, 4 * tokens * features),
    )(jnp.stack(places), x_all, *tables, *pieces)


def gate_body(pieces, *refs):
    place_ref, tokens_ref = refs[:2]
    gate_ref, up_ref, hidden_ref = refs[2 + 2 * pieces :]
    sums = []
    for half in range(2):
        total = jnp.zeros(gate_ref.shape, F)
        for at in range(pieces):
            w_ref = refs[2 + half * pieces + at]
            size = w_ref.shape[1]
            columns = pl.ds(pl.multiple_of(place_ref[at], size), size)
            total += dotg(tokens_ref[:, columns], w_ref[...], NT)
        sums.append(total)
    gate_ref[...] = sums[0]
    up_ref[...] = sums[1]
    hidden_ref[...] = (sums[0] * jax.nn.sigmoid(sums[0]) * sums[1]).astype(B)


def piece_call(body, name, places, blocked, pieces, outs, products):
    tokens = blocked[0].shape[0]
    block = min(TOKEN_BLOCK, tokens)

    def spec(shape):
        if len(shape) == 3:
            return pl.BlockSpec((shape[0], block, shape[2]), lambda i, place: (0, i, 0))
        return pl.BlockSpec((block, shape[1]), lambda i, place: (i, 0))

    size = sum(array.size * array.dtype.itemsize for array in blocked + pieces)
    return pl.pallas_call(
        functools.partial(body, len(places)),
        grid_spec=pltpu.PrefetchScalarGridSpec(
            num_scalar_prefetch=1,
            grid=(tokens // block,),
            in_specs=[spec(array.shape) for array in blocked]
            + [pl.BlockSpec(piece.shape, lambda i, place: (0, 0)) for piece in pieces],
            out_specs=[spec(out.shape) for out in outs],
        ),
        out_shape=outs,
        name=name,
        cost_estimate=cost(products, size),
    )(jnp.stack(places), *blocked, *pieces)


def gate_up_forward(tokens_all, gate, up):
    tokens = tokens_all.shape[0]
    gates, places = gate.pieces()
    ups, _ = up.pieces()
    units = gates[0].shape[0]
    outs = [jax.ShapeDtypeStruct((tokens, units), kind) for kind in (F, F, B)]
    products = 2 * tokens * units * tokens_all.shape[1]
    return piece_call(gate_body, "gate_up", places, [tokens_all], gates + ups, outs, products)


def down_body(pieces, *refs):
    place_ref, hidden_ref = refs[:2]
    out_ref = refs[2 + pieces]
    for at in range(pieces):
        w_ref = refs[2 + at]
        size = w_ref.shape[1]
        columns = pl.ds(pl.multiple_of(place_ref[at], size), size)
        out_ref[:, columns] = jnp.dot(
            hidden_ref[...], w_ref[...], preferred_element_type=F
        ).astype(B)


def down_forward(hidden, down, features):
    tokens, units = hidden.shape
    downs, places = down.pieces()
    outs = [jax.ShapeDtypeStruct((tokens, features), B)]
    return piece_call(
        down_body, "down", places, [hidden], downs, outs, tokens * units * features
    )[0]


def feed_back_body(pieces, *refs):
    place_ref, grads_ref, gate_ref, up_ref = refs[:4]
    weights = refs[4 : 4 + 3 * pieces]
    out_ref, e_ref = refs[4 + 3 * pieces :]
    grad_hidden = jnp.zeros(gate_ref.shape, F)
    for at in range(pieces):
        size = weights[at].shape[1]
        columns = pl.ds(pl.multiple_of(place_ref[at], size), size)
        grad_hidden += dotg(grads_ref[:, columns], weights[at][...], NT)
    gate = gate_ref[...]
    sigmoid = jax.nn.sigmoid(gate)
    grad_gate = grad_hidden * up_ref[...] * sigmoid * (1.0 + gate * (1.0 - sigmoid))
    grad_gate = grad_gate.astype(B)
    grad_up = (grad_hidden * (gate * sigmoid)).astype(B)
    out_ref[0] = grad_gate
    out_ref[1] = grad_up
    for at in range(pieces):
        size = weights[at].shape[1]
        columns = pl.ds(pl.multiple_of(place_ref[at], size), size)
        e = jnp.dot(grad_gate, weights[pieces + at][...], preferred_element_type=F)
        e += jnp.dot(grad_up, weights[2 * pieces + at][...], preferred_element_type=F)
        e_ref[:, columns] = e.astype(B)


def feed_back(grads_all, gate_part, up_part, down, gate, up):
    tokens, features = grads_all.shape
    units = gate_part.shape[1]
    downs, places = down.pieces()
    outs = [
        jax.ShapeDtypeStruct((2, tokens, units), B),
        jax.ShapeDtypeStruct((tokens, features), B),
    ]
    weights = downs + gate.pieces()[0] + up.pieces()[0]
    return piece_call(
        feed_back_body,
        "feed_back",
        places,
        [grads_all, gate_part, up_part],
        weights,
        outs,
        3 * tokens * units * features,
    )


def pair_bias(seg_col, seg_row, first, size, keys):
    same = seg_col[first : first + size, :] == seg_row[:, :keys]
    key_pos = lax.broadcasted_iota(jnp.int32, (size, keys), 1)
    query_pos = first + lax.broadcasted_iota(jnp.int32, (size, keys), 0)
    return jnp.where(same & (key_pos <= query_pos), 0.0, NEG_LARGE)


def head_masks(heads, width):
    lane = lax.broadcasted_iota(jnp.int32, (1, width), 1) // HEAD_DIM
    return [jnp.where(lane == head, 1.0, 0.0).astype(B) for head in range(heads)]


def attend_body(heads, q_ref, k_ref, v_ref, seg_col, seg_row, out_ref, lse_ref):
    tokens, width = q_ref.shape
    block = min(TOKEN_BLOCK, tokens)
    masks = head_masks(heads, width)
    for first in range(0, tokens, block):
        keys = first + block
        bias = pair_bias(seg_col, seg_row, first, block, keys)
        queries = q_ref[first:keys, :]
        total = jnp.zeros((block, width), F)
        for head in range(heads):
            scores = dotg(queries * (masks[head] * SCORE_SCALE), k_ref[:keys, :], NT) + bias
            top = jnp.max(scores, axis=-1, keepdims=True)
            weights = jnp.exp(scores - top)
            norm = jnp.sum(weights, axis=-1, keepdims=True)
            probs = (weights * (1.0 / norm)).astype(B)
            total += jnp.dot(probs, v_ref[:keys, :] * masks[head], preferred_element_type=F)
            lse_ref[first:keys, head : head + 1] = top + jnp.log(norm)
        out_ref[first:keys, :] = total.astype(B)


def attend(q, k, v, seg_col, seg_row, heads):
    tokens, width = q.shape
    return pl.pallas_call(
        functools.partial(attend_body, heads),
        out_shape=[
            jax.ShapeDtypeStruct((tokens, width), B),
            jax.ShapeDtypeStruct((tokens, 128), F),
        ],
        name="attend",
        cost_estimate=cost(heads * tokens * tokens * 512, 8 * tokens * width),
    )(q, k, v, seg_col, seg_row)


def out_project_body(
    core_ref, attended_ref, same_ref, other_ref, x_ref, norm_ref, normed_ref, after_ref
):
    core = core_ref[0]
    width = attended_ref.shape[2]
    total = x_ref[...].astype(F)
    for chip in range(same_ref.shape[1]):
        for w_ref, which in ((same_ref, core), (other_ref, 1 - core)):
            weights = w_ref[:, chip].reshape(width, w_ref.shape[3])
            total += jnp.dot(attended_ref[chip * 2 + which], weights, preferred_element_type=F)
    after_ref[...] = total
    hat, _ = unit_rows(total)
    normed_ref[...] = (hat * norm_ref[0:1, :] + norm_ref[1:2, :]).astype(B)


def out_project(core, attended_all, out_same, out_other, x_all, norm_two):
    owners, tokens, width = attended_all.shape
    features = x_all.shape[1]
    block = min(TOKEN_BLOCK, tokens)
    weights = pl.BlockSpec(out_same.shape, lambda i, core: (0, 0, 0, 0))
    rows = pl.BlockSpec((block, features), lambda i, core: (i, 0))
    return pl.pallas_call(
        out_project_body,
        grid_spec=pltpu.PrefetchScalarGridSpec(
            num_scalar_prefetch=1,
            grid=(tokens // block,),
            in_specs=[
                pl.BlockSpec((owners, block, width), lambda i, core: (0, i, 0)),
                weights,
                weights,
                rows,
                pl.BlockSpec(norm_two.shape, lambda i, core: (0, 0)),
            ],
            out_specs=[rows, rows],
        ),
        out_shape=[
            jax.ShapeDtypeStruct((tokens, features), B),
            jax.ShapeDtypeStruct((tokens, features), F),
        ],
        name="out_project",
        cost_estimate=cost(tokens * features * features, 8 * tokens * features),
    )(core, attended_all, out_same, out_other, x_all, norm_two)


def attend_back_body(
    heads, q_ref, k_ref, v_ref, g_ref, lse_ref, seg_col, seg_row, same_ref, ahead_ref, behind_ref,
    out_ref, bias_ref, dq_ref, dk_ref, dv_ref,
):
    tokens, width = q_ref.shape
    block = min(TOKEN_BLOCK, tokens)
    masks = head_masks(heads, width)
    for first in reversed(range(0, tokens, block)):
        keys = first + block
        bias = pair_bias(seg_col, seg_row, first, block, keys)
        queries = q_ref[first:keys, :]
        grads = g_ref[first:keys, :]
        dq = jnp.zeros((block, width), F)
        stacks = ([], [], [], [])
        for head in range(heads):
            q_head = queries * (masks[head] * SCORE_SCALE)
            g_head = grads * masks[head]
            scores = dotg(q_head, k_ref[:keys, :], NT) + bias
            probs = jnp.exp(scores - lse_ref[first:keys, head : head + 1])
            weighted = probs * dotg(g_head, v_ref[:keys, :], NT)
            delta = jnp.sum(weighted, axis=-1, keepdims=True)
            grad_scores = (weighted - probs * delta).astype(B)
            dq += jnp.dot(grad_scores, k_ref[:keys, :] * masks[head], preferred_element_type=F)
            for stack, value in zip(stacks, (grad_scores, q_head, probs.astype(B), g_head)):
                stack.append(value)
        joined = [jnp.concatenate(stack, 0) for stack in stacks]
        dk = dotg(joined[0], joined[1], TN)
        dv = dotg(joined[2], joined[3], TN)
        if keys == tokens:
            dk_ref[...] = dk
            dv_ref[...] = dv
        else:
            dk_ref[:keys, :] += dk
            dv_ref[:keys, :] += dv
        dq_ref[first:keys, :] = dq * SCORE_SCALE
    tables = wide_tables(width, same_ref, ahead_ref, behind_ref)
    pieces = (unrotated(dq_ref[...], *tables), unrotated(dk_ref[...], *tables), dv_ref[...])
    for at, piece in enumerate(pieces):
        rounded = piece.astype(B)
        out_ref[:, at * width : (at + 1) * width] = rounded
        bias_ref[:, at * width : (at + 1) * width] = jnp.sum(
            rounded.astype(F), axis=0, keepdims=True
        )


def attend_back(q, k, v, grads, lse, seg_col, seg_row, tables, heads):
    tokens, width = q.shape
    return pl.pallas_call(
        functools.partial(attend_back_body, heads),
        out_shape=[
            jax.ShapeDtypeStruct((tokens, 3 * width), B),
            jax.ShapeDtypeStruct((1, 3 * width), F),
        ],
        scratch_shapes=[pltpu.VMEM((tokens, width), F)] * 3,
        name="attend_back",
        cost_estimate=cost(heads * tokens * tokens * 1024, 16 * tokens * width),
    )(q, k, v, grads, lse, seg_col, seg_row, *tables)


def weights_back_body(
    depth, norm_size, hat_ref, grad_ref, w_ref, norms_ref, two_ref, bias_ref, out_ref
):
    blocks, rows, columns = out_ref.shape
    product = dotg(hat_ref[...], grad_ref[...], TN)
    weights = w_ref[...].astype(F)
    bias = bias_ref[...]
    gain = jnp.sum(product * weights, axis=1, keepdims=True)
    shift = jnp.sum(weights * bias, axis=1, keepdims=True)
    lanes = lax.broadcasted_iota(jnp.int32, (gain.shape[0], 128), 1)
    ones = jnp.where(lanes == 0, gain, shift).T
    norms = jnp.concatenate([norms_ref[...]] * 2, 0).T
    product = (product * norms[:, 0:1] + norms[:, 1:2] * bias).astype(B)
    sums = jnp.concatenate([ones[:2], two_ref[...]], 0).astype(B)
    bias = bias.astype(B)
    for block in range(blocks):
        out_ref[block, :depth, :] = product[block * depth : (block + 1) * depth]
        mine = sums[:, block * norm_size : (block + 1) * norm_size]
        out_ref[block, depth:, :] = jnp.concatenate(
            [
                jnp.concatenate([mine, jnp.zeros((4, columns - norm_size), B)], 1),
                bias,
                jnp.zeros((rows - depth - 5, columns), B),
            ],
            0,
        )


def weights_back(hat_all, grad_proj, w_mine, norms, two, bias_grad, depth, norm_size):
    tokens, features = hat_all.shape
    columns = grad_proj.shape[1]
    block = min(256, features)
    flat = lambda array: pl.BlockSpec(array.shape, lambda i: (0, 0))
    across = lambda rows: pl.BlockSpec((rows, block), lambda i: (0, i))
    return pl.pallas_call(
        functools.partial(weights_back_body, depth, norm_size),
        grid=(features // block,),
        in_specs=[
            across(tokens),
            flat(grad_proj),
            row_spec(columns, block),
            across(4),
            across(2),
            flat(bias_grad),
        ],
        out_specs=pl.BlockSpec((block // depth, depth + EXTRA_ROWS, columns), lambda i: (i, 0, 0)),
        out_shape=jax.ShapeDtypeStruct((features // depth, depth + EXTRA_ROWS, columns), B),
        name="weights_back",
        cost_estimate=cost(tokens * features * columns, 4 * tokens * features),
    )(hat_all, grad_proj, w_mine, norms, two, bias_grad)


def norm_back_body(e_ref, x_ref, upstream_ref, gain_ref, grad_ref, *refs):
    hat, inverse = unit_rows(x_ref[...].astype(F))
    e = e_ref[...].astype(F)
    scaled = e * gain_ref[...]
    mean_grad = jnp.mean(scaled, axis=-1, keepdims=True)
    mean_proj = jnp.mean(scaled * hat, axis=-1, keepdims=True)
    grad = upstream_ref[...].astype(F) + inverse * (scaled - mean_grad - hat * mean_proj)
    grad_ref[...] = grad
    if refs:
        rounded_ref, sums_ref = refs
        rounded_ref[...] = grad.astype(B)
        sums_ref[...] = jnp.concatenate(
            [jnp.sum(e * hat, axis=0, keepdims=True), jnp.sum(e, axis=0, keepdims=True)], 0
        )


def norm_back(e, x, upstream, gain, more):
    tokens, features = x.shape
    outs = [jax.ShapeDtypeStruct((tokens, features), F)]
    if more:
        outs += [jax.ShapeDtypeStruct((tokens, features), B), jax.ShapeDtypeStruct((2, features), F)]
    return pl.pallas_call(norm_back_body, out_shape=outs, name="norm_back")(e, x, upstream, gain)


def pack_body(strided, me_ref, w_ref, norm_ref, bias_ref, out_ref):
    wide, _, columns = out_ref.shape
    depth = w_ref.shape[0]
    third = w_ref.shape[1] // 3
    width = columns // 3
    me = me_ref[0]
    held = bias_ref.shape[1]
    padded = jnp.concatenate(
        [norm_ref[...], jnp.zeros((4, columns - norm_ref.shape[1]), B)], 1
    )
    for owner in range(wide):
        biases = []
        for part in range(3):
            for slot in range(width // HEAD_DIM):
                head = slot * wide + owner if strided else owner * (width // HEAD_DIM) + slot
                first = part * third + head * HEAD_DIM
                if slot % 2 == 0:
                    left = w_ref[:, first : first + HEAD_DIM]
                else:
                    to = part * width + (slot - 1) * HEAD_DIM
                    out_ref[owner, :depth, to : to + 2 * HEAD_DIM] = jnp.concatenate(
                        [left, w_ref[:, first : first + HEAD_DIM]], 1
                    )
                last = first + HEAD_DIM
                while first < last:
                    stop = min(last, (first // held + 1) * held)
                    mine = bias_ref[:, first % held : first % held + stop - first]
                    kept = jnp.where(me == first // held, mine.astype(F), 0.0)
                    biases.append(kept.astype(B))
                    first = stop
        out_ref[owner, depth:, :] = jnp.concatenate(
            [padded, jnp.concatenate(biases, 1), jnp.zeros((EXTRA_ROWS - 5, columns), B)], 0
        )


def pack(me, w_qkv, norm_params, b_qkv, strided, wide):
    depth, columns = w_qkv.shape
    memory = [pltpu.SMEM] + [pltpu.VMEM] * 3
    return pl.pallas_call(
        functools.partial(pack_body, strided),
        in_specs=[pl.BlockSpec(memory_space=space) for space in memory],
        out_shape=jax.ShapeDtypeStruct((wide, depth + EXTRA_ROWS, columns // wide), B),
        name="pack",
    )(me[None].astype(jnp.int32), w_qkv, norm_params, b_qkv[None])


def adam_step(parameter, gradient, moments):
    first_moment = BETA_ONE * moments[0] + (1.0 - BETA_ONE) * gradient
    second_moment = BETA_TWO * moments[1] + (1.0 - BETA_TWO) * gradient * gradient
    return first_moment / BIAS_FIRST / (
        jnp.sqrt(second_moment / BIAS_SECOND) + ADAM_EPS
    ) + DECAY_RATE * parameter.astype(F)


def finish_body(strided, wide, got_ref, w_ref, moment_ref, grad_ref, step_ref):
    depth = w_ref.shape[0]
    third = w_ref.shape[1] // 3
    width = got_ref.shape[2] // 3
    for part in range(3):
        for at in range(third // 128):
            if strided:
                slot, owner = at * 2 // wide, at * 2 % wide
                first = part * width + slot * HEAD_DIM
                gradient = jnp.concatenate(
                    [got_ref[owner + k, :depth, first : first + HEAD_DIM] for k in range(2)], 1
                )
            else:
                owner, first = at * 128 // width, part * width + at * 128 % width
                gradient = got_ref[owner, :depth, first : first + 128]
            gradient = gradient.astype(F)
            columns = slice(part * third + at * 128, part * third + at * 128 + 128)
            grad_ref[:, columns] = gradient
            step_ref[:, columns] = adam_step(
                w_ref[:, columns], gradient, (moment_ref[0, :, columns], moment_ref[1, :, columns])
            )


def finish(received, w_qkv, moments, strided):
    return pl.pallas_call(
        functools.partial(finish_body, strided, received.shape[0]),
        out_shape=[jax.ShapeDtypeStruct(w_qkv.shape, F)] * 2,
        name="finish",
    )(received, w_qkv, moments)


def shards(
    block_input, out_grad, segment_ids, positions, norm_params, w_qkv, b_qkv, w_out, gate_up, w_down,
    moment_norm, moment_qkv, moment_bias, moment_out, moment_gate, moment_down,
):
    x_own = block_input[0]
    local_len, features = x_own.shape
    rows = lax.axis_size("rows")
    wide = lax.axis_size("wide")
    my_row = lax.axis_index("rows")
    my_wide = lax.axis_index("wide")
    segment_row = segment_ids[0]
    heads = HEADS // wide
    width = heads * HEAD_DIM
    depth = w_qkv.shape[0]
    norm_size = norm_params.shape[1]
    strided = depth == HEAD_DIM

    bias_size = b_qkv.shape[0]
    chips = wide // 2
    core = my_wide % 2
    blocks = range(rows * wide)
    back = [(b % rows * wide + b // rows, b) for b in blocks]
    received, _ = wide_exchange(
        pack(my_row * wide + my_wide, w_qkv, norm_params, b_qkv, strided, wide)
    )
    received, x_first, segment_row = tie(received, x_own, segment_row)
    x_all = wide_gather(x_first)
    w_rows = RowsGather(received, 0)
    seg_col = segment_row[:, None]
    seg_line = segment_row[None, :]
    tables = w_rows.before(*rotary_tables(seg_col, seg_line))
    w_rows.second()
    gate_first = w_rows.before(gate_up.swapaxes(1, 2))
    gate = RowsGather(gate_first[0], 1)
    if strided:
        x_all, out_first = w_rows.before(x_all, w_out)
        out_line = lax.all_gather(out_first, "wide", axis=0, tiled=False)
    q, k, v, hat_all, w_mine, norms, _ = project(x_all, w_rows, tables, depth, norm_size)
    up = RowsGather(gate_first[1], 1)
    attended, lse = attend(q, k, v, seg_col, seg_line, heads)
    attended = gate.before(up.before(attended))
    if strided:
        attended, out_line = tie(attended, out_line)
    attended_all = lax.all_gather(attended, "wide", axis=0, tiled=False)
    if strided:
        out_line = out_line.reshape(chips, 2, depth, features)
        out_line = lax.dynamic_index_in_dim(out_line, core, 1, False)
        out_rows = RowsGather(out_line.reshape(chips * depth, features), 0)
        out_rows.second()
        out_rows.step = gate.before(*out_rows.step)
        out_rows.step = up.before(*out_rows.step)
        out_same = out_rows.join()
        out_other = core_swap(out_same)
        shape = (rows, chips, depth, features)
    else:
        shape = (1, chips, width, features)
        out_all = lax.all_gather(w_out, ("rows", "wide"), axis=0, tiled=True)
        out_all = out_all.reshape(chips, 2, width, features)
        out_same = lax.dynamic_index_in_dim(out_all, core, 1, False)
        out_other = lax.dynamic_index_in_dim(out_all, 1 - core, 1, False)
    out_same, out_other = out_same.reshape(shape), out_other.reshape(shape)
    out_mine = lax.dynamic_index_in_dim(out_same, my_wide // 2, 1, False).reshape(width, features)
    gate.second()
    up.second()
    attended_all, out_same, upstream, down_first = up.before(
        *gate.before(attended_all, out_same, out_grad[0], w_down)
    )
    grads_all = wide_gather(upstream)
    down = RowsGather(down_first, 1)
    tokens_all, after_all = out_project(
        core[None].astype(jnp.int32), attended_all, out_same, out_other, x_all, norms[2:]
    )
    tokens_all = down.before(tokens_all)
    after_attn = lax.dynamic_slice_in_dim(after_all, my_wide * local_len, local_len, 0)
    gate_part, up_part, hidden = gate_up_forward(tokens_all, gate, up)
    down.second()

    gate_grads, e_two = feed_back(grads_all, gate_part, up_part, down, gate, up)
    grad_normed_two = wide_scatter(e_two)
    gate_grads, hidden, tokens_all, grads_all = tie(gate_grads, hidden, tokens_all, grads_all)
    gate_grad = jnp.einsum("gtf,td->gfd", gate_grads, tokens_all, preferred_element_type=F).astype(B)
    down_grad = jnp.einsum("tf,td->fd", hidden, grads_all, preferred_element_type=F).astype(B)
    grad_down = RowsSum(down_grad, 1)
    grad_gate = RowsSum(gate_grad, 2)
    grad_normed_two = grad_gate.before(grad_down.before(grad_normed_two))
    hidden, *_ = tie(hidden, *grad_down.second(), *grad_gate.second())
    mlp_sum = LineSum(down_forward(hidden, down, features))
    mlp_sum.prepare()

    grad_after, branch, sums_two = norm_back(
        grad_normed_two, after_attn, out_grad[0], norms[2:3], True
    )
    branch_all = wide_gather(branch)
    branch_all = mlp_sum.before(branch_all)
    mlp_sum.advance()
    grad_attended = dotg(branch_all, out_mine, NT).astype(B)
    grad_proj, bias_grad = attend_back(
        q, k, v, grad_attended, lse, seg_col, seg_line, tables, heads
    )
    grad_proj = grad_gate.after(grad_down.after(grad_proj))
    grad_proj = mlp_sum.before(grad_proj)
    mlp_sum.prepare()
    mlp_sum.advance()
    e_one = dotg(grad_proj, w_mine, NT).astype(B)
    e_one, grad_proj = tie(e_one, grad_proj)
    grad_normed_one = wide_scatter(e_one)
    packed = weights_back(
        hat_all, grad_proj, w_mine, norms, sums_two, bias_grad, depth, norm_size
    )
    qkv_sum = RowsSum(packed, 0)
    branch_all = qkv_sum.before(branch_all)
    sent = qkv_sum.second()
    branch_all, *_ = tie(branch_all, *sent)
    grad_out = RowsSum(dotg(attended, branch_all, TN).astype(B), 0)
    qkv_sum.after(*grad_out.arrived_or_whole())
    grad_out.second()
    mlp_sum.before(qkv_sum.whole)
    mlp_sum.prepare()
    mlp_sum.advance()

    def late(first):
        outs = []
        for total in (grad_out, grad_gate, grad_down):
            first = total.after(*first)
            outs.append(total.result())
        if not strided:
            outs[0] = lax.ppermute(outs[0].astype(B), ("rows", "wide"), back).astype(F)
        grads = (outs[0], outs[1].swapaxes(1, 2), outs[2])
        steps = [
            adam_step(*parts)
            for parts in zip((w_out, gate_up, w_down), grads, (moment_out, moment_gate, moment_down))
        ]
        return grads + tuple(steps)

    received, late_values = wide_exchange(qkv_sum.result().astype(B), late)
    grad_out, grad_gate, grad_down, step_out, step_gate, step_down = late_values
    input_grad = norm_back(grad_normed_one, x_own, grad_after, norms[0:1], False)[0]

    received = mlp_sum.before(received)
    block_out = (after_attn + mlp_sum.result()).astype(B)
    received, input_grad = tie(received, input_grad)
    grad_qkv, step_qkv = finish(received, w_qkv, moment_qkv, strided)
    extra = received[:, depth : depth + 5].astype(F)
    grad_norms = jnp.sum(extra[:, :4, :norm_size], axis=0)
    bias_all = extra[:, 4].reshape(wide, 3, heads, HEAD_DIM)
    bias_all = bias_all.transpose((1, 2, 0, 3) if strided else (1, 0, 2, 3)).reshape(-1)
    grad_bias = lax.dynamic_slice_in_dim(
        bias_all, (my_row * wide + my_wide) * bias_size, bias_size, 0
    )

    return (
        block_out[None],
        input_grad[None],
        grad_norms,
        grad_qkv,
        grad_bias,
        grad_out,
        grad_gate,
        grad_down,
        adam_step(norm_params, grad_norms, moment_norm),
        step_qkv,
        adam_step(b_qkv, grad_bias, moment_bias),
        step_out,
        step_gate,
        step_down,
    )


def solution(mesh):
    both = ("rows", "wide")
    tokens = P("rows", "wide", None)
    weights = (P(None, both), P(both, None), P(both), P(both, None), P(None, "rows", "wide"), P("wide", "rows"))
    moments = tuple(P(None, *spec) for spec in weights)
    return jax.shard_map(
        shards,
        mesh=mesh,
        in_specs=(tokens, tokens, P("rows", None), P("rows", "wide")) + weights + moments,
        out_specs=(tokens, tokens) + weights + weights,
        check_vma=False,
    )
```

time: 644 us -> 515 us (0.80)
  waiting for transfers between devices: 344 us -> 200 us
  Pallas kernels: 43.3 us -> 125 us
  matrix products: 65.1 us -> 26.5 us
  local copies, waits for them, and re-layouts: 71.1 us -> 41.8 us
  starting transfers between devices: 51.1 us -> 69.1 us
  other arithmetic: 45.2 us -> 30.9 us
    reduce_scatter x4 -> x2, waiting for transfers between devices: 98.6 us -> 8.93 us  [wide_scatter(): return lax.psum_scatter(whole, 'wide', scatter_dimension=0, tiled=True)]
    pallas_call x2 -> x11, Pallas kernels: 19.6 us -> 102 us  [the longest x3 41.1 us: piece_call(): pl.pallas_call(functools.partial(body, len(places)), grid_spec=pltpu.Pref...]
    dot_general x6 -> x1, matrix products: 50.5 us -> 9.11 us  [shards(): jnp.einsum('gtf,td->gfd', gate_grads, tokens_all, preferred_element_type=F)]
    ppermute x32 -> x36, waiting for transfers between devices: 137 us -> 96 us  [rows_swap(): return lax.ppermute(value, 'rows', [(i, i ^ bits) for i in range(4)])]
    ppermute x14, waiting for transfers between devices: 59.6 us -> 25.4 us  [wide_exchange(): lax.ppermute(block, 'wide', [(i, (i + step) % count) for i in range(count)])]
    ppermute x0 -> x8, waiting for transfers between devices: none -> 27.3 us  [the longest x3 11.9 us: line_step(): lax.ppermute(right, 'wide', chip_pairs(lambda chip, core: (chip + 1, core...]
    ppermute x0 -> x8, starting transfers between devices: none -> 19.9 us  [the longest x3 8.7 us: line_step(): lax.ppermute(right, 'wide', chip_pairs(lambda chip, core: (chip + 1, core...]
    another operation x13 -> x6, local copies, waits for them, and re-layouts: 12.4 us -> 1.47 us  [the longest x1 0.65 us: piece_call(): jnp.stack(places)]
  transfers between devices with their start and end apart: 54 -> 65, of which waited for: 30 -> 33; matrix products, arithmetic and copies ran while one was open for 21% -> 16% of each run, Pallas kernels for 0% -> 18%
where the time goes in v2:
time: 515 us; the launch traced here: 509 us
  waiting for transfers between devices  200 us (39%)
  Pallas kernels  125 us (24%)
  starting transfers between devices  69.1 us (13%)
  local copies, waits for them, and re-layouts  41.8 us (8%)
  other arithmetic  30.9 us (6%)
  matrix products  26.5 us (5%)
  between operations  15.4 us (3%)
    ppermute x36, waiting for transfers between devices, rows_swap(): return lax.ppermute(value, 'rows', [(i, i ^ bits) for i in range(4)])  96 us
    all_gather x3, waiting for transfers between devices, wide_gather(): return lax.all_gather(shard, 'wide', axis=0, tiled=True)  41.7 us
    pallas_call x3, Pallas kernels, piece_call(): pl.pallas_call(functools.partial(body, len(places)), grid_spec=pltpu.Pref...  41.1 us
    ppermute x36, starting transfers between devices, rows_swap(): return lax.ppermute(value, 'rows', [(i, i ^ bits) for i in range(4)])  29.7 us
    ppermute x14, waiting for transfers between devices, wide_exchange(): lax.ppermute(block, 'wide', [(i, (i + step) % count) for i in range(count)])  25.4 us
    ppermute x14, starting transfers between devices, wide_exchange(): lax.ppermute(block, 'wide', [(i, (i + step) % count) for i in range(count)])  18.5 us
    pallas_call x1, Pallas kernels, out_project(): pl.pallas_call(out_project_body, grid_spec=pltpu.PrefetchScalarGridSpec(n...  17.2 us
    pallas_call x1, Pallas kernels, attend_back(): pl.pallas_call(functools.partial(attend_back_body, heads), out_shape=[jax...  14.8 us
  transfers between devices with their start and end apart: 65, of which 33 were waited for; matrix products, arithmetic and copies ran while one was open for 16% of the time, Pallas kernels for 18%

profile of v2, /device:TPU:9, one launch (start us, length us, event | category | flops | bytes accessed | tf_op | source)
XLA Modules:
  0.0 508.5 jit_solution(459946795543171660)
XLA Ops:
  20.7 9.2 %collective-permute-done.1 = bf16[1,72,768]{2,1,0:T(8,128)(2,1)S(1)} collective-permute-done((bf16[1,72,768]{2,1,0:T(8,128)(2,1)S(1)}, bf16[1,72,768]{2,1,0:T(8,128)(2,1)S(1)}, u32[]{:S(2)}, u32[]{:S(2)}) %collective-permute-start.1) | collective-permute-done | bytes 110624 | tf_op jit(solution)/shard_map/ppermute | solution.py:150
  37.9 5.4 %tables.1 = (f32[1024,128]{1,0:T(8,128)}, f32[1024,128]{1,0:T(8,128)}, f32[1024,128]{1,0:T(8,128)}) custom-call(s32[1024,1]{1,0:T(8,128)} %copy.31.col_ref.seg_col, s32[1,1024]{1,0:T(1,128)} %param.18), custom_call_target="tpu_custom_call" | custom-call | tf_op jit(solution)/shard_map/tables/pallas_call | solution.py:294
  43.3 9.4 %collective-permute-done.8.refs_7_ = bf16[8,72,768]{2,1,0:T(8,128)(2,1)S(1)} collective-permute-done((bf16[8,72,768]{2,1,0:T(8,128)(2,1)S(1)}, bf16[8,72,768]{2,1,0:T(8,128)(2,1)S(1)}, u32[]{:S(2)}, u32[]{:S(2)}) %collective-permute-start.8) | collective-permute-done | bytes 884768 | tf_op jit(solution)/shard_map/ppermute | solution.py:42
  56.7 5.9 %collective-permute-done.10.refs_9_ = bf16[4,72,768]{2,1,0:T(8,128)(2,1)S(1)} collective-permute-done((bf16[4,72,768]{2,1,0:T(8,128)(2,1)S(1)}, bf16[4,72,768]{2,1,0:T(8,128)(2,1)S(1)}, u32[]{:S(2)}, u32[]{:S(2)}) %collective-permute-start.10) | collective-permute-done | bytes 442400 | tf_op jit(solution)/shard_map/ppermute | solution.py:42
  64.5 19.3 %all-gather.8.cloned.1.call-done.refs_1_.x_ref = bf16[1024,2048]{1,0:T(8,128)(2,1)} async-done(((bf16[128,2048]{1,0:T(8,128)(2,1)}), bf16[1024,2048]{1,0:T(8,128)(2,1)}) %all-gather.8.cloned.1.call-update) | async-done | bytes 4194320 | tf_op jit(solution)/shard_map/all_gather | solution.py:162
  88.5 12.7 %project.1 = (bf16[1024,256]{1,0:T(8,128)(2,1)}, bf16[1024,256]{1,0:T(8,128)(2,1)}, bf16[1024,256]{1,0:T(8,128)(2,1)}, bf16[1024,2048]{1,0:T(8,128)(2,1)}, bf16[...) custom-call(s32[5]{0:T(128)} %stack.53.refs_0_, ...), custom_call_target="tpu_custom_call" | custom-call | flops 3221225472 | bytes 8388608 | tf_op jit(solution)/shard_map/project/pallas_call | solution.py:356
  101.2 8.2 %attend.1 = (bf16[1024,256]{1,0:T(8,128)(2,1)}, f32[1024,128]{1,0:T(8,128)}) custom-call(bf16[1024,256]{1,0:T(8,128)(2,1)} %get-tuple-element.156.q_ref, bf16[1024,256]{1,0:T(8,128)(2,1)} %get-tuple-element.157.k_ref, bf16[1024,256]{1,0:T(8,128)(2,1)} %get-tuple-element.158.v_ref, s32[1024,1]{1,0:T(8,128)} %copy.31.col_ref.seg_col, s32[1,1024]{1,0:T(1,128)} %param.18), custom_call_target="tpu_custom_call" | custom-call | flops 4294967296 | bytes 2097152 | tf_op jit(solution)/shard_map/attend/pallas_call | solution.py:530
  109.4 8.8 %collective-permute-done.14.refs_4_.refs_11_ = bf16[704,512]{1,0:T(8,128)(2,1)} collective-permute-done((bf16[704,512]{1,0:T(8,128)(2,1)S(1)}, bf16[704,512]{1,0:T(8,128)(2,1)}, u32[]{:S(2)}, u32[]{:S(2)}) %collective-permute-start.14) | collective-permute-done | bytes 720928 | tf_op jit(solution)/shard_map/ppermute | solution.py:42
  122.1 21.8 %collective-permute-done.17 = bf16[256,2048]{1,0:T(8,128)(2,1)S(1)} collective-permute-done((bf16[256,2048]{1,0:T(8,128)(2,1)S(1)}, bf16[256,2048]{1,0:T(8,128)(2,1)S(1)}, u32[]{:S(2)}, u32[]{:S(2)}) %collective-permute-start.17) | collective-permute-done | bytes 1048608 | tf_op jit(solution)/shard_map/ppermute | solution.py:42
  167.4 7.5 %collective-permute-done.20.refs_11_.refs_18_ = bf16[704,256]{1,0:T(8,128)(2,1)} collective-permute-done((bf16[704,256]{1,0:T(8,128)(2,1)S(1)}, bf16[704,256]{1,0:T(8,128)(2,1)}, u32[]{:S(2)}, u32[]{:S(2)}) %collective-permute-start.20) | collective-permute-done | bytes 360480 | tf_op jit(solution)/shard_map/ppermute | solution.py:42
  175.3 4.6 collective-permute-start.23
  187.0 17.2 %out_project.1 = (bf16[1024,2048]{1,0:T(8,128)(2,1)}, f32[1024,2048]{1,0:T(8,128)}) custom-call(s32[1]{0:T(128)} %bitcast.core_ref, bf16[8,1024,256]{2,1,0:T(8,128)(2,1)} %bitcast.136, bf16[4,4,64,2048]{3,2,1,0:T(8,128)(2,1)} %bitcast.18.same_ref, bf16[4,4,64,2048]{3,2,1,0:T(8,128)(2,1)} %bitcast.20.other_ref, ...), custom_call_target="tpu_custom_call" | custom-call | flops 8589934592 | bytes 16777216 | tf_op jit(solution)/shard_map/out_project/pallas_call | solution.py:562
  207.3 12.4 %gate_up.1 = (f32[1024,704]{1,0:T(8,128)}, f32[1024,704]{1,0:T(8,128)}, bf16[1024,704]{1,0:T(8,128)(2,1)}) custom-call(s32[5]{0:T(128)} %stack.59.refs_0_, bf16[1024,2048]{1,0:T(8,128)(2,1)} %get-tuple-element.205.refs_1_, bf16[704,512]{1,0:T(8,128)(2,1)} %copy-done.11, bf16[704,512]{1,0:T(8,128)(2,1)} %collective-permute-done.13.refs_3_.refs_10_, ...), custom_call_target="tpu_custom_call" | custom-call | flops 5905580032 | bytes 9961472 | tf_op jit(solution)/shard_map/gate_up/pallas_call | solution.py:406
  219.8 4.7 all-gather.10.cloned.1.call-done.refs_1_
  224.5 20.8 %feed_back.1 = (bf16[2,1024,704]{2,1,0:T(8,128)(2,1)}, bf16[1024,2048]{1,0:T(8,128)(2,1)}) custom-call(s32[5]{0:T(128)} %stack.59.refs_0_, bf16[1024,2048]{1,0:T(8,128)(2,1)} %all-gather.10.cloned.1.call-done.refs_1_, f32[1024,704]{1,0:T(8,128)} %get-tuple-element.193.refs_2_, f32[1024,704]{1,0:T(8,128)} %get-tuple-element.194.refs_3_, ...), custom_call_target="tpu_custom_call" | custom-call | flops 8858370048 | bytes 18612224 | tf_op jit(solution)/shard_map/feed_back/pallas_call | solution.py:406
  245.7 9.1 %convolution_convert_fusion = bf16[2,704,2048]{2,1,0:T(8,128)(2,1)S(1)} fusion(bf16[2,1024,704]{2,1,0:T(8,128)(2,1)} %get-tuple-element.204, bf16[1024,2048]{1,0:T(8,128)(2,1)} %get-tuple-element.205.refs_1_), kind=kOutput, calls=%fused_computation | convolution fusion | flops 5908463616 | bytes 12845056 | tf_op jit(solution)/shard_map/gtf,td->gfd/dot_general | solution.py:885
  271.4 12.6 %collective-permute-done.28 = bf16[352,512]{1,0:T(8,128)(2,1)} collective-permute-done((bf16[352,512]{1,0:T(8,128)(2,1)S(1)}, bf16[352,512]{1,0:T(8,128)(2,1)}, u32[]{:S(2)}, u32[]{:S(2)}) %collective-permute-start.28) | collective-permute-done | bytes 360480 | tf_op jit(solution)/shard_map/ppermute | solution.py:42
  284.8 8.9 %reduce-scatter.3.cloned.1.call-done.e_ref = bf16[128,2048]{1,0:T(8,128)(2,1)} async-done(((bf16[1024,2048]{1,0:T(8,128)(2,1)}), bf16[128,2048]{1,0:T(8,128)(2,1)}) %reduce-scatter.3.cloned.1.call-update) | async-done | bytes 524304 | tf_op jit(solution)/shard_map/reduce_scatter | solution.py:166
  306.3 7.9 %down.1 = bf16[1024,2048]{1,0:T(8,128)(2,1)} custom-call(s32[5]{0:T(128)} %stack.59.refs_0_, bf16[1024,704]{1,0:T(8,128)(2,1)} %get-tuple-element.209.refs_1_, bf16[704,512]{1,0:T(8,128)(2,1)} %refs_2_, bf16[704,512]{1,0:T(8,128)(2,1)} %collective-permute-done.24.refs_5_.refs_3_, bf16[704,512]{1,0:T(8,128)(2,1)} %copy-done.16, ...), custom_call_target="tpu_custom_call" | custom-call | flops 2952790016 | bytes 4325376 | tf_op jit(solution)/shard_map/down/pallas_call | solution.py:406
  325.5 17.7 %all-gather.12.cloned.1.call-done = bf16[1024,2048]{1,0:T(8,128)(2,1)} async-done(((bf16[128,2048]{1,0:T(8,128)(2,1)}), bf16[1024,2048]{1,0:T(8,128)(2,1)}) %all-gather.12.cloned.1.call-update) | async-done | bytes 4194320 | tf_op jit(solution)/shard_map/all_gather | solution.py:162
  344.5 4.6 convolution_convert_fusion.4.g_ref
  350.7 14.8 %attend_back.1 = (bf16[1024,768]{1,0:T(8,128)(2,1)}, f32[1,768]{1,0:T(1,128)}) custom-call(bf16[1024,256]{1,0:T(8,128)(2,1)} %get-tuple-element.156.q_ref, bf16[1024,256]{1,0:T(8,128)(2,1)} %get-tuple-element.157.k_ref, bf16[1024,256]{1,0:T(8,128)(2,1)} %get-tuple-element.158.v_ref, bf16[1024,256]{1,0:T(8,128)(2,1)} %convolution_convert_fusion.4.g_ref, ...), custom_call_target="tpu_custom_call" | custom-call | flops 8589934592 | bytes 4194304 | tf_op jit(solution)/shard_map/attend_back/pallas_call | solution.py:632
  367.8 8.1 %convolution_convert_fusion.1 = bf16[1024,2048]{1,0:T(8,128)(2,1)} fusion(bf16[1024,768]{1,0:T(8,128)(2,1)} %get-tuple-element.224.grad_ref, bf16[2048,768]{1,0:T(8,128)(2,1)} %get-tuple-element.223.w_ref), kind=kOutput, calls=%fused_computation.5 | convolution fusion | flops 3223322624 | bytes 8912896 | tf_op jit(solution)/shard_map/dot_general | solution.py:34
  376.6 6.7 %fusion.7 = (f32[2,512,704]{1,2,0:T(8,128)}, f32[2,512,704]{1,2,0:T(8,128)}) fusion(bf16[2,512,704]{1,2,0:T(8,128)(2,1)S(1)} %copy-done.2, f32[2,2,512,704]{2,3,1,0:T(8,128)} %param.29, bf16[2,704,512]{2,1,0:T(8,128)(2,1)} %collective-permute-done.36, bf16[2,704,512]{2,1,0:T(8,128)(2,1)} %collective-permute-done.35, bf16[2,704,2048]{2,1,0:T(8,128)(2,1)} %copy-done.1, ...), kind=kLoop, calls=%fused_computation.12 | loop fusion | flops 13697024 | bytes 17301508 | tf_op jit(solution)/shard_map/add | solution.py:769
  383.2 11.6 %weights_back.1 = bf16[32,72,768]{2,1,0:T(8,128)(2,1)} custom-call(bf16[1024,2048]{1,0:T(8,128)(2,1)} %get-tuple-element.221.hat_ref, bf16[1024,768]{1,0:T(8,128)(2,1)} %get-tuple-element.224.grad_ref, bf16[2048,768]{1,0:T(8,128)(2,1)} %get-tuple-element.223.w_ref, f32[4,2048]{1,0:T(4,128)} %get-tuple-element.183.norms_ref, ...), custom_call_target="tpu_custom_call" | custom-call | flops 3221225472 | bytes 8388608 | tf_op jit(solution)/shard_map/weights_back/pallas_call | solution.py:678
  410.7 4.4 fusion.14
  415.7 11.2 %collective-permute-done.40 = bf16[128,2048]{1,0:T(8,128)(2,1)S(1)} collective-permute-done((bf16[128,2048]{1,0:T(8,128)(2,1)S(1)}, bf16[128,2048]{1,0:T(8,128)(2,1)S(1)}, u32[]{:S(2)}, u32[]{:S(2)}) %collective-permute-start.40) | collective-permute-done | bytes 524320 | tf_op jit(solution)/shard_map/ppermute | solution.py:204
  433.3 12.4 %collective-permute-done.46 = bf16[8,72,768]{2,1,0:T(8,128)(2,1)S(1)} collective-permute-done((bf16[8,72,768]{2,1,0:T(8,128)(2,1)S(1)}, bf16[8,72,768]{2,1,0:T(8,128)(2,1)S(1)}, u32[]{:S(2)}, u32[]{:S(2)}) %collective-permute-start.46) | collective-permute-done | bytes 884768 | tf_op jit(solution)/shard_map/ppermute | solution.py:42
  446.2 5.6 %collective-permute-start.51 = (bf16[1,72,768]{2,1,0:T(8,128)(2,1)S(1)}, bf16[1,72,768]{2,1,0:T(8,128)(2,1)S(1)}, u32[]{:S(2)}, u32[]{:S(2)}) collective-permute-start(bf16[1,72,768]{2,1,0:T(8,128)(2,1)S(1)} %get-tuple-element.308), channel_id=1, source_target_pairs={{0,3},{1,4},{2,5},{3,6},{4,7},{5,0},{6,1},{7,2},{8,11},{9,12},{10,... | collective-permute-start | bytes 331784 | tf_op jit(solution)/shard_map/ppermute | solution.py:150
  464.0 9.5 %collective-permute-done.55 = bf16[1,72,768]{2,1,0:T(8,128)(2,1)S(1)} collective-permute-done((bf16[1,72,768]{2,1,0:T(8,128)(2,1)S(1)}, bf16[1,72,768]{2,1,0:T(8,128)(2,1)S(1)}, u32[]{:S(2)}, u32[]{:S(2)}) %collective-permute-start.55) | collective-permute-done | bytes 110624 | tf_op jit(solution)/shard_map/ppermute | solution.py:150
  478.2 10.8 %collective-permute-done.41 = bf16[128,2048]{1,0:T(8,128)(2,1)S(1)} collective-permute-done((bf16[128,2048]{1,0:T(8,128)(2,1)S(1)}, bf16[128,2048]{1,0:T(8,128)(2,1)S(1)}, u32[]{:S(2)}, u32[]{:S(2)}) %collective-permute-start.41) | collective-permute-done | bytes 524320 | tf_op jit(solution)/shard_map/ppermute | solution.py:197
  494.8 5.3 %finish.1 = (f32[64,6144]{1,0:T(8,128)}, f32[64,6144]{1,0:T(8,128)}) custom-call(bf16[8,72,768]{2,1,0:T(8,128)(2,1)} %copy-done.3, bf16[64,6144]{1,0:T(8,128)(2,1)} %w_ref.3, f32[2,64,6144]{2,1,0:T(8,128)} %moment_ref.1), custom_call_target="tpu_custom_call" | custom-call | tf_op jit(solution)/shard_map/finish/pallas_call | solution.py:798
  (264 shorter events, 164.2 us)
Async XLA Ops:
  7.2 76.6 %all-gather.8.cloned.1.call-start = ((), (), s32[]{:S(2)}) async-start(), calls=%async_computation.2 | async-start | bytes 4718592 | tf_op jit(solution)/shard_map/all_gather | solution.py:162
  14.2 19.9 %collective-permute-start.6 = (bf16[1,72,768]{2,1,0:T(8,128)(2,1)S(1)}, bf16[1,72,768]{2,1,0:T(8,128)(2,1)S(1)}, u32[]{:S(2)}, u32[]{:S(2)}) collective-permute-start(bf16[1,72,768]{2,1,0:T(8,128)(2,1)S(1)} %get-tuple-element.312), channel_id=1, source_target_pairs={{0,7},{1,0},{2,1},{3,2},{4,3},{5,4},{6,5},{7,6},{8,15},{9,8},{10,9... | collective-permute-start | bytes 331784 | tf_op jit(solution)/shard_map/ppermute | solution.py:150
  14.2 19.9 %collective-permute-start.5 = (bf16[1,72,768]{2,1,0:T(8,128)(2,1)S(1)}, bf16[1,72,768]{2,1,0:T(8,128)(2,1)S(1)}, u32[]{:S(2)}, u32[]{:S(2)}) collective-permute-start(bf16[1,72,768]{2,1,0:T(8,128)(2,1)S(1)} %get-tuple-element.313), channel_id=1, source_target_pairs={{0,6},{1,7},{2,0},{3,1},{4,2},{5,3},{6,4},{7,5},{8,14},{9,15},{10,... | collective-permute-start | bytes 331784 | tf_op jit(solution)/shard_map/ppermute | solution.py:150
  14.4 19.7 %collective-permute-start.4 = (bf16[1,72,768]{2,1,0:T(8,128)(2,1)S(1)}, bf16[1,72,768]{2,1,0:T(8,128)(2,1)S(1)}, u32[]{:S(2)}, u32[]{:S(2)}) collective-permute-start(bf16[1,72,768]{2,1,0:T(8,128)(2,1)S(1)} %get-tuple-element.314), channel_id=1, source_target_pairs={{0,5},{1,6},{2,7},{3,0},{4,1},{5,2},{6,3},{7,4},{8,13},{9,14},{10,... | collective-permute-start | bytes 331784 | tf_op jit(solution)/shard_map/ppermute | solution.py:150
  34.2 84.9 %all-gather.14.cloned.1.call-start = ((), (), s32[]{:S(2)}) async-start(), calls=%async_computation.7 | async-start | bytes 2359296 | tf_op jit(solution)/shard_map/all_gather | solution.py:841
  83.8 83.6 %all-gather.16.cloned.1.call-start = ((), (), s32[]{:S(2)}) async-start(), calls=%async_computation.8 | async-start | bytes 4718592 | tf_op jit(solution)/shard_map/all_gather | solution.py:848
  85.0 24.4 %collective-permute-start.12 = (bf16[704,512]{1,0:T(8,128)(2,1)}, bf16[704,512]{1,0:T(8,128)(2,1)S(1)}, u32[]{:S(2)}, u32[]{:S(2)}) collective-permute-start(bf16[704,512]{1,0:T(8,128)(2,1)} %get-tuple-element.297.refs_7_.refs_14_), channel_id=1, source_target_pairs={{0,16},{8,24},{16,0},{24,8},{1,17},{9,25},{17,1},{25,9},{2,18},{10... | collective-permute-start | bytes 2162696 | tf_op jit(solution)/shard_map/ppermute | solution.py:42
  86.2 23.2 %collective-permute-start.11 = (bf16[704,512]{1,0:T(8,128)(2,1)}, bf16[704,512]{1,0:T(8,128)(2,1)}, u32[]{:S(2)}, u32[]{:S(2)}) collective-permute-start(bf16[704,512]{1,0:T(8,128)(2,1)} %get-tuple-element.297.refs_7_.refs_14_), channel_id=1, source_target_pairs={{0,8},{8,0},{16,24},{24,16},{1,9},{9,1},{17,25},{25,17},{2,10},{10... | collective-permute-start | bytes 2162696 | tf_op jit(solution)/shard_map/ppermute | solution.py:42
  87.4 30.9 %collective-permute-start.14 = (bf16[704,512]{1,0:T(8,128)(2,1)S(1)}, bf16[704,512]{1,0:T(8,128)(2,1)}, u32[]{:S(2)}, u32[]{:S(2)}) collective-permute-start(bf16[704,512]{1,0:T(8,128)(2,1)S(1)} %get-tuple-element.296.refs_2_.refs_9_), channel_id=1, source_target_pairs={{0,16},{8,24},{16,0},{24,8},{1,17},{9,25},{17,1},{25,9},{2,18},{10... | collective-permute-start | bytes 2162696 | tf_op jit(solution)/shard_map/ppermute | solution.py:42
  87.7 31.5 %collective-permute-start.13 = (bf16[704,512]{1,0:T(8,128)(2,1)S(1)}, bf16[704,512]{1,0:T(8,128)(2,1)}, u32[]{:S(2)}, u32[]{:S(2)}) collective-permute-start(bf16[704,512]{1,0:T(8,128)(2,1)S(1)} %get-tuple-element.296.refs_2_.refs_9_), channel_id=1, source_target_pairs={{0,8},{8,0},{16,24},{24,16},{1,9},{9,1},{17,25},{25,17},{2,10},{10... | collective-permute-start | bytes 2162696 | tf_op jit(solution)/shard_map/ppermute | solution.py:42
  119.2 105.3 %all-gather.10.cloned.1.call-start = ((), (), s32[]{:S(2)}) async-start(), calls=%async_computation.3 | async-start | bytes 4718592 | tf_op jit(solution)/shard_map/all_gather | solution.py:162
  120.5 23.4 %collective-permute-start.17 = (bf16[256,2048]{1,0:T(8,128)(2,1)S(1)}, bf16[256,2048]{1,0:T(8,128)(2,1)S(1)}, u32[]{:S(2)}, u32[]{:S(2)}) collective-permute-start(bf16[256,2048]{1,0:T(8,128)(2,1)S(1)} %bitcast.122), channel_id=1, source_target_pairs={{0,16},{8,24},{16,0},{24,8},{1,17},{9,25},{17,1},{25,9},{2,18},{10... | collective-permute-start | bytes 3145736 | tf_op jit(solution)/shard_map/ppermute | solution.py:42
  120.9 24.3 %collective-permute-start.15 = (bf16[256,2048]{1,0:T(8,128)(2,1)S(1)}, bf16[256,2048]{1,0:T(8,128)(2,1)}, u32[]{:S(2)}, u32[]{:S(2)}) collective-permute-start(bf16[256,2048]{1,0:T(8,128)(2,1)S(1)} %bitcast.123), channel_id=1, source_target_pairs={{0,8},{8,0},{16,24},{24,16},{1,9},{9,1},{17,25},{25,17},{2,10},{10... | collective-permute-start | bytes 3145736 | tf_op jit(solution)/shard_map/ppermute | solution.py:42
  175.0 118.7 %reduce-scatter.3.cloned.1.call-start = ((), (), s32[]{:S(2)}) async-start(), calls=%async_computation.4 | async-start | bytes 4718592 | tf_op jit(solution)/shard_map/reduce_scatter | solution.py:166
  181.2 23.0 %collective-permute-start.25 = (bf16[704,512]{1,0:T(8,128)(2,1)S(1)}, bf16[704,512]{1,0:T(8,128)(2,1)S(1)}, u32[]{:S(2)}, u32[]{:S(2)}) collective-permute-start(bf16[704,512]{1,0:T(8,128)(2,1)S(1)} %copy-done.9), channel_id=1, source_target_pairs={{0,16},{8,24},{16,0},{24,8},{1,17},{9,25},{17,1},{25,9},{2,18},{10... | collective-permute-start | bytes 2162696 | tf_op jit(solution)/shard_map/ppermute | solution.py:42
  181.7 22.5 %collective-permute-start.24 = (bf16[704,512]{1,0:T(8,128)(2,1)S(1)}, bf16[704,512]{1,0:T(8,128)(2,1)}, u32[]{:S(2)}, u32[]{:S(2)}) collective-permute-start(bf16[704,512]{1,0:T(8,128)(2,1)S(1)} %copy-done.9), channel_id=1, source_target_pairs={{0,8},{8,0},{16,24},{24,16},{1,9},{9,1},{17,25},{25,17},{2,10},{10... | collective-permute-start | bytes 2162696 | tf_op jit(solution)/shard_map/ppermute | solution.py:42
  245.3 97.9 %all-gather.12.cloned.1.call-start = ((), (), s32[]{:S(2)}) async-start(), calls=%async_computation.5 | async-start | bytes 4718592 | tf_op jit(solution)/shard_map/all_gather | solution.py:162
  258.5 35.3 %collective-permute-start.30 = (bf16[1,704,512]{2,1,0:T(8,128)(2,1)}, bf16[1,704,512]{2,1,0:T(8,128)(2,1)}, u32[]{:S(2)}, u32[]{:S(2)}) collective-permute-start(bf16[1,704,512]{2,1,0:T(8,128)(2,1)} %get-tuple-element.273), channel_id=1, source_target_pairs={{0,8},{8,0},{16,24},{24,16},{1,9},{9,1},{17,25},{25,17},{2,10},{10... | collective-permute-start | bytes 2162696 | tf_op jit(solution)/shard_map/ppermute | solution.py:42
  259.6 34.1 %collective-permute-start.31 = (bf16[1,704,512]{2,1,0:T(8,128)(2,1)}, bf16[1,704,512]{2,1,0:T(8,128)(2,1)}, u32[]{:S(2)}, u32[]{:S(2)}) collective-permute-start(bf16[1,704,512]{2,1,0:T(8,128)(2,1)} %get-tuple-element.274), channel_id=1, source_target_pairs={{0,16},{8,24},{16,0},{24,8},{1,17},{9,25},{17,1},{25,9},{2,18},{10... | collective-permute-start | bytes 2162696 | tf_op jit(solution)/shard_map/ppermute | solution.py:42
  297.3 194.0 %reduce-scatter.5.cloned.1.call-start = ((), (), s32[]{:S(2)}) async-start(), calls=%async_computation.6 | async-start | bytes 4718592 | tf_op jit(solution)/shard_map/reduce_scatter | solution.py:166
  318.4 30.6 %collective-permute-start.37 = (bf16[704,512]{1,0:T(8,128)(2,1)}, bf16[704,512]{1,0:T(8,128)(2,1)}, u32[]{:S(2)}, u32[]{:S(2)}) collective-permute-start(bf16[704,512]{1,0:T(8,128)(2,1)} %pad_maximum_fusion.4), channel_id=1, source_target_pairs={{0,16},{8,24},{16,0},{24,8},{1,17},{9,25},{17,1},{25,9},{2,18},{10... | collective-permute-start | bytes 2162696 | tf_op jit(solution)/shard_map/ppermute | solution.py:42
  319.6 45.9 %collective-permute-start.38 = (bf16[704,512]{1,0:T(8,128)(2,1)}, bf16[704,512]{1,0:T(8,128)(2,1)}, u32[]{:S(2)}, u32[]{:S(2)}) collective-permute-start(bf16[704,512]{1,0:T(8,128)(2,1)} %pad_maximum_fusion.5), channel_id=1, source_target_pairs={{0,8},{8,0},{16,24},{24,16},{1,9},{9,1},{17,25},{25,17},{2,10},{10... | collective-permute-start | bytes 2162696 | tf_op jit(solution)/shard_map/ppermute | solution.py:42
  320.8 46.1 %collective-permute-start.35 = (bf16[2,704,512]{2,1,0:T(8,128)(2,1)}, bf16[2,704,512]{2,1,0:T(8,128)(2,1)}, u32[]{:S(2)}, u32[]{:S(2)}) collective-permute-start(bf16[2,704,512]{2,1,0:T(8,128)(2,1)} %pad_maximum_fusion), channel_id=1, source_target_pairs={{0,16},{8,24},{16,0},{24,8},{1,17},{9,25},{17,1},{25,9},{2,18},{10... | collective-permute-start | bytes 4325384 | tf_op jit(solution)/shard_map/ppermute | solution.py:42
  321.1 46.7 %collective-permute-start.36 = (bf16[2,704,512]{2,1,0:T(8,128)(2,1)}, bf16[2,704,512]{2,1,0:T(8,128)(2,1)}, u32[]{:S(2)}, u32[]{:S(2)}) collective-permute-start(bf16[2,704,512]{2,1,0:T(8,128)(2,1)} %pad_maximum_fusion.1), channel_id=1, source_target_pairs={{0,8},{8,0},{16,24},{24,16},{1,9},{9,1},{17,25},{25,17},{2,10},{10... | collective-permute-start | bytes 4325384 | tf_op jit(solution)/shard_map/ppermute | solution.py:42
  343.2 24.6 %collective-permute-start.33 = (bf16[128,2048]{1,0:T(8,128)(2,1)}, bf16[128,2048]{1,0:T(8,128)(2,1)}, u32[]{:S(2)}, u32[]{:S(2)}) collective-permute-start(bf16[128,2048]{1,0:T(8,128)(2,1)} %get-tuple-element.212), channel_id=1, source_target_pairs={{0,2},{1,3},{8,10},{9,11},{16,18},{17,19},{24,26},{25,27}} | collective-permute-start | bytes 1572872 | tf_op jit(solution)/shard_map/ppermute | solution.py:197
  400.0 27.0 %collective-permute-start.40 = (bf16[128,2048]{1,0:T(8,128)(2,1)S(1)}, bf16[128,2048]{1,0:T(8,128)(2,1)S(1)}, u32[]{:S(2)}, u32[]{:S(2)}) collective-permute-start(bf16[128,2048]{1,0:T(8,128)(2,1)S(1)} %get-tuple-element.292), channel_id=1, source_target_pairs={{4,2},{5,3},{6,4},{7,5},{12,10},{13,11},{14,12},{15,13},{20,18},{2... | collective-permute-start | bytes 1572872 | tf_op jit(solution)/shard_map/ppermute | solution.py:204
  401.3 27.0 %collective-permute-start.39 = (bf16[128,2048]{1,0:T(8,128)(2,1)S(1)}, bf16[128,2048]{1,0:T(8,128)(2,1)S(1)}, u32[]{:S(2)}, u32[]{:S(2)}) collective-permute-start(bf16[128,2048]{1,0:T(8,128)(2,1)S(1)} %get-tuple-element.293), channel_id=1, source_target_pairs={{0,2},{1,3},{2,4},{3,5},{8,10},{9,11},{10,12},{11,13},{16,18},{17,... | collective-permute-start | bytes 1572872 | tf_op jit(solution)/shard_map/ppermute | solution.py:197
  428.3 25.2 %collective-permute-start.56 = (bf16[64,2048]{1,0:T(8,128)(2,1)S(1)}, bf16[64,2048]{1,0:T(8,128)(2,1)S(1)}, u32[]{:S(2)}, u32[]{:S(2)}) collective-permute-start(bf16[64,2048]{1,0:T(8,128)(2,1)S(1)} %pad_maximum_fusion.6), channel_id=1, source_target_pairs={{0,16},{8,24},{16,0},{24,8},{1,17},{9,25},{17,1},{25,9},{2,18},{10... | collective-permute-start | bytes 786440 | tf_op jit(solution)/shard_map/ppermute | solution.py:42
  429.5 27.6 %collective-permute-start.57 = (bf16[64,2048]{1,0:T(8,128)(2,1)S(1)}, bf16[64,2048]{1,0:T(8,128)(2,1)S(1)}, u32[]{:S(2)}, u32[]{:S(2)}) collective-permute-start(bf16[64,2048]{1,0:T(8,128)(2,1)S(1)} %pad_maximum_fusion.7), channel_id=1, source_target_pairs={{0,8},{8,0},{16,24},{24,16},{1,9},{9,1},{17,25},{25,17},{2,10},{10... | collective-permute-start | bytes 786440 | tf_op jit(solution)/shard_map/ppermute | solution.py:42
  453.5 24.6 %collective-permute-start.42 = (bf16[128,2048]{1,0:T(8,128)(2,1)S(1)}, bf16[128,2048]{1,0:T(8,128)(2,1)S(1)}, u32[]{:S(2)}, u32[]{:S(2)}) collective-permute-start(bf16[128,2048]{1,0:T(8,128)(2,1)S(1)} %get-tuple-element.290), channel_id=1, source_target_pairs={{2,0},{3,1},{4,2},{5,3},{6,4},{7,5},{10,8},{11,9},{12,10},{13,11},... | collective-permute-start | bytes 1572872 | tf_op jit(solution)/shard_map/ppermute | solution.py:204
  457.3 19.3 %collective-permute-start.54 = (bf16[1,72,768]{2,1,0:T(8,128)(2,1)S(1)}, bf16[1,72,768]{2,1,0:T(8,128)(2,1)S(1)}, u32[]{:S(2)}, u32[]{:S(2)}) collective-permute-start(bf16[1,72,768]{2,1,0:T(8,128)(2,1)S(1)} %get-tuple-element.305), channel_id=1, source_target_pairs={{0,6},{1,7},{2,0},{3,1},{4,2},{5,3},{6,4},{7,5},{8,14},{9,15},{10,... | collective-permute-start | bytes 331784 | tf_op jit(solution)/shard_map/ppermute | solution.py:150
  458.7 19.3 %collective-permute-start.53 = (bf16[1,72,768]{2,1,0:T(8,128)(2,1)S(1)}, bf16[1,72,768]{2,1,0:T(8,128)(2,1)S(1)}, u32[]{:S(2)}, u32[]{:S(2)}) collective-permute-start(bf16[1,72,768]{2,1,0:T(8,128)(2,1)S(1)} %get-tuple-element.306), channel_id=1, source_target_pairs={{0,5},{1,6},{2,7},{3,0},{4,1},{5,2},{6,3},{7,4},{8,13},{9,14},{10,... | collective-permute-start | bytes 331784 | tf_op jit(solution)/shard_map/ppermute | solution.py:150
  (64 other events, 869.4 us)
Sparse Core Ops, SparseCore 0:
  34.4 49.3 all-gather.7
  85.4 29.3 all-gather.13
  119.3 46.0 all-gather.15
  175.2 49.2 all-gather.9
  245.4 48.3 reduce-scatter.2
  297.4 45.6 all-gather.11
  376.0 60.3 reduce-scatter.4

commit v3 on v2

--- a/solution.py
+++ b/solution.py
@@ -59,6 +59,10 @@
             self.step = (near, far)
         return values if len(values) > 1 else values[0]
 
+    def after(self, *values):
+        if self.step is not None:
+            self.step = tie(*self.step, *values)[:2]
+
     def second(self):
         if self.step is not None:
             self.near, self.far = self.step
@@ -139,23 +143,35 @@
         return values if len(values) > 1 else values[0]
 
 
-def wide_exchange(blocks, between=None):
-    count = lax.axis_size("wide")
-    me = lax.axis_index("wide")
-    whole = jnp.zeros(blocks.shape, blocks.dtype)
-    moved = []
-    for step in range(count):
-        block = lax.dynamic_slice_in_dim(blocks, (me + step) % count, 1, 0)
-        if step:
-            block = lax.ppermute(block, "wide", [(i, (i + step) % count) for i in range(count)])
-        moved.append(block)
-    values = ()
-    if between is not None:
-        half = count // 2
-        moved[half:], values = split_tie(moved[half:], between(moved[:half]))
-    for step, block in enumerate(moved):
-        whole = lax.dynamic_update_slice_in_dim(whole, block, (me - step) % count, 0)
-    return whole, values
+def no_change(value):
+    return jnp.minimum(jnp.abs(value[(0,) * value.ndim].astype(F)), 0.0)
+
+
+class WideExchange:
+    def __init__(self, blocks):
+        self.shape = blocks.shape
+        self.count = lax.axis_size("wide")
+        me = lax.axis_index("wide")
+        self.moved = []
+        for step in range(self.count):
+            block = lax.dynamic_slice_in_dim(blocks, (me + step) % self.count, 1, 0)
+            if step:
+                pairs = [(i, (i + step) % self.count) for i in range(self.count)]
+                block = lax.ppermute(block, "wide", pairs)
+            self.moved.append(block)
+
+    def before(self, *values):
+        half = self.count // 2
+        self.moved[:half], values = split_tie(self.moved[:half], values)
+        return values
+
+    def join(self):
+        me = lax.axis_index("wide")
+        whole = jnp.zeros(self.shape, self.moved[0].dtype)
+        for step, block in enumerate(self.moved):
+            place = (me - step) % self.count
+            whole = lax.dynamic_update_slice_in_dim(whole, block, place, 0)
+        return whole
 
 
 def wide_gather(shard):
@@ -186,69 +202,6 @@
 
 def core_swap(value):
     return lax.ppermute(value, "wide", chip_pairs(lambda chip, core: (chip, 1 - core)))
-
-
-def line_step(right, left, step, spread):
-    chips = lax.axis_size("wide") // 2
-
-    def sends(passed):
-        return step <= passed if spread else passed <= step
-
-    right = lax.ppermute(
-        right,
-        "wide",
-        chip_pairs(
-            lambda chip, core: (chip + 1, core) if chip < chips - 1 and sends(chip) else None
-        ),
-    )
-    left = lax.ppermute(
-        left,
-        "wide",
-        chip_pairs(
-            lambda chip, core: (chip - 1, core) if 0 < chip and sends(chips - 1 - chip) else None
-        ),
-    )
-    return right, left
-
-
-class LineSum:
-    def __init__(self, whole):
-        self.chips = lax.axis_size("wide") // 2
-        at = lax.axis_index("wide")
-        self.chip, core = at // 2, at % 2
-        size = whole.shape[0] // (2 * self.chips)
-        parts = whole.reshape((self.chips, 2, size) + whole.shape[1:])
-        mine = lax.dynamic_index_in_dim(parts, core, 1, False)
-        swapped = core_swap(lax.dynamic_index_in_dim(parts, 1 - core, 1, False))
-        self.parts = plus(mine, swapped)
-        self.flows = None
-        self.step = 0
-
-    def part(self, chip):
-        return lax.dynamic_index_in_dim(self.parts, jnp.clip(chip, 0, self.chips - 1), 0, False)
-
-    def prepare(self):
-        to_right = self.part(self.chips - 1 - self.step + self.chip)
-        to_left = self.part(self.step - (self.chips - 1 - self.chip))
-        if self.flows is not None:
-            to_right = plus(to_right, self.flows[0])
-            to_left = plus(to_left, self.flows[1])
-        self.flows = (to_right, to_left)
-
-    def advance(self):
-        self.flows = line_step(*self.flows, self.step, False)
-        self.step += 1
-
-    def before(self, value):
-        right, left, value = tie(*self.flows, value)
-        self.flows = (right, left)
-        return value
-
-    def result(self):
-        while self.step < self.chips - 1:
-            self.prepare()
-            self.advance()
-        return self.part(self.chip).astype(F) + self.flows[0].astype(F) + self.flows[1].astype(F)
 
 
 def rotated(value, same, ahead, behind):
@@ -538,48 +491,79 @@
     )(q, k, v, seg_col, seg_row)
 
 
-def out_project_body(
-    core_ref, attended_ref, same_ref, other_ref, x_ref, norm_ref, normed_ref, after_ref
-):
-    core = core_ref[0]
-    width = attended_ref.shape[2]
+def out_project_body(pieces, *refs):
+    at_ref, place_ref, attended_ref, x_ref, norm_ref = refs[:5]
+    piece_refs = (refs[5 : 5 + pieces], refs[5 + pieces : 5 + 2 * pieces])
+    normed_ref, after_ref, mine_ref, w_ref = refs[5 + 2 * pieces :]
+    core = at_ref[0]
+    _, chips, width, features = w_ref.shape
+
+    @pl.when(pl.program_id(0) == 0)
+    def _():
+        for same, group in enumerate(piece_refs):
+            for at, piece in enumerate(group):
+                place = place_ref[at]
+                whole = group[0].shape[0]
+                size = width * whole // (chips * width) if pieces == 1 else whole // chips
+                held = piece.shape[0] // size
+                slot = place // whole
+                first = place % whole // size
+                for chip in range(held):
+                    rows = pl.ds(pl.multiple_of(slot * size, size), size)
+                    w_ref[same, first + chip, rows, :] = piece[chip * size : (chip + 1) * size]
+        mine_ref[...] = w_ref[0, at_ref[1]]
+
     total = x_ref[...].astype(F)
-    for chip in range(same_ref.shape[1]):
-        for w_ref, which in ((same_ref, core), (other_ref, 1 - core)):
-            weights = w_ref[:, chip].reshape(width, w_ref.shape[3])
-            total += jnp.dot(attended_ref[chip * 2 + which], weights, preferred_element_type=F)
+    for chip in range(chips):
+        for same, which in enumerate((core, 1 - core)):
+            total += jnp.dot(
+                attended_ref[chip * 2 + which], w_ref[same, chip], preferred_element_type=F
+            )
     after_ref[...] = total
     hat, _ = unit_rows(total)
     normed_ref[...] = (hat * norm_ref[0:1, :] + norm_ref[1:2, :]).astype(B)
 
 
-def out_project(core, attended_all, out_same, out_other, x_all, norm_two):
+def out_project(at, attended_all, same, other, places, x_all, norm_two):
     owners, tokens, width = attended_all.shape
     features = x_all.shape[1]
     block = min(TOKEN_BLOCK, tokens)
-    weights = pl.BlockSpec(out_same.shape, lambda i, core: (0, 0, 0, 0))
-    rows = pl.BlockSpec((block, features), lambda i, core: (i, 0))
+    flat = lambda array: pl.BlockSpec(array.shape, lambda i, at, place: (0, 0))
+    rows = pl.BlockSpec((block, features), lambda i, at, place: (i, 0))
     return pl.pallas_call(
-        out_project_body,
+        functools.partial(out_project_body, len(same)),
         grid_spec=pltpu.PrefetchScalarGridSpec(
-            num_scalar_prefetch=1,
+            num_scalar_prefetch=2,
             grid=(tokens // block,),
             in_specs=[
-                pl.BlockSpec((owners, block, width), lambda i, core: (0, i, 0)),
-                weights,
-                weights,
+                pl.BlockSpec((owners, block, width), lambda i, at, place: (0, i, 0)),
                 rows,
-                pl.BlockSpec(norm_two.shape, lambda i, core: (0, 0)),
+                flat(norm_two),
+            ]
+            + [flat(piece) for piece in same + other],
+            out_specs=[
+                rows,
+                rows,
+                pl.BlockSpec((width, features), lambda i, at, place: (0, 0)),
             ],
-            out_specs=[rows, rows],
+            scratch_shapes=[pltpu.VMEM((2, owners // 2, width, features), B)],
         ),
         out_shape=[
             jax.ShapeDtypeStruct((tokens, features), B),
             jax.ShapeDtypeStruct((tokens, features), F),
+            jax.ShapeDtypeStruct((width, features), B),
         ],
         name="out_project",
         cost_estimate=cost(tokens * features * features, 8 * tokens * features),
-    )(core, attended_all, out_same, out_other, x_all, norm_two)
+    )(
+        jnp.stack(at).astype(jnp.int32),
+        jnp.stack(places).astype(jnp.int32),
+        attended_all,
+        x_all,
+        norm_two,
+        *same,
+        *other,
+    )
 
 
 def attend_back_body(
@@ -672,7 +656,7 @@
 def weights_back(hat_all, grad_proj, w_mine, norms, two, bias_grad, depth, norm_size):
     tokens, features = hat_all.shape
     columns = grad_proj.shape[1]
-    block = min(256, features)
+    block = min(512, features)
     flat = lambda array: pl.BlockSpec(array.shape, lambda i: (0, 0))
     across = lambda rows: pl.BlockSpec((rows, block), lambda i: (0, i))
     return pl.pallas_call(
@@ -824,23 +808,30 @@
     core = my_wide % 2
     blocks = range(rows * wide)
     back = [(b % rows * wide + b // rows, b) for b in blocks]
-    received, _ = wide_exchange(
+    gate_first = gate_up.swapaxes(1, 2)
+    gate = RowsGather(gate_first[0], 1)
+    exchange = WideExchange(
         pack(my_row * wide + my_wide, w_qkv, norm_params, b_qkv, strided, wide)
     )
-    received, x_first, segment_row = tie(received, x_own, segment_row)
+    segment_row, *arrived = exchange.before(segment_row, *(gate.step or ()))
+    gate.step = arrived or None
+    received, x_first = tie(exchange.join(), x_own)
     x_all = wide_gather(x_first)
     w_rows = RowsGather(received, 0)
     seg_col = segment_row[:, None]
     seg_line = segment_row[None, :]
     tables = w_rows.before(*rotary_tables(seg_col, seg_line))
     w_rows.second()
-    gate_first = w_rows.before(gate_up.swapaxes(1, 2))
-    gate = RowsGather(gate_first[0], 1)
+    if gate.step:
+        up_first, *gate.step = w_rows.before(gate_first[1], *gate.step)
+    else:
+        up_first = gate_first[1]
+    up = RowsGather(up_first, 1)
+    gate.second()
     if strided:
         x_all, out_first = w_rows.before(x_all, w_out)
         out_line = lax.all_gather(out_first, "wide", axis=0, tiled=False)
     q, k, v, hat_all, w_mine, norms, _ = project(x_all, w_rows, tables, depth, norm_size)
-    up = RowsGather(gate_first[1], 1)
     attended, lse = attend(q, k, v, seg_col, seg_line, heads)
     attended = gate.before(up.before(attended))
     if strided:
@@ -851,33 +842,27 @@
         out_line = lax.dynamic_index_in_dim(out_line, core, 1, False)
         out_rows = RowsGather(out_line.reshape(chips * depth, features), 0)
         out_rows.second()
-        out_rows.step = gate.before(*out_rows.step)
-        out_rows.step = up.before(*out_rows.step)
-        out_same = out_rows.join()
-        out_other = core_swap(out_same)
-        shape = (rows, chips, depth, features)
+        out_rows.step = up.before(*out_rows.step) if out_rows.step else None
+        out_pieces, out_places = out_rows.pieces()
     else:
-        shape = (1, chips, width, features)
         out_all = lax.all_gather(w_out, ("rows", "wide"), axis=0, tiled=True)
         out_all = out_all.reshape(chips, 2, width, features)
-        out_same = lax.dynamic_index_in_dim(out_all, core, 1, False)
-        out_other = lax.dynamic_index_in_dim(out_all, 1 - core, 1, False)
-    out_same, out_other = out_same.reshape(shape), out_other.reshape(shape)
-    out_mine = lax.dynamic_index_in_dim(out_same, my_wide // 2, 1, False).reshape(width, features)
-    gate.second()
+        out_line = lax.dynamic_index_in_dim(out_all, core, 1, False)
+        out_pieces, out_places = [out_line.reshape(chips * width, features)], [jnp.int32(0)]
+    swapped = [core_swap(piece) for piece in out_pieces]
     up.second()
-    attended_all, out_same, upstream, down_first = up.before(
-        *gate.before(attended_all, out_same, out_grad[0], w_down)
-    )
+    attended_all, upstream, down_first, *swapped = tie(
+        attended_all, out_grad[0], w_down, *swapped
+    )
+    down = RowsGather(down_first, 1)
     grads_all = wide_gather(upstream)
-    down = RowsGather(down_first, 1)
-    tokens_all, after_all = out_project(
-        core[None].astype(jnp.int32), attended_all, out_same, out_other, x_all, norms[2:]
+    tokens_all, after_all, out_mine = out_project(
+        (core, my_wide // 2), attended_all, out_pieces, swapped, out_places, x_all, norms[2:]
     )
     tokens_all = down.before(tokens_all)
+    down.second()
     after_attn = lax.dynamic_slice_in_dim(after_all, my_wide * local_len, local_len, 0)
     gate_part, up_part, hidden = gate_up_forward(tokens_all, gate, up)
-    down.second()
 
     gate_grads, e_two = feed_back(grads_all, gate_part, up_part, down, gate, up)
     grad_normed_two = wide_scatter(e_two)
@@ -888,62 +873,46 @@
     grad_gate = RowsSum(gate_grad, 2)
     grad_normed_two = grad_gate.before(grad_down.before(grad_normed_two))
     hidden, *_ = tie(hidden, *grad_down.second(), *grad_gate.second())
-    mlp_sum = LineSum(down_forward(hidden, down, features))
-    mlp_sum.prepare()
+    mlp_part = down_forward(hidden, down, features)
 
     grad_after, branch, sums_two = norm_back(
         grad_normed_two, after_attn, out_grad[0], norms[2:3], True
     )
     branch_all = wide_gather(branch)
-    branch_all = mlp_sum.before(branch_all)
-    mlp_sum.advance()
+    mlp_part, branch_all = grad_gate.after(mlp_part, branch_all)
+    mlp_out = wide_scatter(mlp_part)
     grad_attended = dotg(branch_all, out_mine, NT).astype(B)
     grad_proj, bias_grad = attend_back(
         q, k, v, grad_attended, lse, seg_col, seg_line, tables, heads
     )
-    grad_proj = grad_gate.after(grad_down.after(grad_proj))
-    grad_proj = mlp_sum.before(grad_proj)
-    mlp_sum.prepare()
-    mlp_sum.advance()
+    grad_proj = grad_down.after(grad_proj)
     e_one = dotg(grad_proj, w_mine, NT).astype(B)
-    e_one, grad_proj = tie(e_one, grad_proj)
+    e_one, grad_proj, branch_all = tie(e_one, grad_proj, branch_all)
     grad_normed_one = wide_scatter(e_one)
+    grad_out = RowsSum(dotg(attended, branch_all, TN).astype(B), 0)
     packed = weights_back(
         hat_all, grad_proj, w_mine, norms, sums_two, bias_grad, depth, norm_size
     )
     qkv_sum = RowsSum(packed, 0)
-    branch_all = qkv_sum.before(branch_all)
-    sent = qkv_sum.second()
-    branch_all, *_ = tie(branch_all, *sent)
-    grad_out = RowsSum(dotg(attended, branch_all, TN).astype(B), 0)
-    qkv_sum.after(*grad_out.arrived_or_whole())
+    qkv_sum.whole = grad_out.before(qkv_sum.whole)
     grad_out.second()
-    mlp_sum.before(qkv_sum.whole)
-    mlp_sum.prepare()
-    mlp_sum.advance()
-
-    def late(first):
-        outs = []
-        for total in (grad_out, grad_gate, grad_down):
-            first = total.after(*first)
-            outs.append(total.result())
-        if not strided:
-            outs[0] = lax.ppermute(outs[0].astype(B), ("rows", "wide"), back).astype(F)
-        grads = (outs[0], outs[1].swapaxes(1, 2), outs[2])
-        steps = [
-            adam_step(*parts)
-            for parts in zip((w_out, gate_up, w_down), grads, (moment_out, moment_gate, moment_down))
-        ]
-        return grads + tuple(steps)
-
-    received, late_values = wide_exchange(qkv_sum.result().astype(B), late)
-    grad_out, grad_gate, grad_down, step_out, step_gate, step_down = late_values
+    start = no_change(qkv_sum.second()[0])
+    mlp_out = qkv_sum.after(mlp_out)
+    exchange = WideExchange(qkv_sum.result().astype(B))
+    grad_out = grad_out.result() + start
+    if not strided:
+        grad_out = lax.ppermute(grad_out.astype(B), ("rows", "wide"), back).astype(F)
+    grad_down = grad_down.result() + start
+    grad_gate = (grad_gate.result() + start).swapaxes(1, 2)
+    step_out = adam_step(w_out, grad_out, moment_out)
+    step_gate = adam_step(gate_up, grad_gate, moment_gate)
+    step_down = adam_step(w_down, grad_down, moment_down)
+    received = exchange.join()
+
+    block_out = (after_attn + mlp_out.astype(F)).astype(B)
+    grad_qkv, step_qkv = finish(received, w_qkv, moment_qkv, strided)
+    grad_qkv, step_qkv, grad_normed_one = tie(grad_qkv, step_qkv, grad_normed_one)
     input_grad = norm_back(grad_normed_one, x_own, grad_after, norms[0:1], False)[0]
-
-    received = mlp_sum.before(received)
-    block_out = (after_attn + mlp_sum.result()).astype(B)
-    received, input_grad = tie(received, input_grad)
-    grad_qkv, step_qkv = finish(received, w_qkv, moment_qkv, strided)
     extra = received[:, depth : depth + 5].astype(F)
     grad_norms = jnp.sum(extra[:, :4, :norm_size], axis=0)
     bias_all = extra[:, 4].reshape(wide, 3, heads, HEAD_DIM)

time: 515 us -> 477 us (0.926)
  waiting for transfers between devices: 200 us -> 175 us
  starting transfers between devices: 69.1 us -> 55.1 us
    all_gather x3, waiting for transfers between devices: 41.7 us -> 15.4 us  [wide_gather(): return lax.all_gather(shard, 'wide', axis=0, tiled=True)]
    ppermute x20 -> x14, waiting for transfers between devices: 48.6 us -> 33.5 us  [__init__(): block = lax.ppermute(block, 'wide', pairs)]
    ppermute x20 -> x14, starting transfers between devices: 33.7 us -> 19.1 us  [__init__(): block = lax.ppermute(block, 'wide', pairs)]
    ppermute x36, waiting for transfers between devices: 96 us -> 108 us  [rows_swap(): return lax.ppermute(value, 'rows', [(i, i ^ bits) for i in range(4)])]
    unnamed x62 -> x102, local copies, waits for them, and re-layouts: 5.26 us -> 13.1 us
    reduce_scatter x2 -> x3, waiting for transfers between devices: 8.93 us -> 10.7 us  [wide_scatter(): return lax.psum_scatter(whole, 'wide', scatter_dimension=0, tiled=True)]
  transfers between devices with their start and end apart: 65 -> 63, of which waited for: 33 -> 32; matrix products, arithmetic and copies ran while one was open for 16% -> 18% of each run, Pallas kernels for 18% -> 21%
where the time goes in v3:
time: 477 us; the launch traced here: 471 us
  waiting for transfers between devices  175 us (37%)
  Pallas kernels  125 us (26%)
  starting transfers between devices  55.1 us (12%)
  local copies, waits for them, and re-layouts  41.6 us (9%)
  other arithmetic  31 us (6%)
  matrix products  26.3 us (6%)
  between operations  15.9 us (3%)
    ppermute x36, waiting for transfers between devices, rows_swap(): return lax.ppermute(value, 'rows', [(i, i ^ bits) for i in range(4)])  108 us
    pallas_call x3, Pallas kernels, piece_call(): pl.pallas_call(functools.partial(body, len(places)), grid_spec=pltpu.Pref...  41 us
    ppermute x14, waiting for transfers between devices, __init__(): block = lax.ppermute(block, 'wide', pairs)  33.5 us
    ppermute x36, starting transfers between devices, rows_swap(): return lax.ppermute(value, 'rows', [(i, i ^ bits) for i in range(4)])  30.3 us
    ppermute x14, starting transfers between devices, __init__(): block = lax.ppermute(block, 'wide', pairs)  19.1 us
    pallas_call x1, Pallas kernels, out_project(): pl.pallas_call(functools.partial(out_project_body, len(same)), grid_spec=...  18.9 us
    pallas_call x1, Pallas kernels, attend_back(): pl.pallas_call(functools.partial(attend_back_body, heads), out_shape=[jax...  15.5 us
    all_gather x3, waiting for transfers between devices, wide_gather(): return lax.all_gather(shard, 'wide', axis=0, tiled=True)  15.4 us
  transfers between devices with their start and end apart: 63, of which 32 were waited for; matrix products, arithmetic and copies ran while one was open for 18% of the time, Pallas kernels for 21%

profile of v3, /device:TPU:9, one launch (start us, length us, event | category | flops | bytes accessed | tf_op | source)
XLA Modules:
  0.0 470.6 jit_solution(12448735252285732221)
XLA Ops:
  25.6 7.4 %collective-permute-done.2 = bf16[1,72,768]{2,1,0:T(8,128)(2,1)} collective-permute-done((bf16[1,72,768]{2,1,0:T(8,128)(2,1)S(1)}, bf16[1,72,768]{2,1,0:T(8,128)(2,1)}, u32[]{:S(2)}, u32[]{:S(2)}) %collective-permute-start.2) | collective-permute-done | bytes 110624 | tf_op jit(solution)/shard_map/ppermute | solution.py:160
  41.2 5.4 %tables.1 = (f32[1024,128]{1,0:T(8,128)}, f32[1024,128]{1,0:T(8,128)}, f32[1024,128]{1,0:T(8,128)}) custom-call(s32[1024,1]{1,0:T(8,128)} %copy.30.col_ref.seg_col, s32[1,1024]{1,0:T(1,128)} %param.18), custom_call_target="tpu_custom_call" | custom-call | tf_op jit(solution)/shard_map/tables/pallas_call | solution.py:247
  46.5 14.4 %collective-permute-done.10.refs_7_ = bf16[8,72,768]{2,1,0:T(8,128)(2,1)S(1)} collective-permute-done((bf16[8,72,768]{2,1,0:T(8,128)(2,1)S(1)}, bf16[8,72,768]{2,1,0:T(8,128)(2,1)S(1)}, u32[]{:S(2)}, u32[]{:S(2)}) %collective-permute-start.10) | collective-permute-done | bytes 884768 | tf_op jit(solution)/shard_map/ppermute | solution.py:42
  65.1 10.4 %collective-permute-done.11.refs_8_ = bf16[4,72,768]{2,1,0:T(8,128)(2,1)S(1)} collective-permute-done((bf16[4,72,768]{2,1,0:T(8,128)(2,1)S(1)}, bf16[4,72,768]{2,1,0:T(8,128)(2,1)S(1)}, u32[]{:S(2)}, u32[]{:S(2)}) %collective-permute-start.11) | collective-permute-done | bytes 442400 | tf_op jit(solution)/shard_map/ppermute | solution.py:42
  77.2 9.1 %all-gather.8.cloned.1.call-done.refs_1_.refs_3_ = bf16[1024,2048]{1,0:T(8,128)(2,1)} async-done(((bf16[128,2048]{1,0:T(8,128)(2,1)}), bf16[1024,2048]{1,0:T(8,128)(2,1)}) %all-gather.8.cloned.1.call-update) | async-done | bytes 4194320 | tf_op jit(solution)/shard_map/all_gather | solution.py:178
  92.3 12.7 %project.1 = (bf16[1024,256]{1,0:T(8,128)(2,1)}, bf16[1024,256]{1,0:T(8,128)(2,1)}, bf16[1024,256]{1,0:T(8,128)(2,1)}, bf16[1024,2048]{1,0:T(8,128)(2,1)}, bf16[...) custom-call(s32[5]{0:T(128)} %stack.89.refs_0_, ...), custom_call_target="tpu_custom_call" | custom-call | flops 3221225472 | bytes 8388608 | tf_op jit(solution)/shard_map/project/pallas_call | solution.py:309
  105.0 8.2 %attend.1 = (bf16[1024,256]{1,0:T(8,128)(2,1)}, f32[1024,128]{1,0:T(8,128)}) custom-call(bf16[1024,256]{1,0:T(8,128)(2,1)} %get-tuple-element.141.q_ref, bf16[1024,256]{1,0:T(8,128)(2,1)} %get-tuple-element.142.k_ref, bf16[1024,256]{1,0:T(8,128)(2,1)} %get-tuple-element.143.v_ref, s32[1024,1]{1,0:T(8,128)} %copy.30.col_ref.seg_col, s32[1,1024]{1,0:T(1,128)} %param.18), custom_call_target="tpu_custom_call" | custom-call | flops 4294967296 | bytes 2097152 | tf_op jit(solution)/shard_map/attend/pallas_call | solution.py:483
  113.2 4.1 all-gather.14.cloned.1.call-done
  121.2 22.1 %collective-permute-done.18.refs_6_ = bf16[256,2048]{1,0:T(8,128)(2,1)S(1)} collective-permute-done((bf16[256,2048]{1,0:T(8,128)(2,1)S(1)}, bf16[256,2048]{1,0:T(8,128)(2,1)S(1)}, u32[]{:S(2)}, u32[]{:S(2)}) %collective-permute-start.18) | collective-permute-done | bytes 1048608 | tf_op jit(solution)/shard_map/ppermute | solution.py:42
  148.1 7.8 %collective-permute-done.22.refs_8_ = bf16[128,2048]{1,0:T(8,128)(2,1)S(1)} collective-permute-done((bf16[128,2048]{1,0:T(8,128)(2,1)S(1)}, bf16[128,2048]{1,0:T(8,128)(2,1)S(1)}, u32[]{:S(2)}, u32[]{:S(2)}) %collective-permute-start.22) | collective-permute-done | bytes 524320 | tf_op jit(solution)/shard_map/ppermute | solution.py:42
  172.7 18.9 %out_project.1 = (bf16[1024,2048]{1,0:T(8,128)(2,1)}, f32[1024,2048]{1,0:T(8,128)}, bf16[256,2048]{1,0:T(8,128)(2,1)}) custom-call(s32[2]{0:T(128)} %pad_add_fusion.refs_0_, s32[5]{0:T(128)} %stack.83.refs_1_, bf16[8,1024,256]{2,1,0:T(8,128)(2,1)} %bitcast.111, bf16[1024,2048]{1,0:T(8,128)(2,1)} %all-gather.8.cloned.1.call-done.refs_1_.refs_3_, ...), custom_call_target="tpu_custom_call" | custom-call | flops 8589934592 | bytes 16777216 | tf_op jit(solution)/shard_map/out_project/pallas_call | solution.py:533
  191.6 4.3 collective-permute-done.26.refs_5_.refs_3_
  199.5 12.4 %gate_up.1 = (f32[1024,704]{1,0:T(8,128)}, f32[1024,704]{1,0:T(8,128)}, bf16[1024,704]{1,0:T(8,128)(2,1)}) custom-call(s32[5]{0:T(128)} %stack.95.refs_0_, bf16[1024,2048]{1,0:T(8,128)(2,1)} %get-tuple-element.182.refs_1_, bf16[704,512]{1,0:T(8,128)(2,1)} %copy-done.19, bf16[704,512]{1,0:T(8,128)(2,1)} %copy-done.26, bf16[704,512]{1,0:T(8,128)(2,1)} %copy-done.27, ...), custom_call_target="tpu_custom_call" | custom-call | flops 5905580032 | bytes 9961472 | tf_op jit(solution)/shard_map/gate_up/pallas_call | solution.py:359
  212.8 20.7 %feed_back.1 = (bf16[2,1024,704]{2,1,0:T(8,128)(2,1)}, bf16[1024,2048]{1,0:T(8,128)(2,1)}) custom-call(s32[5]{0:T(128)} %stack.95.refs_0_, bf16[1024,2048]{1,0:T(8,128)(2,1)} %all-gather.10.cloned.1.call-done.refs_1_, f32[1024,704]{1,0:T(8,128)} %get-tuple-element.170.refs_2_, f32[1024,704]{1,0:T(8,128)} %get-tuple-element.171.refs_3_, ...), custom_call_target="tpu_custom_call" | custom-call | flops 8858370048 | bytes 18612224 | tf_op jit(solution)/shard_map/feed_back/pallas_call | solution.py:359
  235.4 8.6 %convolution_convert_fusion = bf16[2,704,2048]{2,1,0:T(8,128)(2,1)S(1)} fusion(bf16[2,1024,704]{2,1,0:T(8,128)(2,1)S(1)} %copy-done.48, bf16[1024,2048]{1,0:T(8,128)(2,1)} %get-tuple-element.182.refs_1_), kind=kOutput, calls=%fused_computation | convolution fusion | flops 5908463616 | bytes 12845056 | tf_op jit(solution)/shard_map/gtf,td->gfd/dot_general | solution.py:870
  258.7 13.4 %collective-permute-done.32 = bf16[352,512]{1,0:T(8,128)(2,1)} collective-permute-done((bf16[352,512]{1,0:T(8,128)(2,1)S(1)}, bf16[352,512]{1,0:T(8,128)(2,1)}, u32[]{:S(2)}, u32[]{:S(2)}) %collective-permute-start.32) | collective-permute-done | bytes 360480 | tf_op jit(solution)/shard_map/ppermute | solution.py:42
  272.1 10.7 %reduce-scatter.4.cloned.1.call-done.e_ref = bf16[128,2048]{1,0:T(8,128)(2,1)} async-done(((bf16[1024,2048]{1,0:T(8,128)(2,1)}), bf16[128,2048]{1,0:T(8,128)(2,1)}) %reduce-scatter.4.cloned.1.call-update) | async-done | bytes 524304 | tf_op jit(solution)/shard_map/reduce_scatter | solution.py:182
  282.8 3.6 norm_back.2
  296.8 7.9 %down.1 = bf16[1024,2048]{1,0:T(8,128)(2,1)} custom-call(s32[5]{0:T(128)} %stack.95.refs_0_, bf16[1024,704]{1,0:T(8,128)(2,1)} %get-tuple-element.186.refs_1_, bf16[704,512]{1,0:T(8,128)(2,1)} %refs_2_, bf16[704,512]{1,0:T(8,128)(2,1)} %collective-permute-done.26.refs_5_.refs_3_, bf16[704,512]{1,0:T(8,128)(2,1)} %collective-permute-done.27.refs_6_.refs_4_, ...), custom_call_target="tpu_custom_call" | custom-call | flops 2952790016 | bytes 4325376 | tf_op jit(solution)/shard_map/down/pallas_call | solution.py:359
  304.7 18.1 %collective-permute-done.39 = bf16[2,704,512]{2,1,0:T(8,128)(2,1)} collective-permute-done((bf16[2,704,512]{2,1,0:T(8,128)(2,1)}, bf16[2,704,512]{2,1,0:T(8,128)(2,1)}, u32[]{:S(2)}, u32[]{:S(2)}) %collective-permute-start.39) | collective-permute-done | bytes 1441824 | tf_op jit(solution)/shard_map/ppermute | solution.py:42
  326.0 6.3 %all-gather.12.cloned.1.call-done = bf16[1024,2048]{1,0:T(8,128)(2,1)} async-done(((bf16[128,2048]{1,0:T(8,128)(2,1)}), bf16[1024,2048]{1,0:T(8,128)(2,1)}) %all-gather.12.cloned.1.call-update) | async-done | bytes 4194320 | tf_op jit(solution)/shard_map/all_gather | solution.py:178
  334.9 4.3 convolution_convert_fusion.4.g_ref
  339.2 15.5 %attend_back.1 = (bf16[1024,768]{1,0:T(8,128)(2,1)}, f32[1,768]{1,0:T(1,128)}) custom-call(bf16[1024,256]{1,0:T(8,128)(2,1)} %get-tuple-element.141.q_ref, bf16[1024,256]{1,0:T(8,128)(2,1)} %get-tuple-element.142.k_ref, bf16[1024,256]{1,0:T(8,128)(2,1)} %get-tuple-element.143.v_ref, bf16[1024,256]{1,0:T(8,128)(2,1)} %convolution_convert_fusion.4.g_ref, ...), custom_call_target="tpu_custom_call" | custom-call | flops 8589934592 | bytes 4194304 | tf_op jit(solution)/shard_map/attend_back/pallas_call | solution.py:616
  354.7 6.5 %convolution_convert_fusion.1 = bf16[1024,2048]{1,0:T(8,128)(2,1)} fusion(bf16[1024,768]{1,0:T(8,128)(2,1)} %get-tuple-element.197.grad_ref, bf16[2048,768]{1,0:T(8,128)(2,1)S(1)} %copy-done.4), kind=kOutput, calls=%fused_computation.3 | convolution fusion | flops 3223322624 | bytes 8912896 | tf_op jit(solution)/shard_map/dot_general | solution.py:34
  367.8 9.3 %weights_back.1 = bf16[32,72,768]{2,1,0:T(8,128)(2,1)} custom-call(bf16[1024,2048]{1,0:T(8,128)(2,1)} %get-tuple-element.196.hat_ref, bf16[1024,768]{1,0:T(8,128)(2,1)} %get-tuple-element.197.grad_ref, bf16[2048,768]{1,0:T(8,128)(2,1)} %get-tuple-element.194.w_ref, f32[4,2048]{1,0:T(4,128)} %get-tuple-element.155.norms_ref, ...), custom_call_target="tpu_custom_call" | custom-call | flops 3221225472 | bytes 8388608 | tf_op jit(solution)/shard_map/weights_back/pallas_call | solution.py:662
  384.6 4.1 collective-permute-done.42
  398.0 4.6 fusion.13
  402.6 5.8 %fusion.6 = (f32[2,512,704]{1,2,0:T(8,128)}, f32[2,512,704]{1,2,0:T(8,128)}) fusion(bf16[2,512,704]{1,2,0:T(8,128)(2,1)S(1)} %copy-done.2, f32[2,2,512,704]{2,3,1,0:T(8,128)S(1)} %bitcast.95, f32[]{:T(128)} %bitcast.34, bf16[2,704,512]{2,1,0:T(8,128)(2,1)} %collective-permute-done.39, bf16[2,704,512]{2,1,0:T(8,128)(2,1)} %collective-permute-done.38, ...), kind=kLoop, calls=%fused_computation.10 | loop fusion | flops 14417920 | bytes 17301512 | tf_op jit(solution)/shard_map/add | solution.py:753
  408.4 4.0 collective-permute-done.45
  416.3 4.0 collective-permute-start.46
  431.4 14.7 %collective-permute-done.48 = bf16[1,72,768]{2,1,0:T(8,128)(2,1)S(1)} collective-permute-done((bf16[1,72,768]{2,1,0:T(8,128)(2,1)S(1)}, bf16[1,72,768]{2,1,0:T(8,128)(2,1)S(1)}, u32[]{:S(2)}, u32[]{:S(2)}) %collective-permute-start.48) | collective-permute-done | bytes 110624 | tf_op jit(solution)/shard_map/ppermute | solution.py:160
  452.5 5.3 %finish.1 = (f32[64,6144]{1,0:T(8,128)}, f32[64,6144]{1,0:T(8,128)}) custom-call(bf16[8,72,768]{2,1,0:T(8,128)(2,1)} %copy-done.3, bf16[64,6144]{1,0:T(8,128)(2,1)} %w_ref.3, f32[2,64,6144]{2,1,0:T(8,128)} %moment_ref.1), custom_call_target="tpu_custom_call" | custom-call | tf_op jit(solution)/shard_map/finish/pallas_call | solution.py:782
  (295 shorter events, 150.3 us)
Async XLA Ops:
  7.2 79.1 %all-gather.8.cloned.1.call-start = ((), (), s32[]{:S(2)}) async-start(), calls=%async_computation.3 | async-start | bytes 4718592 | tf_op jit(solution)/shard_map/all_gather | solution.py:178
  8.7 24.3 %collective-permute-start.3 = (bf16[704,512]{1,0:T(8,128)(2,1)S(1)}, bf16[704,512]{1,0:T(8,128)(2,1)S(1)}, u32[]{:S(2)}, u32[]{:S(2)}) collective-permute-start(bf16[704,512]{1,0:T(8,128)(2,1)S(1)} %get-tuple-element.245.refs_2_.refs_9_), channel_id=1, source_target_pairs={{0,8},{8,0},{16,24},{24,16},{1,9},{9,1},{17,25},{25,17},{2,10},{10... | collective-permute-start | bytes 2162696 | tf_op jit(solution)/shard_map/ppermute | solution.py:42
  10.0 24.7 %collective-permute-start.4 = (bf16[704,512]{1,0:T(8,128)(2,1)S(1)}, bf16[704,512]{1,0:T(8,128)(2,1)S(1)}, u32[]{:S(2)}, u32[]{:S(2)}) collective-permute-start(bf16[704,512]{1,0:T(8,128)(2,1)S(1)} %get-tuple-element.245.refs_2_.refs_9_), channel_id=1, source_target_pairs={{0,16},{8,24},{16,0},{24,8},{1,17},{9,25},{17,1},{25,9},{2,18},{10... | collective-permute-start | bytes 2162696 | tf_op jit(solution)/shard_map/ppermute | solution.py:42
  39.7 77.6 %all-gather.14.cloned.1.call-start = ((), (), s32[]{:S(2)}) async-start(), calls=%async_computation.9 | async-start | bytes 2359296 | tf_op jit(solution)/shard_map/all_gather | solution.py:833
  39.7 21.2 %collective-permute-start.10 = (bf16[8,72,768]{2,1,0:T(8,128)(2,1)S(1)}, bf16[8,72,768]{2,1,0:T(8,128)(2,1)S(1)}, u32[]{:S(2)}, u32[]{:S(2)}) collective-permute-start(bf16[8,72,768]{2,1,0:T(8,128)(2,1)S(1)} %constant_dynamic-update-slice_fusion.7.refs_5_), channel_id=1, source_target_pairs={{0,16},{8,24},{16,0},{24,8},{1,17},{9,25},{17,1},{25,9},{2,18},{10... | collective-permute-start | bytes 2654216 | tf_op jit(solution)/shard_map/ppermute | solution.py:42
  40.0 21.4 %collective-permute-start.9 = (bf16[8,72,768]{2,1,0:T(8,128)(2,1)S(1)}, bf16[8,72,768]{2,1,0:T(8,128)(2,1)S(1)}, u32[]{:S(2)}, u32[]{:S(2)}) collective-permute-start(bf16[8,72,768]{2,1,0:T(8,128)(2,1)S(1)} %constant_dynamic-update-slice_fusion.7.refs_5_), channel_id=1, source_target_pairs={{0,8},{8,0},{16,24},{24,16},{1,9},{9,1},{17,25},{25,17},{2,10},{10... | collective-permute-start | bytes 2654216 | tf_op jit(solution)/shard_map/ppermute | solution.py:42
  86.3 77.7 %all-gather.16.cloned.1.call-start = ((), (), s32[]{:S(2)}) async-start(), calls=%async_computation.10 | async-start | bytes 4718592 | tf_op jit(solution)/shard_map/all_gather | solution.py:839
  86.5 26.6 %collective-permute-start.15 = (bf16[704,512]{1,0:T(8,128)(2,1)S(1)}, bf16[704,512]{1,0:T(8,128)(2,1)}, u32[]{:S(2)}, u32[]{:S(2)}) collective-permute-start(bf16[704,512]{1,0:T(8,128)(2,1)S(1)} %get-tuple-element.131.refs_7_.refs_14_), channel_id=1, source_target_pairs={{0,8},{8,0},{16,24},{24,16},{1,9},{9,1},{17,25},{25,17},{2,10},{10... | collective-permute-start | bytes 2162696 | tf_op jit(solution)/shard_map/ppermute | solution.py:42
  87.8 25.4 %collective-permute-start.16 = (bf16[704,512]{1,0:T(8,128)(2,1)S(1)}, bf16[704,512]{1,0:T(8,128)(2,1)}, u32[]{:S(2)}, u32[]{:S(2)}) collective-permute-start(bf16[704,512]{1,0:T(8,128)(2,1)S(1)} %get-tuple-element.131.refs_7_.refs_14_), channel_id=1, source_target_pairs={{0,16},{8,24},{16,0},{24,8},{1,17},{9,25},{17,1},{25,9},{2,18},{10... | collective-permute-start | bytes 2162696 | tf_op jit(solution)/shard_map/ppermute | solution.py:42
  90.6 22.6 %collective-permute-start.13 = (bf16[704,256]{1,0:T(8,128)(2,1)S(1)}, bf16[704,256]{1,0:T(8,128)(2,1)}, u32[]{:S(2)}, u32[]{:S(2)}) collective-permute-start(bf16[704,256]{1,0:T(8,128)(2,1)S(1)} %slice.163), channel_id=1, source_target_pairs={{0,16},{8,24},{16,0},{24,8},{1,17},{9,25},{17,1},{25,9},{2,18},{10... | collective-permute-start | bytes 1081352 | tf_op jit(solution)/shard_map/ppermute | solution.py:42
  91.9 21.2 %collective-permute-start.14 = (bf16[704,256]{1,0:T(8,128)(2,1)S(1)}, bf16[704,256]{1,0:T(8,128)(2,1)}, u32[]{:S(2)}, u32[]{:S(2)}) collective-permute-start(bf16[704,256]{1,0:T(8,128)(2,1)S(1)} %slice.164), channel_id=1, source_target_pairs={{0,8},{8,0},{16,24},{24,16},{1,9},{9,1},{17,25},{25,17},{2,10},{10... | collective-permute-start | bytes 1081352 | tf_op jit(solution)/shard_map/ppermute | solution.py:42
  117.3 94.7 %all-gather.10.cloned.1.call-start = ((), (), s32[]{:S(2)}) async-start(), calls=%async_computation.4 | async-start | bytes 4718592 | tf_op jit(solution)/shard_map/all_gather | solution.py:178
  118.7 24.6 %collective-permute-start.18 = (bf16[256,2048]{1,0:T(8,128)(2,1)S(1)}, bf16[256,2048]{1,0:T(8,128)(2,1)S(1)}, u32[]{:S(2)}, u32[]{:S(2)}) collective-permute-start(bf16[256,2048]{1,0:T(8,128)(2,1)S(1)} %bitcast.102), channel_id=1, source_target_pairs={{0,8},{8,0},{16,24},{24,16},{1,9},{9,1},{17,25},{25,17},{2,10},{10... | collective-permute-start | bytes 3145736 | tf_op jit(solution)/shard_map/ppermute | solution.py:42
  120.0 24.6 %collective-permute-start.20 = (bf16[256,2048]{1,0:T(8,128)(2,1)S(1)}, bf16[256,2048]{1,0:T(8,128)(2,1)S(1)}, u32[]{:S(2)}, u32[]{:S(2)}) collective-permute-start(bf16[256,2048]{1,0:T(8,128)(2,1)S(1)} %bitcast.103), channel_id=1, source_target_pairs={{0,16},{8,24},{16,0},{24,8},{1,17},{9,25},{17,1},{25,9},{2,18},{10... | collective-permute-start | bytes 3145736 | tf_op jit(solution)/shard_map/ppermute | solution.py:42
  164.0 118.8 %reduce-scatter.4.cloned.1.call-start = ((), (), s32[]{:S(2)}) async-start(), calls=%async_computation.5 | async-start | bytes 4718592 | tf_op jit(solution)/shard_map/reduce_scatter | solution.py:182
  168.6 30.9 %collective-permute-start.28 = (bf16[704,256]{1,0:T(8,128)(2,1)S(1)}, bf16[704,256]{1,0:T(8,128)(2,1)}, u32[]{:S(2)}, u32[]{:S(2)}) collective-permute-start(bf16[704,256]{1,0:T(8,128)(2,1)S(1)} %slice.168), channel_id=1, source_target_pairs={{0,16},{8,24},{16,0},{24,8},{1,17},{9,25},{17,1},{25,9},{2,18},{10... | collective-permute-start | bytes 1081352 | tf_op jit(solution)/shard_map/ppermute | solution.py:42
  170.9 28.7 %collective-permute-start.29 = (bf16[704,256]{1,0:T(8,128)(2,1)S(1)}, bf16[704,256]{1,0:T(8,128)(2,1)}, u32[]{:S(2)}, u32[]{:S(2)}) collective-permute-start(bf16[704,256]{1,0:T(8,128)(2,1)S(1)} %slice.169), channel_id=1, source_target_pairs={{0,8},{8,0},{16,24},{24,16},{1,9},{9,1},{17,25},{25,17},{2,10},{10... | collective-permute-start | bytes 1081352 | tf_op jit(solution)/shard_map/ppermute | solution.py:42
  172.1 23.8 %collective-permute-start.26 = (bf16[704,512]{1,0:T(8,128)(2,1)S(1)}, bf16[704,512]{1,0:T(8,128)(2,1)}, u32[]{:S(2)}, u32[]{:S(2)}) collective-permute-start(bf16[704,512]{1,0:T(8,128)(2,1)S(1)} %copy-done.16), channel_id=1, source_target_pairs={{0,8},{8,0},{16,24},{24,16},{1,9},{9,1},{17,25},{25,17},{2,10},{10... | collective-permute-start | bytes 2162696 | tf_op jit(solution)/shard_map/ppermute | solution.py:42
  172.4 23.5 %collective-permute-start.27 = (bf16[704,512]{1,0:T(8,128)(2,1)S(1)}, bf16[704,512]{1,0:T(8,128)(2,1)}, u32[]{:S(2)}, u32[]{:S(2)}) collective-permute-start(bf16[704,512]{1,0:T(8,128)(2,1)S(1)} %copy-done.16), channel_id=1, source_target_pairs={{0,16},{8,24},{16,0},{24,8},{1,17},{9,25},{17,1},{25,9},{2,18},{10... | collective-permute-start | bytes 2162696 | tf_op jit(solution)/shard_map/ppermute | solution.py:42
  233.5 98.7 %all-gather.12.cloned.1.call-start = ((), (), s32[]{:S(2)}) async-start(), calls=%async_computation.6 | async-start | bytes 4718592 | tf_op jit(solution)/shard_map/all_gather | solution.py:178
  248.3 34.5 %collective-permute-start.36 = (bf16[1,704,512]{2,1,0:T(8,128)(2,1)}, bf16[1,704,512]{2,1,0:T(8,128)(2,1)}, u32[]{:S(2)}, u32[]{:S(2)}) collective-permute-start(bf16[1,704,512]{2,1,0:T(8,128)(2,1)} %get-tuple-element.227), channel_id=1, source_target_pairs={{0,8},{8,0},{16,24},{24,16},{1,9},{9,1},{17,25},{25,17},{2,10},{10... | collective-permute-start | bytes 2162696 | tf_op jit(solution)/shard_map/ppermute | solution.py:42
  248.6 34.2 %collective-permute-start.37 = (bf16[1,704,512]{2,1,0:T(8,128)(2,1)}, bf16[1,704,512]{2,1,0:T(8,128)(2,1)}, u32[]{:S(2)}, u32[]{:S(2)}) collective-permute-start(bf16[1,704,512]{2,1,0:T(8,128)(2,1)} %get-tuple-element.228), channel_id=1, source_target_pairs={{0,16},{8,24},{16,0},{24,8},{1,17},{9,25},{17,1},{25,9},{2,18},{10... | collective-permute-start | bytes 2162696 | tf_op jit(solution)/shard_map/ppermute | solution.py:42
  286.4 127.9 %reduce-scatter.6.cloned.1.call-start = ((), (), s32[]{:S(2)}) async-start(), calls=%async_computation.7 | async-start | bytes 4718592 | tf_op jit(solution)/shard_map/reduce_scatter | solution.py:182
  290.0 32.8 %collective-permute-start.39 = (bf16[2,704,512]{2,1,0:T(8,128)(2,1)}, bf16[2,704,512]{2,1,0:T(8,128)(2,1)}, u32[]{:S(2)}, u32[]{:S(2)}) collective-permute-start(bf16[2,704,512]{2,1,0:T(8,128)(2,1)} %pad_maximum_fusion.1), channel_id=1, source_target_pairs={{0,8},{8,0},{16,24},{24,16},{1,9},{9,1},{17,25},{25,17},{2,10},{10... | collective-permute-start | bytes 4325384 | tf_op jit(solution)/shard_map/ppermute | solution.py:42
  292.4 33.5 %collective-permute-start.38 = (bf16[2,704,512]{2,1,0:T(8,128)(2,1)}, bf16[2,704,512]{2,1,0:T(8,128)(2,1)}, u32[]{:S(2)}, u32[]{:S(2)}) collective-permute-start(bf16[2,704,512]{2,1,0:T(8,128)(2,1)} %pad_maximum_fusion), channel_id=1, source_target_pairs={{0,16},{8,24},{16,0},{24,8},{1,17},{9,25},{17,1},{25,9},{2,18},{10... | collective-permute-start | bytes 4325384 | tf_op jit(solution)/shard_map/ppermute | solution.py:42
  332.3 126.5 %reduce-scatter.8.cloned.1.call-start = ((), (), s32[]{:S(2)}) async-start(), calls=%async_computation.8 | async-start | bytes 4718592 | tf_op jit(solution)/shard_map/reduce_scatter | solution.py:182
  332.5 22.2 %collective-permute-start.35 = (bf16[704,512]{1,0:T(8,128)(2,1)}, bf16[704,512]{1,0:T(8,128)(2,1)}, u32[]{:S(2)}, u32[]{:S(2)}) collective-permute-start(bf16[704,512]{1,0:T(8,128)(2,1)} %pad_maximum_fusion.5), channel_id=1, source_target_pairs={{0,8},{8,0},{16,24},{24,16},{1,9},{9,1},{17,25},{25,17},{2,10},{10... | collective-permute-start | bytes 2162696 | tf_op jit(solution)/shard_map/ppermute | solution.py:42
  391.6 22.8 %collective-permute-start.43 = (bf16[8,72,768]{2,1,0:T(8,128)(2,1)S(1)}, bf16[8,72,768]{2,1,0:T(8,128)(2,1)}, u32[]{:S(2)}, u32[]{:S(2)}) collective-permute-start(bf16[8,72,768]{2,1,0:T(8,128)(2,1)S(1)} %pad_maximum_fusion.2), channel_id=1, source_target_pairs={{0,16},{8,24},{16,0},{24,8},{1,17},{9,25},{17,1},{25,9},{2,18},{10... | collective-permute-start | bytes 2654216 | tf_op jit(solution)/shard_map/ppermute | solution.py:42
  420.6 25.5 %collective-permute-start.48 = (bf16[1,72,768]{2,1,0:T(8,128)(2,1)S(1)}, bf16[1,72,768]{2,1,0:T(8,128)(2,1)S(1)}, u32[]{:S(2)}, u32[]{:S(2)}) collective-permute-start(bf16[1,72,768]{2,1,0:T(8,128)(2,1)S(1)} %get-tuple-element.256), channel_id=1, source_target_pairs={{0,3},{1,4},{2,5},{3,6},{4,7},{5,0},{6,1},{7,2},{8,11},{9,12},{10,... | collective-permute-start | bytes 331784 | tf_op jit(solution)/shard_map/ppermute | solution.py:160
  423.5 25.8 %collective-permute-start.49 = (bf16[1,72,768]{2,1,0:T(8,128)(2,1)S(1)}, bf16[1,72,768]{2,1,0:T(8,128)(2,1)S(1)}, u32[]{:S(2)}, u32[]{:S(2)}) collective-permute-start(bf16[1,72,768]{2,1,0:T(8,128)(2,1)S(1)} %get-tuple-element.255), channel_id=1, source_target_pairs={{0,4},{1,5},{2,6},{3,7},{4,0},{5,1},{6,2},{7,3},{8,12},{9,13},{10,... | collective-permute-start | bytes 331784 | tf_op jit(solution)/shard_map/ppermute | solution.py:160
  423.5 25.8 %collective-permute-start.50 = (bf16[1,72,768]{2,1,0:T(8,128)(2,1)S(1)}, bf16[1,72,768]{2,1,0:T(8,128)(2,1)S(1)}, u32[]{:S(2)}, u32[]{:S(2)}) collective-permute-start(bf16[1,72,768]{2,1,0:T(8,128)(2,1)S(1)} %get-tuple-element.254), channel_id=1, source_target_pairs={{0,5},{1,6},{2,7},{3,0},{4,1},{5,2},{6,3},{7,4},{8,13},{9,14},{10,... | collective-permute-start | bytes 331784 | tf_op jit(solution)/shard_map/ppermute | solution.py:160
  427.4 24.1 %collective-permute-start.51 = (bf16[1,72,768]{2,1,0:T(8,128)(2,1)S(1)}, bf16[1,72,768]{2,1,0:T(8,128)(2,1)S(1)}, u32[]{:S(2)}, u32[]{:S(2)}) collective-permute-start(bf16[1,72,768]{2,1,0:T(8,128)(2,1)S(1)} %get-tuple-element.253), channel_id=1, source_target_pairs={{0,6},{1,7},{2,0},{3,1},{4,2},{5,3},{6,4},{7,5},{8,14},{9,15},{10,... | collective-permute-start | bytes 331784 | tf_op jit(solution)/shard_map/ppermute | solution.py:160
  (82 other events, 1010.8 us)
Sparse Core Ops, SparseCore 0:
  39.8 46.4 all-gather.7
  87.9 29.3 all-gather.13
  118.8 45.1 all-gather.15
  165.5 45.8 all-gather.9
  233.7 49.0 reduce-scatter.3
  286.5 45.6 all-gather.11
  334.5 48.3 reduce-scatter.5
  385.2 65.6 reduce-scatter.7

commit v4 on v3

--- a/solution.py
+++ b/solution.py
@@ -25,6 +25,7 @@
 ADAM_EPS = 1e-08
 DECAY_RATE = 0.1
 TOKEN_BLOCK = 256
+FEED_BLOCK = 512
 EXTRA_ROWS = 8
 NT = (((1,), (1,)), ((), ()))
 TN = (((0,), (0,)), ((), ()))
@@ -46,7 +47,7 @@
     def __init__(self, shard, axis):
         self.axis = axis
         self.size = shard.shape[axis]
-        self.step = self.whole = None
+        self.step = self.whole = self.sends = None
         if lax.axis_size("rows") == 4:
             self.shard = shard
             self.step = (rows_swap(shard, 1), rows_swap(shard, 2))
@@ -63,13 +64,21 @@
         if self.step is not None:
             self.step = tie(*self.step, *values)[:2]
 
-    def second(self):
+    def halves(self, *values):
         if self.step is not None:
             self.near, self.far = self.step
             half = self.size // 2
             first = lax.slice_in_dim(self.near, 0, half, axis=self.axis)
             last = lax.slice_in_dim(self.far, half, self.size, axis=self.axis)
-            self.step = (rows_swap(first, 2), rows_swap(last, 1))
+            first, last, *values = tie(first, last, *values) if values else (first, last)
+            self.sends = (first, last)
+        return values if len(values) > 1 else values[0] if values else None
+
+    def second(self):
+        if self.step is not None:
+            if self.sends is None:
+                self.halves()
+            self.step = (rows_swap(self.sends[0], 2), rows_swap(self.sends[1], 1))
         return self
 
     def pieces(self):
@@ -348,7 +357,7 @@
 
 def piece_call(body, name, places, blocked, pieces, outs, products):
     tokens = blocked[0].shape[0]
-    block = min(TOKEN_BLOCK, tokens)
+    block = min(FEED_BLOCK, tokens)
 
     def spec(shape):
         if len(shape) == 3:
@@ -688,9 +697,17 @@
     if refs:
         rounded_ref, sums_ref = refs
         rounded_ref[...] = grad.astype(B)
-        sums_ref[...] = jnp.concatenate(
+        sums = jnp.concatenate(
             [jnp.sum(e * hat, axis=0, keepdims=True), jnp.sum(e, axis=0, keepdims=True)], 0
         )
+
+        @pl.when(pl.program_id(0) == 0)
+        def _():
+            sums_ref[...] = sums
+
+        @pl.when(pl.program_id(0) != 0)
+        def _():
+            sums_ref[...] += sums
 
 
 def norm_back(e, x, upstream, gain, more):
@@ -698,7 +715,17 @@
     outs = [jax.ShapeDtypeStruct((tokens, features), F)]
     if more:
         outs += [jax.ShapeDtypeStruct((tokens, features), B), jax.ShapeDtypeStruct((2, features), F)]
-    return pl.pallas_call(norm_back_body, out_shape=outs, name="norm_back")(e, x, upstream, gain)
+    block = min(64, tokens)
+    rows = row_spec(features, block)
+    sums = pl.BlockSpec((2, features), lambda i: (0, 0))
+    return pl.pallas_call(
+        norm_back_body,
+        grid=(tokens // block,),
+        in_specs=[rows, rows, rows, whole_spec(gain)],
+        out_specs=[rows, rows, sums] if more else [rows],
+        out_shape=outs,
+        name="norm_back",
+    )(e, x, upstream, gain)
 
 
 def pack_body(strided, me_ref, w_ref, norm_ref, bias_ref, out_ref):
@@ -756,31 +783,40 @@
 
 
 def finish_body(strided, wide, got_ref, w_ref, moment_ref, grad_ref, step_ref):
-    depth = w_ref.shape[0]
-    third = w_ref.shape[1] // 3
-    width = got_ref.shape[2] // 3
-    for part in range(3):
-        for at in range(third // 128):
-            if strided:
-                slot, owner = at * 2 // wide, at * 2 % wide
-                first = part * width + slot * HEAD_DIM
-                gradient = jnp.concatenate(
-                    [got_ref[owner + k, :depth, first : first + HEAD_DIM] for k in range(2)], 1
-                )
-            else:
-                owner, first = at * 128 // width, part * width + at * 128 % width
-                gradient = got_ref[owner, :depth, first : first + 128]
-            gradient = gradient.astype(F)
-            columns = slice(part * third + at * 128, part * third + at * 128 + 128)
-            grad_ref[:, columns] = gradient
-            step_ref[:, columns] = adam_step(
-                w_ref[:, columns], gradient, (moment_ref[0, :, columns], moment_ref[1, :, columns])
+    depth, third = w_ref.shape
+    width = got_ref.shape[2]
+    for at in range(third // 128):
+        if strided:
+            slot, owner = at * 2 // wide, at * 2 % wide
+            first = slot * HEAD_DIM
+            gradient = jnp.concatenate(
+                [got_ref[owner + k, :depth, first : first + HEAD_DIM] for k in range(2)], 1
             )
+        else:
+            owner, first = at * 128 // width, at * 128 % width
+            gradient = got_ref[owner, :depth, first : first + 128]
+        gradient = gradient.astype(F)
+        columns = slice(at * 128, at * 128 + 128)
+        grad_ref[:, columns] = gradient
+        step_ref[:, columns] = adam_step(
+            w_ref[:, columns], gradient, (moment_ref[0, :, columns], moment_ref[1, :, columns])
+        )
 
 
 def finish(received, w_qkv, moments, strided):
+    wide, rows, columns = received.shape
+    depth = w_qkv.shape[0]
+    third = w_qkv.shape[1] // 3
+    part = pl.BlockSpec((depth, third), lambda i: (0, i))
     return pl.pallas_call(
-        functools.partial(finish_body, strided, received.shape[0]),
+        functools.partial(finish_body, strided, wide),
+        grid=(3,),
+        in_specs=[
+            pl.BlockSpec((wide, rows, columns // 3), lambda i: (0, 0, i)),
+            part,
+            pl.BlockSpec((2, depth, third), lambda i: (0, 0, i)),
+        ],
+        out_specs=[part, part],
         out_shape=[jax.ShapeDtypeStruct(w_qkv.shape, F)] * 2,
         name="finish",
     )(received, w_qkv, moments)
@@ -809,10 +845,10 @@
     blocks = range(rows * wide)
     back = [(b % rows * wide + b // rows, b) for b in blocks]
     gate_first = gate_up.swapaxes(1, 2)
-    gate = RowsGather(gate_first[0], 1)
-    exchange = WideExchange(
-        pack(my_row * wide + my_wide, w_qkv, norm_params, b_qkv, strided, wide)
-    )
+    packed = pack(my_row * wide + my_wide, w_qkv, norm_params, b_qkv, strided, wide)
+    packed, gate_shard = tie(packed, gate_first[0])
+    gate = RowsGather(gate_shard, 1)
+    exchange = WideExchange(packed)
     segment_row, *arrived = exchange.before(segment_row, *(gate.step or ()))
     gate.step = arrived or None
     received, x_first = tie(exchange.join(), x_own)
@@ -826,6 +862,7 @@
         up_first, *gate.step = w_rows.before(gate_first[1], *gate.step)
     else:
         up_first = gate_first[1]
+    x_all, up_first = tie(gate.halves(x_all), up_first)
     up = RowsGather(up_first, 1)
     gate.second()
     if strided:
@@ -850,14 +887,16 @@
         out_line = lax.dynamic_index_in_dim(out_all, core, 1, False)
         out_pieces, out_places = [out_line.reshape(chips * width, features)], [jnp.int32(0)]
     swapped = [core_swap(piece) for piece in out_pieces]
+    norms_two = norms[2:]
+    attended_all = up.halves(attended_all)
     up.second()
-    attended_all, upstream, down_first, *swapped = tie(
-        attended_all, out_grad[0], w_down, *swapped
+    attended_all, upstream, down_first, norms_two, *swapped = tie(
+        attended_all, out_grad[0], w_down, norms_two, *swapped
     )
     down = RowsGather(down_first, 1)
     grads_all = wide_gather(upstream)
     tokens_all, after_all, out_mine = out_project(
-        (core, my_wide // 2), attended_all, out_pieces, swapped, out_places, x_all, norms[2:]
+        (core, my_wide // 2), attended_all, out_pieces, swapped, out_places, x_all, norms_two
     )
     tokens_all = down.before(tokens_all)
     down.second()

time: 477 us -> 476 us (level)
    unnamed x102 -> x88, local copies, waits for them, and re-layouts: 13.1 us -> 10.5 us
  transfers between devices with their start and end apart: 63 -> 63, of which waited for: 32 -> 32; matrix products, arithmetic and copies ran while one was open for 18% -> 18% of each run, Pallas kernels for 21% -> 20%
where the time goes in v4:
time: 476 us; the launch traced here: 470 us
  waiting for transfers between devices  173 us (36%)
  Pallas kernels  126 us (26%)
  starting transfers between devices  56.1 us (12%)
  local copies, waits for them, and re-layouts  40.8 us (9%)
  other arithmetic  31 us (7%)
  matrix products  26.3 us (6%)
  between operations  15.8 us (3%)
    ppermute x36, waiting for transfers between devices, rows_swap(): return lax.ppermute(value, 'rows', [(i, i ^ bits) for i in range(4)])  108 us
    pallas_call x3, Pallas kernels, piece_call(): pl.pallas_call(functools.partial(body, len(places)), grid_spec=pltpu.Pref...  42 us
    ppermute x14, waiting for transfers between devices, __init__(): block = lax.ppermute(block, 'wide', pairs)  33.7 us
    ppermute x36, starting transfers between devices, rows_swap(): return lax.ppermute(value, 'rows', [(i, i ^ bits) for i in range(4)])  31.8 us
    all_gather x3, waiting for transfers between devices, wide_gather(): return lax.all_gather(shard, 'wide', axis=0, tiled=True)  19.1 us
    pallas_call x1, Pallas kernels, out_project(): pl.pallas_call(functools.partial(out_project_body, len(same)), grid_spec=...  18.9 us
    ppermute x14, starting transfers between devices, __init__(): block = lax.ppermute(block, 'wide', pairs)  18.9 us
    pallas_call x1, Pallas kernels, attend_back(): pl.pallas_call(functools.partial(attend_back_body, heads), out_shape=[jax...  15.5 us
  transfers between devices with their start and end apart: 63, of which 32 were waited for; matrix products, arithmetic and copies ran while one was open for 18% of the time, Pallas kernels for 20%

profile of v4, /device:TPU:9, one launch (start us, length us, event | category | flops | bytes accessed | tf_op | source)
XLA Modules:
  0.0 469.5 jit_solution(16547648710121775639)
XLA Ops:
  26.6 7.4 %collective-permute-done.2 = bf16[1,72,768]{2,1,0:T(8,128)(2,1)} collective-permute-done((bf16[1,72,768]{2,1,0:T(8,128)(2,1)S(1)}, bf16[1,72,768]{2,1,0:T(8,128)(2,1)}, u32[]{:S(2)}, u32[]{:S(2)}) %collective-permute-start.2) | collective-permute-done | bytes 110624 | tf_op jit(solution)/shard_map/ppermute | solution.py:169
  42.3 5.4 %tables.1 = (f32[1024,128]{1,0:T(8,128)}, f32[1024,128]{1,0:T(8,128)}, f32[1024,128]{1,0:T(8,128)}) custom-call(s32[1024,1]{1,0:T(8,128)} %copy.30.col_ref.seg_col, s32[1,1024]{1,0:T(1,128)} %param.18), custom_call_target="tpu_custom_call" | custom-call | tf_op jit(solution)/shard_map/tables/pallas_call | solution.py:256
  47.6 14.5 %collective-permute-done.10.refs_7_ = bf16[8,72,768]{2,1,0:T(8,128)(2,1)S(1)} collective-permute-done((bf16[8,72,768]{2,1,0:T(8,128)(2,1)S(1)}, bf16[8,72,768]{2,1,0:T(8,128)(2,1)S(1)}, u32[]{:S(2)}, u32[]{:S(2)}) %collective-permute-start.10) | collective-permute-done | bytes 884768 | tf_op jit(solution)/shard_map/ppermute | solution.py:43
  66.2 10.3 %collective-permute-done.11.refs_8_ = bf16[4,72,768]{2,1,0:T(8,128)(2,1)S(1)} collective-permute-done((bf16[4,72,768]{2,1,0:T(8,128)(2,1)S(1)}, bf16[4,72,768]{2,1,0:T(8,128)(2,1)S(1)}, u32[]{:S(2)}, u32[]{:S(2)}) %collective-permute-start.11) | collective-permute-done | bytes 442400 | tf_op jit(solution)/shard_map/ppermute | solution.py:43
  80.3 7.1 %all-gather.8.cloned.1.call-done.refs_1_.refs_3_ = bf16[1024,2048]{1,0:T(8,128)(2,1)} async-done(((bf16[128,2048]{1,0:T(8,128)(2,1)}), bf16[1024,2048]{1,0:T(8,128)(2,1)}) %all-gather.8.cloned.1.call-update) | async-done | bytes 4194320 | tf_op jit(solution)/shard_map/all_gather | solution.py:187
  91.2 12.7 %project.1 = (bf16[1024,256]{1,0:T(8,128)(2,1)}, bf16[1024,256]{1,0:T(8,128)(2,1)}, bf16[1024,256]{1,0:T(8,128)(2,1)}, bf16[1024,2048]{1,0:T(8,128)(2,1)}, bf16[...) custom-call(s32[5]{0:T(128)} %stack.89.refs_0_, ...), custom_call_target="tpu_custom_call" | custom-call | flops 3221225472 | bytes 8388608 | tf_op jit(solution)/shard_map/project/pallas_call | solution.py:318
  103.9 8.2 %attend.1 = (bf16[1024,256]{1,0:T(8,128)(2,1)}, f32[1024,128]{1,0:T(8,128)}) custom-call(bf16[1024,256]{1,0:T(8,128)(2,1)} %get-tuple-element.157.q_ref, bf16[1024,256]{1,0:T(8,128)(2,1)} %get-tuple-element.158.k_ref, bf16[1024,256]{1,0:T(8,128)(2,1)} %get-tuple-element.159.v_ref, s32[1024,1]{1,0:T(8,128)} %copy.30.col_ref.seg_col, s32[1,1024]{1,0:T(1,128)} %param.18), custom_call_target="tpu_custom_call" | custom-call | flops 4294967296 | bytes 2097152 | tf_op jit(solution)/shard_map/attend/pallas_call | solution.py:492
  113.8 4.5 all-gather.14.cloned.1.call-done
  122.3 22.2 %collective-permute-done.17.refs_6_ = bf16[256,2048]{1,0:T(8,128)(2,1)S(1)} collective-permute-done((bf16[256,2048]{1,0:T(8,128)(2,1)S(1)}, bf16[256,2048]{1,0:T(8,128)(2,1)S(1)}, u32[]{:S(2)}, u32[]{:S(2)}) %collective-permute-start.17) | collective-permute-done | bytes 1048608 | tf_op jit(solution)/shard_map/ppermute | solution.py:43
  150.2 7.0 %collective-permute-done.18.refs_8_ = bf16[128,2048]{1,0:T(8,128)(2,1)} collective-permute-done((bf16[128,2048]{1,0:T(8,128)(2,1)S(1)}, bf16[128,2048]{1,0:T(8,128)(2,1)}, u32[]{:S(2)}, u32[]{:S(2)}) %collective-permute-start.18) | collective-permute-done | bytes 524320 | tf_op jit(solution)/shard_map/ppermute | solution.py:43
  170.3 18.9 %out_project.1 = (bf16[1024,2048]{1,0:T(8,128)(2,1)}, f32[1024,2048]{1,0:T(8,128)}, bf16[256,2048]{1,0:T(8,128)(2,1)}) custom-call(s32[2]{0:T(128)} %pad_add_fusion.refs_0_, s32[5]{0:T(128)} %stack.83.refs_1_, bf16[8,1024,256]{2,1,0:T(8,128)(2,1)} %bitcast.111, bf16[1024,2048]{1,0:T(8,128)(2,1)} %all-gather.8.cloned.1.call-done.refs_1_.refs_3_, ...), custom_call_target="tpu_custom_call" | custom-call | flops 8589934592 | bytes 16777216 | tf_op jit(solution)/shard_map/out_project/pallas_call | solution.py:542
  193.8 12.9 %gate_up.1 = (f32[1024,704]{1,0:T(8,128)}, f32[1024,704]{1,0:T(8,128)}, bf16[1024,704]{1,0:T(8,128)(2,1)}) custom-call(s32[5]{0:T(128)} %stack.95.refs_0_, bf16[1024,2048]{1,0:T(8,128)(2,1)} %get-tuple-element.204.refs_1_, bf16[704,512]{1,0:T(8,128)(2,1)} %copy-done.19, bf16[704,512]{1,0:T(8,128)(2,1)} %copy-done.25, bf16[704,512]{1,0:T(8,128)(2,1)} %copy-done.26, ...), custom_call_target="tpu_custom_call" | custom-call | flops 5905580032 | bytes 9961472 | tf_op jit(solution)/shard_map/gate_up/pallas_call | solution.py:368
  206.7 5.7 %all-gather.10.cloned.1.call-done.refs_1_ = bf16[1024,2048]{1,0:T(8,128)(2,1)} async-done(((bf16[128,2048]{1,0:T(8,128)(2,1)}), bf16[1024,2048]{1,0:T(8,128)(2,1)}) %all-gather.10.cloned.1.call-update) | async-done | bytes 4194320 | tf_op jit(solution)/shard_map/all_gather | solution.py:187
  212.5 21.4 %feed_back.1 = (bf16[2,1024,704]{2,1,0:T(8,128)(2,1)}, bf16[1024,2048]{1,0:T(8,128)(2,1)}) custom-call(s32[5]{0:T(128)} %stack.95.refs_0_, bf16[1024,2048]{1,0:T(8,128)(2,1)} %all-gather.10.cloned.1.call-done.refs_1_, f32[1024,704]{1,0:T(8,128)} %get-tuple-element.192.refs_2_, f32[1024,704]{1,0:T(8,128)} %get-tuple-element.193.refs_3_, ...), custom_call_target="tpu_custom_call" | custom-call | flops 8858370048 | bytes 18612224 | tf_op jit(solution)/shard_map/feed_back/pallas_call | solution.py:368
  235.8 8.6 %convolution_convert_fusion = bf16[2,704,2048]{2,1,0:T(8,128)(2,1)S(1)} fusion(bf16[2,1024,704]{2,1,0:T(8,128)(2,1)S(1)} %copy-done.41, bf16[1024,2048]{1,0:T(8,128)(2,1)} %get-tuple-element.204.refs_1_), kind=kOutput, calls=%fused_computation | convolution fusion | flops 5908463616 | bytes 12845056 | tf_op jit(solution)/shard_map/gtf,td->gfd/dot_general | solution.py:909
  260.0 14.3 %collective-permute-done.32 = bf16[352,512]{1,0:T(8,128)(2,1)} collective-permute-done((bf16[352,512]{1,0:T(8,128)(2,1)S(1)}, bf16[352,512]{1,0:T(8,128)(2,1)}, u32[]{:S(2)}, u32[]{:S(2)}) %collective-permute-start.32) | collective-permute-done | bytes 360480 | tf_op jit(solution)/shard_map/ppermute | solution.py:43
  275.1 7.3 %reduce-scatter.4.cloned.1.call-done.e_ref = bf16[128,2048]{1,0:T(8,128)(2,1)} async-done(((bf16[1024,2048]{1,0:T(8,128)(2,1)}), bf16[128,2048]{1,0:T(8,128)(2,1)}) %reduce-scatter.4.cloned.1.call-update) | async-done | bytes 524304 | tf_op jit(solution)/shard_map/reduce_scatter | solution.py:191
  296.0 7.6 %down.1 = bf16[1024,2048]{1,0:T(8,128)(2,1)} custom-call(s32[5]{0:T(128)} %stack.95.refs_0_, bf16[1024,704]{1,0:T(8,128)(2,1)} %get-tuple-element.208.refs_1_, bf16[704,512]{1,0:T(8,128)(2,1)} %refs_2_, bf16[704,512]{1,0:T(8,128)(2,1)} %collective-permute-done.26.refs_5_.refs_3_, bf16[704,512]{1,0:T(8,128)(2,1)} %collective-permute-done.27.refs_6_.refs_4_, ...), custom_call_target="tpu_custom_call" | custom-call | flops 2952790016 | bytes 4325376 | tf_op jit(solution)/shard_map/down/pallas_call | solution.py:368
  303.7 18.2 %collective-permute-done.39 = bf16[2,704,512]{2,1,0:T(8,128)(2,1)} collective-permute-done((bf16[2,704,512]{2,1,0:T(8,128)(2,1)}, bf16[2,704,512]{2,1,0:T(8,128)(2,1)}, u32[]{:S(2)}, u32[]{:S(2)}) %collective-permute-start.39) | collective-permute-done | bytes 1441824 | tf_op jit(solution)/shard_map/ppermute | solution.py:43
  325.1 6.3 %all-gather.12.cloned.1.call-done = bf16[1024,2048]{1,0:T(8,128)(2,1)} async-done(((bf16[128,2048]{1,0:T(8,128)(2,1)}), bf16[1024,2048]{1,0:T(8,128)(2,1)}) %all-gather.12.cloned.1.call-update) | async-done | bytes 4194320 | tf_op jit(solution)/shard_map/all_gather | solution.py:187
  334.1 4.3 convolution_convert_fusion.4.g_ref
  338.4 15.5 %attend_back.1 = (bf16[1024,768]{1,0:T(8,128)(2,1)}, f32[1,768]{1,0:T(1,128)}) custom-call(bf16[1024,256]{1,0:T(8,128)(2,1)} %get-tuple-element.157.q_ref, bf16[1024,256]{1,0:T(8,128)(2,1)} %get-tuple-element.158.k_ref, bf16[1024,256]{1,0:T(8,128)(2,1)} %get-tuple-element.159.v_ref, bf16[1024,256]{1,0:T(8,128)(2,1)} %convolution_convert_fusion.4.g_ref, ...), custom_call_target="tpu_custom_call" | custom-call | flops 8589934592 | bytes 4194304 | tf_op jit(solution)/shard_map/attend_back/pallas_call | solution.py:625
  353.9 6.5 %convolution_convert_fusion.1 = bf16[1024,2048]{1,0:T(8,128)(2,1)} fusion(bf16[1024,768]{1,0:T(8,128)(2,1)} %get-tuple-element.219.grad_ref, bf16[2048,768]{1,0:T(8,128)(2,1)S(1)} %copy-done.4), kind=kOutput, calls=%fused_computation.3 | convolution fusion | flops 3223322624 | bytes 8912896 | tf_op jit(solution)/shard_map/dot_general | solution.py:35
  361.4 3.5 convolution_convert_fusion.3
  366.9 9.3 %weights_back.1 = bf16[32,72,768]{2,1,0:T(8,128)(2,1)} custom-call(bf16[1024,2048]{1,0:T(8,128)(2,1)} %get-tuple-element.218.hat_ref, bf16[1024,768]{1,0:T(8,128)(2,1)} %get-tuple-element.219.grad_ref, bf16[2048,768]{1,0:T(8,128)(2,1)} %get-tuple-element.216.w_ref, f32[4,2048]{1,0:T(4,128)} %get-tuple-element.173.norms_ref, ...), custom_call_target="tpu_custom_call" | custom-call | flops 3221225472 | bytes 8388608 | tf_op jit(solution)/shard_map/weights_back/pallas_call | solution.py:671
  383.8 4.1 collective-permute-done.42
  397.1 4.6 fusion.13
  401.7 5.8 %fusion.6 = (f32[2,512,704]{1,2,0:T(8,128)}, f32[2,512,704]{1,2,0:T(8,128)}) fusion(bf16[2,512,704]{1,2,0:T(8,128)(2,1)S(1)} %copy-done.2, f32[2,2,512,704]{2,3,1,0:T(8,128)S(1)} %bitcast.95, f32[]{:T(128)} %bitcast.34, bf16[2,704,512]{2,1,0:T(8,128)(2,1)} %collective-permute-done.39, bf16[2,704,512]{2,1,0:T(8,128)(2,1)} %collective-permute-done.38, ...), kind=kLoop, calls=%fused_computation.10 | loop fusion | flops 14417920 | bytes 17301512 | tf_op jit(solution)/shard_map/add | solution.py:780
  407.5 3.9 collective-permute-done.45
  415.5 4.0 collective-permute-start.46
  430.3 15.0 %collective-permute-done.48 = bf16[1,72,768]{2,1,0:T(8,128)(2,1)S(1)} collective-permute-done((bf16[1,72,768]{2,1,0:T(8,128)(2,1)S(1)}, bf16[1,72,768]{2,1,0:T(8,128)(2,1)S(1)}, u32[]{:S(2)}, u32[]{:S(2)}) %collective-permute-start.48) | collective-permute-done | bytes 110624 | tf_op jit(solution)/shard_map/ppermute | solution.py:169
  451.7 5.4 %finish.1 = (f32[64,6144]{1,0:T(8,128)}, f32[64,6144]{1,0:T(8,128)}) custom-call(bf16[8,72,768]{2,1,0:T(8,128)(2,1)} %copy-done.3, bf16[64,6144]{1,0:T(8,128)(2,1)} %w_ref.3, f32[2,64,6144]{2,1,0:T(8,128)} %moment_ref.1), custom_call_target="tpu_custom_call" | custom-call | tf_op jit(solution)/shard_map/finish/pallas_call | solution.py:811
  (281 shorter events, 151.2 us)
Async XLA Ops:
  7.2 80.2 %all-gather.8.cloned.1.call-start = ((), (), s32[]{:S(2)}) async-start(), calls=%async_computation.3 | async-start | bytes 4718592 | tf_op jit(solution)/shard_map/all_gather | solution.py:187
  12.8 21.2 %collective-permute-start.3 = (bf16[704,512]{1,0:T(8,128)(2,1)S(1)}, bf16[704,512]{1,0:T(8,128)(2,1)S(1)}, u32[]{:S(2)}, u32[]{:S(2)}) collective-permute-start(bf16[704,512]{1,0:T(8,128)(2,1)S(1)} %get-tuple-element.128.refs_2_.refs_9_), channel_id=1, source_target_pairs={{0,8},{8,0},{16,24},{24,16},{1,9},{9,1},{17,25},{25,17},{2,10},{10... | collective-permute-start | bytes 2162696 | tf_op jit(solution)/shard_map/ppermute | solution.py:43
  14.0 21.8 %collective-permute-start.4 = (bf16[704,512]{1,0:T(8,128)(2,1)S(1)}, bf16[704,512]{1,0:T(8,128)(2,1)S(1)}, u32[]{:S(2)}, u32[]{:S(2)}) collective-permute-start(bf16[704,512]{1,0:T(8,128)(2,1)S(1)} %get-tuple-element.128.refs_2_.refs_9_), channel_id=1, source_target_pairs={{0,16},{8,24},{16,0},{24,8},{1,17},{9,25},{17,1},{25,9},{2,18},{10... | collective-permute-start | bytes 2162696 | tf_op jit(solution)/shard_map/ppermute | solution.py:43
  40.8 77.6 %all-gather.14.cloned.1.call-start = ((), (), s32[]{:S(2)}) async-start(), calls=%async_computation.9 | async-start | bytes 2359296 | tf_op jit(solution)/shard_map/all_gather | solution.py:870
  40.8 21.3 %collective-permute-start.10 = (bf16[8,72,768]{2,1,0:T(8,128)(2,1)S(1)}, bf16[8,72,768]{2,1,0:T(8,128)(2,1)S(1)}, u32[]{:S(2)}, u32[]{:S(2)}) collective-permute-start(bf16[8,72,768]{2,1,0:T(8,128)(2,1)S(1)} %constant_dynamic-update-slice_fusion.7.refs_5_), channel_id=1, source_target_pairs={{0,16},{8,24},{16,0},{24,8},{1,17},{9,25},{17,1},{25,9},{2,18},{10... | collective-permute-start | bytes 2654216 | tf_op jit(solution)/shard_map/ppermute | solution.py:43
  41.1 21.5 %collective-permute-start.9 = (bf16[8,72,768]{2,1,0:T(8,128)(2,1)S(1)}, bf16[8,72,768]{2,1,0:T(8,128)(2,1)S(1)}, u32[]{:S(2)}, u32[]{:S(2)}) collective-permute-start(bf16[8,72,768]{2,1,0:T(8,128)(2,1)S(1)} %constant_dynamic-update-slice_fusion.7.refs_5_), channel_id=1, source_target_pairs={{0,8},{8,0},{16,24},{24,16},{1,9},{9,1},{17,25},{25,17},{2,10},{10... | collective-permute-start | bytes 2654216 | tf_op jit(solution)/shard_map/ppermute | solution.py:43
  87.4 77.7 %all-gather.16.cloned.1.call-start = ((), (), s32[]{:S(2)}) async-start(), calls=%async_computation.10 | async-start | bytes 4718592 | tf_op jit(solution)/shard_map/all_gather | solution.py:876
  87.6 24.5 %collective-permute-start.13 = (bf16[704,512]{1,0:T(8,128)(2,1)S(1)}, bf16[704,512]{1,0:T(8,128)(2,1)}, u32[]{:S(2)}, u32[]{:S(2)}) collective-permute-start(bf16[704,512]{1,0:T(8,128)(2,1)S(1)} %get-tuple-element.147.refs_7_.refs_14_), channel_id=1, source_target_pairs={{0,8},{8,0},{16,24},{24,16},{1,9},{9,1},{17,25},{25,17},{2,10},{10... | collective-permute-start | bytes 2162696 | tf_op jit(solution)/shard_map/ppermute | solution.py:43
  88.9 23.2 %collective-permute-start.14 = (bf16[704,512]{1,0:T(8,128)(2,1)S(1)}, bf16[704,512]{1,0:T(8,128)(2,1)}, u32[]{:S(2)}, u32[]{:S(2)}) collective-permute-start(bf16[704,512]{1,0:T(8,128)(2,1)S(1)} %get-tuple-element.147.refs_7_.refs_14_), channel_id=1, source_target_pairs={{0,16},{8,24},{16,0},{24,8},{1,17},{9,25},{17,1},{25,9},{2,18},{10... | collective-permute-start | bytes 2162696 | tf_op jit(solution)/shard_map/ppermute | solution.py:43
  90.7 23.2 %collective-permute-start.15 = (bf16[704,256]{1,0:T(8,128)(2,1)S(1)}, bf16[704,256]{1,0:T(8,128)(2,1)}, u32[]{:S(2)}, u32[]{:S(2)}) collective-permute-start(bf16[704,256]{1,0:T(8,128)(2,1)S(1)} %slice.163), channel_id=1, source_target_pairs={{0,16},{8,24},{16,0},{24,8},{1,17},{9,25},{17,1},{25,9},{2,18},{10... | collective-permute-start | bytes 1081352 | tf_op jit(solution)/shard_map/ppermute | solution.py:43
  90.9 22.9 %collective-permute-start.16 = (bf16[704,256]{1,0:T(8,128)(2,1)S(1)}, bf16[704,256]{1,0:T(8,128)(2,1)}, u32[]{:S(2)}, u32[]{:S(2)}) collective-permute-start(bf16[704,256]{1,0:T(8,128)(2,1)S(1)} %slice.164), channel_id=1, source_target_pairs={{0,8},{8,0},{16,24},{24,16},{1,9},{9,1},{17,25},{25,17},{2,10},{10... | collective-permute-start | bytes 1081352 | tf_op jit(solution)/shard_map/ppermute | solution.py:43
  118.4 94.1 %all-gather.10.cloned.1.call-start = ((), (), s32[]{:S(2)}) async-start(), calls=%async_computation.4 | async-start | bytes 4718592 | tf_op jit(solution)/shard_map/all_gather | solution.py:187
  119.8 24.7 %collective-permute-start.17 = (bf16[256,2048]{1,0:T(8,128)(2,1)S(1)}, bf16[256,2048]{1,0:T(8,128)(2,1)S(1)}, u32[]{:S(2)}, u32[]{:S(2)}) collective-permute-start(bf16[256,2048]{1,0:T(8,128)(2,1)S(1)} %bitcast.102), channel_id=1, source_target_pairs={{0,8},{8,0},{16,24},{24,16},{1,9},{9,1},{17,25},{25,17},{2,10},{10... | collective-permute-start | bytes 3145736 | tf_op jit(solution)/shard_map/ppermute | solution.py:43
  121.1 24.7 %collective-permute-start.19 = (bf16[256,2048]{1,0:T(8,128)(2,1)S(1)}, bf16[256,2048]{1,0:T(8,128)(2,1)}, u32[]{:S(2)}, u32[]{:S(2)}) collective-permute-start(bf16[256,2048]{1,0:T(8,128)(2,1)S(1)} %bitcast.103), channel_id=1, source_target_pairs={{0,16},{8,24},{16,0},{24,8},{1,17},{9,25},{17,1},{25,9},{2,18},{10... | collective-permute-start | bytes 3145736 | tf_op jit(solution)/shard_map/ppermute | solution.py:43
  165.1 117.2 %reduce-scatter.4.cloned.1.call-start = ((), (), s32[]{:S(2)}) async-start(), calls=%async_computation.5 | async-start | bytes 4718592 | tf_op jit(solution)/shard_map/reduce_scatter | solution.py:191
  167.4 21.9 %collective-permute-start.26 = (bf16[704,512]{1,0:T(8,128)(2,1)S(1)}, bf16[704,512]{1,0:T(8,128)(2,1)}, u32[]{:S(2)}, u32[]{:S(2)}) collective-permute-start(bf16[704,512]{1,0:T(8,128)(2,1)S(1)} %copy-done.16), channel_id=1, source_target_pairs={{0,8},{8,0},{16,24},{24,16},{1,9},{9,1},{17,25},{25,17},{2,10},{10... | collective-permute-start | bytes 2162696 | tf_op jit(solution)/shard_map/ppermute | solution.py:43
  169.8 24.0 %collective-permute-start.28 = (bf16[704,256]{1,0:T(8,128)(2,1)S(1)}, bf16[704,256]{1,0:T(8,128)(2,1)}, u32[]{:S(2)}, u32[]{:S(2)}) collective-permute-start(bf16[704,256]{1,0:T(8,128)(2,1)S(1)} %slice.167), channel_id=1, source_target_pairs={{0,16},{8,24},{16,0},{24,8},{1,17},{9,25},{17,1},{25,9},{2,18},{10... | collective-permute-start | bytes 1081352 | tf_op jit(solution)/shard_map/ppermute | solution.py:43
  170.0 23.8 %collective-permute-start.29 = (bf16[704,256]{1,0:T(8,128)(2,1)S(1)}, bf16[704,256]{1,0:T(8,128)(2,1)}, u32[]{:S(2)}, u32[]{:S(2)}) collective-permute-start(bf16[704,256]{1,0:T(8,128)(2,1)S(1)} %slice.168), channel_id=1, source_target_pairs={{0,8},{8,0},{16,24},{24,16},{1,9},{9,1},{17,25},{25,17},{2,10},{10... | collective-permute-start | bytes 1081352 | tf_op jit(solution)/shard_map/ppermute | solution.py:43
  233.9 97.5 %all-gather.12.cloned.1.call-start = ((), (), s32[]{:S(2)}) async-start(), calls=%async_computation.6 | async-start | bytes 4718592 | tf_op jit(solution)/shard_map/all_gather | solution.py:187
  248.7 33.7 %collective-permute-start.36 = (bf16[1,704,512]{2,1,0:T(8,128)(2,1)}, bf16[1,704,512]{2,1,0:T(8,128)(2,1)}, u32[]{:S(2)}, u32[]{:S(2)}) collective-permute-start(bf16[1,704,512]{2,1,0:T(8,128)(2,1)} %get-tuple-element.249), channel_id=1, source_target_pairs={{0,8},{8,0},{16,24},{24,16},{1,9},{9,1},{17,25},{25,17},{2,10},{10... | collective-permute-start | bytes 2162696 | tf_op jit(solution)/shard_map/ppermute | solution.py:43
  249.9 32.5 %collective-permute-start.37 = (bf16[1,704,512]{2,1,0:T(8,128)(2,1)}, bf16[1,704,512]{2,1,0:T(8,128)(2,1)}, u32[]{:S(2)}, u32[]{:S(2)}) collective-permute-start(bf16[1,704,512]{2,1,0:T(8,128)(2,1)} %get-tuple-element.250), channel_id=1, source_target_pairs={{0,16},{8,24},{16,0},{24,8},{1,17},{9,25},{17,1},{25,9},{2,18},{10... | collective-permute-start | bytes 2162696 | tf_op jit(solution)/shard_map/ppermute | solution.py:43
  285.6 127.9 %reduce-scatter.6.cloned.1.call-start = ((), (), s32[]{:S(2)}) async-start(), calls=%async_computation.7 | async-start | bytes 4718592 | tf_op jit(solution)/shard_map/reduce_scatter | solution.py:191
  289.2 32.7 %collective-permute-start.39 = (bf16[2,704,512]{2,1,0:T(8,128)(2,1)}, bf16[2,704,512]{2,1,0:T(8,128)(2,1)}, u32[]{:S(2)}, u32[]{:S(2)}) collective-permute-start(bf16[2,704,512]{2,1,0:T(8,128)(2,1)} %pad_maximum_fusion.1), channel_id=1, source_target_pairs={{0,8},{8,0},{16,24},{24,16},{1,9},{9,1},{17,25},{25,17},{2,10},{10... | collective-permute-start | bytes 4325384 | tf_op jit(solution)/shard_map/ppermute | solution.py:43
  291.6 33.5 %collective-permute-start.38 = (bf16[2,704,512]{2,1,0:T(8,128)(2,1)}, bf16[2,704,512]{2,1,0:T(8,128)(2,1)}, u32[]{:S(2)}, u32[]{:S(2)}) collective-permute-start(bf16[2,704,512]{2,1,0:T(8,128)(2,1)} %pad_maximum_fusion), channel_id=1, source_target_pairs={{0,16},{8,24},{16,0},{24,8},{1,17},{9,25},{17,1},{25,9},{2,18},{10... | collective-permute-start | bytes 4325384 | tf_op jit(solution)/shard_map/ppermute | solution.py:43
  331.5 126.7 %reduce-scatter.8.cloned.1.call-start = ((), (), s32[]{:S(2)}) async-start(), calls=%async_computation.8 | async-start | bytes 4718592 | tf_op jit(solution)/shard_map/reduce_scatter | solution.py:191
  331.7 22.2 %collective-permute-start.35 = (bf16[704,512]{1,0:T(8,128)(2,1)}, bf16[704,512]{1,0:T(8,128)(2,1)}, u32[]{:S(2)}, u32[]{:S(2)}) collective-permute-start(bf16[704,512]{1,0:T(8,128)(2,1)} %pad_maximum_fusion.5), channel_id=1, source_target_pairs={{0,8},{8,0},{16,24},{24,16},{1,9},{9,1},{17,25},{25,17},{2,10},{10... | collective-permute-start | bytes 2162696 | tf_op jit(solution)/shard_map/ppermute | solution.py:43
  390.3 21.2 %collective-permute-start.45 = (bf16[8,72,768]{2,1,0:T(8,128)(2,1)S(1)}, bf16[8,72,768]{2,1,0:T(8,128)(2,1)S(1)}, u32[]{:S(2)}, u32[]{:S(2)}) collective-permute-start(bf16[8,72,768]{2,1,0:T(8,128)(2,1)S(1)} %pad_maximum_fusion.3), channel_id=1, source_target_pairs={{0,8},{8,0},{16,24},{24,16},{1,9},{9,1},{17,25},{25,17},{2,10},{10... | collective-permute-start | bytes 2654216 | tf_op jit(solution)/shard_map/ppermute | solution.py:43
  390.7 22.7 %collective-permute-start.43 = (bf16[8,72,768]{2,1,0:T(8,128)(2,1)S(1)}, bf16[8,72,768]{2,1,0:T(8,128)(2,1)}, u32[]{:S(2)}, u32[]{:S(2)}) collective-permute-start(bf16[8,72,768]{2,1,0:T(8,128)(2,1)S(1)} %pad_maximum_fusion.2), channel_id=1, source_target_pairs={{0,16},{8,24},{16,0},{24,8},{1,17},{9,25},{17,1},{25,9},{2,18},{10... | collective-permute-start | bytes 2654216 | tf_op jit(solution)/shard_map/ppermute | solution.py:43
  419.7 25.5 %collective-permute-start.48 = (bf16[1,72,768]{2,1,0:T(8,128)(2,1)S(1)}, bf16[1,72,768]{2,1,0:T(8,128)(2,1)S(1)}, u32[]{:S(2)}, u32[]{:S(2)}) collective-permute-start(bf16[1,72,768]{2,1,0:T(8,128)(2,1)S(1)} %get-tuple-element.278), channel_id=1, source_target_pairs={{0,3},{1,4},{2,5},{3,6},{4,7},{5,0},{6,1},{7,2},{8,11},{9,12},{10,... | collective-permute-start | bytes 331784 | tf_op jit(solution)/shard_map/ppermute | solution.py:169
  422.6 25.9 %collective-permute-start.49 = (bf16[1,72,768]{2,1,0:T(8,128)(2,1)S(1)}, bf16[1,72,768]{2,1,0:T(8,128)(2,1)S(1)}, u32[]{:S(2)}, u32[]{:S(2)}) collective-permute-start(bf16[1,72,768]{2,1,0:T(8,128)(2,1)S(1)} %get-tuple-element.277), channel_id=1, source_target_pairs={{0,4},{1,5},{2,6},{3,7},{4,0},{5,1},{6,2},{7,3},{8,12},{9,13},{10,... | collective-permute-start | bytes 331784 | tf_op jit(solution)/shard_map/ppermute | solution.py:169
  422.6 25.9 %collective-permute-start.50 = (bf16[1,72,768]{2,1,0:T(8,128)(2,1)S(1)}, bf16[1,72,768]{2,1,0:T(8,128)(2,1)S(1)}, u32[]{:S(2)}, u32[]{:S(2)}) collective-permute-start(bf16[1,72,768]{2,1,0:T(8,128)(2,1)S(1)} %get-tuple-element.276), channel_id=1, source_target_pairs={{0,5},{1,6},{2,7},{3,0},{4,1},{5,2},{6,3},{7,4},{8,13},{9,14},{10,... | collective-permute-start | bytes 331784 | tf_op jit(solution)/shard_map/ppermute | solution.py:169
  426.5 24.2 %collective-permute-start.51 = (bf16[1,72,768]{2,1,0:T(8,128)(2,1)S(1)}, bf16[1,72,768]{2,1,0:T(8,128)(2,1)S(1)}, u32[]{:S(2)}, u32[]{:S(2)}) collective-permute-start(bf16[1,72,768]{2,1,0:T(8,128)(2,1)S(1)} %get-tuple-element.275), channel_id=1, source_target_pairs={{0,6},{1,7},{2,0},{3,1},{4,2},{5,3},{6,4},{7,5},{8,14},{9,15},{10,... | collective-permute-start | bytes 331784 | tf_op jit(solution)/shard_map/ppermute | solution.py:169
  (75 other events, 983.4 us)
Sparse Core Ops, SparseCore 0:
  40.9 46.4 all-gather.7
  89.0 29.3 all-gather.13
  119.9 45.1 all-gather.15
  166.5 45.8 all-gather.9
  234.0 48.2 reduce-scatter.3
  285.7 45.6 all-gather.11
  333.7 48.3 reduce-scatter.5
  384.4 65.6 reduce-scatter.7

commit v5 on v4

--- a/solution.py
+++ b/solution.py
@@ -25,7 +25,7 @@
 ADAM_EPS = 1e-08
 DECAY_RATE = 0.1
 TOKEN_BLOCK = 256
-FEED_BLOCK = 512
+FEED_BLOCK = 256
 EXTRA_ROWS = 8
 NT = (((1,), (1,)), ((), ()))
 TN = (((0,), (0,)), ((), ()))

time: 476 us -> 475 us (level)
  no operation moved by 1% of the time
where the time goes in v5:
time: 475 us; the launch traced here: 469 us
  waiting for transfers between devices  173 us (36%)
  Pallas kernels  125 us (26%)
  starting transfers between devices  56.2 us (12%)
  local copies, waits for them, and re-layouts  40.8 us (9%)
  other arithmetic  31 us (7%)
  matrix products  26.3 us (6%)
  between operations  15.8 us (3%)
    ppermute x36, waiting for transfers between devices, rows_swap(): return lax.ppermute(value, 'rows', [(i, i ^ bits) for i in range(4)])  108 us
    pallas_call x3, Pallas kernels, piece_call(): pl.pallas_call(functools.partial(body, len(places)), grid_spec=pltpu.Pref...  41 us
    ppermute x14, waiting for transfers between devices, __init__(): block = lax.ppermute(block, 'wide', pairs)  33.7 us
    ppermute x36, starting transfers between devices, rows_swap(): return lax.ppermute(value, 'rows', [(i, i ^ bits) for i in range(4)])  31.8 us
    all_gather x3, waiting for transfers between devices, wide_gather(): return lax.all_gather(shard, 'wide', axis=0, tiled=True)  19.9 us
    ppermute x14, starting transfers between devices, __init__(): block = lax.ppermute(block, 'wide', pairs)  18.9 us
    pallas_call x1, Pallas kernels, out_project(): pl.pallas_call(functools.partial(out_project_body, len(same)), grid_spec=...  18.9 us
    pallas_call x1, Pallas kernels, attend_back(): pl.pallas_call(functools.partial(attend_back_body, heads), out_shape=[jax...  15.5 us
  transfers between devices with their start and end apart: 63, of which 32 were waited for; matrix products, arithmetic and copies ran while one was open for 18% of the time, Pallas kernels for 20%

profile of v5, /device:TPU:9, one launch (start us, length us, event | category | flops | bytes accessed | tf_op | source)
XLA Modules:
  0.0 468.9 jit_solution(3810554382183107015)
XLA Ops:
  26.6 7.4 %collective-permute-done.2 = bf16[1,72,768]{2,1,0:T(8,128)(2,1)} collective-permute-done((bf16[1,72,768]{2,1,0:T(8,128)(2,1)S(1)}, bf16[1,72,768]{2,1,0:T(8,128)(2,1)}, u32[]{:S(2)}, u32[]{:S(2)}) %collective-permute-start.2) | collective-permute-done | bytes 110624 | tf_op jit(solution)/shard_map/ppermute | solution.py:169
  42.3 5.4 %tables.1 = (f32[1024,128]{1,0:T(8,128)}, f32[1024,128]{1,0:T(8,128)}, f32[1024,128]{1,0:T(8,128)}) custom-call(s32[1024,1]{1,0:T(8,128)} %copy.30.col_ref.seg_col, s32[1,1024]{1,0:T(1,128)} %param.18), custom_call_target="tpu_custom_call" | custom-call | tf_op jit(solution)/shard_map/tables/pallas_call | solution.py:256
  47.6 14.5 %collective-permute-done.10.refs_7_ = bf16[8,72,768]{2,1,0:T(8,128)(2,1)S(1)} collective-permute-done((bf16[8,72,768]{2,1,0:T(8,128)(2,1)S(1)}, bf16[8,72,768]{2,1,0:T(8,128)(2,1)S(1)}, u32[]{:S(2)}, u32[]{:S(2)}) %collective-permute-start.10) | collective-permute-done | bytes 884768 | tf_op jit(solution)/shard_map/ppermute | solution.py:43
  66.2 10.3 %collective-permute-done.11.refs_8_ = bf16[4,72,768]{2,1,0:T(8,128)(2,1)S(1)} collective-permute-done((bf16[4,72,768]{2,1,0:T(8,128)(2,1)S(1)}, bf16[4,72,768]{2,1,0:T(8,128)(2,1)S(1)}, u32[]{:S(2)}, u32[]{:S(2)}) %collective-permute-start.11) | collective-permute-done | bytes 442400 | tf_op jit(solution)/shard_map/ppermute | solution.py:43
  80.3 7.1 %all-gather.8.cloned.1.call-done.refs_1_.refs_3_ = bf16[1024,2048]{1,0:T(8,128)(2,1)} async-done(((bf16[128,2048]{1,0:T(8,128)(2,1)}), bf16[1024,2048]{1,0:T(8,128)(2,1)}) %all-gather.8.cloned.1.call-update) | async-done | bytes 4194320 | tf_op jit(solution)/shard_map/all_gather | solution.py:187
  91.2 12.7 %project.1 = (bf16[1024,256]{1,0:T(8,128)(2,1)}, bf16[1024,256]{1,0:T(8,128)(2,1)}, bf16[1024,256]{1,0:T(8,128)(2,1)}, bf16[1024,2048]{1,0:T(8,128)(2,1)}, bf16[...) custom-call(s32[5]{0:T(128)} %stack.89.refs_0_, ...), custom_call_target="tpu_custom_call" | custom-call | flops 3221225472 | bytes 8388608 | tf_op jit(solution)/shard_map/project/pallas_call | solution.py:318
  103.9 8.2 %attend.1 = (bf16[1024,256]{1,0:T(8,128)(2,1)}, f32[1024,128]{1,0:T(8,128)}) custom-call(bf16[1024,256]{1,0:T(8,128)(2,1)} %get-tuple-element.157.q_ref, bf16[1024,256]{1,0:T(8,128)(2,1)} %get-tuple-element.158.k_ref, bf16[1024,256]{1,0:T(8,128)(2,1)} %get-tuple-element.159.v_ref, s32[1024,1]{1,0:T(8,128)} %copy.30.col_ref.seg_col, s32[1,1024]{1,0:T(1,128)} %param.18), custom_call_target="tpu_custom_call" | custom-call | flops 4294967296 | bytes 2097152 | tf_op jit(solution)/shard_map/attend/pallas_call | solution.py:492
  113.8 4.5 all-gather.14.cloned.1.call-done
  122.3 22.2 %collective-permute-done.17.refs_6_ = bf16[256,2048]{1,0:T(8,128)(2,1)S(1)} collective-permute-done((bf16[256,2048]{1,0:T(8,128)(2,1)S(1)}, bf16[256,2048]{1,0:T(8,128)(2,1)S(1)}, u32[]{:S(2)}, u32[]{:S(2)}) %collective-permute-start.17) | collective-permute-done | bytes 1048608 | tf_op jit(solution)/shard_map/ppermute | solution.py:43
  150.2 7.0 %collective-permute-done.18.refs_8_ = bf16[128,2048]{1,0:T(8,128)(2,1)} collective-permute-done((bf16[128,2048]{1,0:T(8,128)(2,1)S(1)}, bf16[128,2048]{1,0:T(8,128)(2,1)}, u32[]{:S(2)}, u32[]{:S(2)}) %collective-permute-start.18) | collective-permute-done | bytes 524320 | tf_op jit(solution)/shard_map/ppermute | solution.py:43
  170.3 18.9 %out_project.1 = (bf16[1024,2048]{1,0:T(8,128)(2,1)}, f32[1024,2048]{1,0:T(8,128)}, bf16[256,2048]{1,0:T(8,128)(2,1)}) custom-call(s32[2]{0:T(128)} %pad_add_fusion.refs_0_, s32[5]{0:T(128)} %stack.83.refs_1_, bf16[8,1024,256]{2,1,0:T(8,128)(2,1)} %bitcast.111, bf16[1024,2048]{1,0:T(8,128)(2,1)} %all-gather.8.cloned.1.call-done.refs_1_.refs_3_, ...), custom_call_target="tpu_custom_call" | custom-call | flops 8589934592 | bytes 16777216 | tf_op jit(solution)/shard_map/out_project/pallas_call | solution.py:542
  193.8 12.4 %gate_up.1 = (f32[1024,704]{1,0:T(8,128)}, f32[1024,704]{1,0:T(8,128)}, bf16[1024,704]{1,0:T(8,128)(2,1)}) custom-call(s32[5]{0:T(128)} %stack.95.refs_0_, bf16[1024,2048]{1,0:T(8,128)(2,1)} %get-tuple-element.204.refs_1_, bf16[704,512]{1,0:T(8,128)(2,1)} %copy-done.19, bf16[704,512]{1,0:T(8,128)(2,1)} %copy-done.25, bf16[704,512]{1,0:T(8,128)(2,1)} %copy-done.26, ...), custom_call_target="tpu_custom_call" | custom-call | flops 5905580032 | bytes 9961472 | tf_op jit(solution)/shard_map/gate_up/pallas_call | solution.py:368
  206.2 6.2 %all-gather.10.cloned.1.call-done.refs_1_ = bf16[1024,2048]{1,0:T(8,128)(2,1)} async-done(((bf16[128,2048]{1,0:T(8,128)(2,1)}), bf16[1024,2048]{1,0:T(8,128)(2,1)}) %all-gather.10.cloned.1.call-update) | async-done | bytes 4194320 | tf_op jit(solution)/shard_map/all_gather | solution.py:187
  212.5 20.7 %feed_back.1 = (bf16[2,1024,704]{2,1,0:T(8,128)(2,1)}, bf16[1024,2048]{1,0:T(8,128)(2,1)}) custom-call(s32[5]{0:T(128)} %stack.95.refs_0_, bf16[1024,2048]{1,0:T(8,128)(2,1)} %all-gather.10.cloned.1.call-done.refs_1_, f32[1024,704]{1,0:T(8,128)} %get-tuple-element.192.refs_2_, f32[1024,704]{1,0:T(8,128)} %get-tuple-element.193.refs_3_, ...), custom_call_target="tpu_custom_call" | custom-call | flops 8858370048 | bytes 18612224 | tf_op jit(solution)/shard_map/feed_back/pallas_call | solution.py:368
  235.1 8.6 %convolution_convert_fusion = bf16[2,704,2048]{2,1,0:T(8,128)(2,1)S(1)} fusion(bf16[2,1024,704]{2,1,0:T(8,128)(2,1)S(1)} %copy-done.41, bf16[1024,2048]{1,0:T(8,128)(2,1)} %get-tuple-element.204.refs_1_), kind=kOutput, calls=%fused_computation | convolution fusion | flops 5908463616 | bytes 12845056 | tf_op jit(solution)/shard_map/gtf,td->gfd/dot_general | solution.py:909
  259.3 14.2 %collective-permute-done.32 = bf16[352,512]{1,0:T(8,128)(2,1)} collective-permute-done((bf16[352,512]{1,0:T(8,128)(2,1)S(1)}, bf16[352,512]{1,0:T(8,128)(2,1)}, u32[]{:S(2)}, u32[]{:S(2)}) %collective-permute-start.32) | collective-permute-done | bytes 360480 | tf_op jit(solution)/shard_map/ppermute | solution.py:43
  274.4 7.3 %reduce-scatter.4.cloned.1.call-done.e_ref = bf16[128,2048]{1,0:T(8,128)(2,1)} async-done(((bf16[1024,2048]{1,0:T(8,128)(2,1)}), bf16[128,2048]{1,0:T(8,128)(2,1)}) %reduce-scatter.4.cloned.1.call-update) | async-done | bytes 524304 | tf_op jit(solution)/shard_map/reduce_scatter | solution.py:191
  295.3 7.9 %down.1 = bf16[1024,2048]{1,0:T(8,128)(2,1)} custom-call(s32[5]{0:T(128)} %stack.95.refs_0_, bf16[1024,704]{1,0:T(8,128)(2,1)} %get-tuple-element.208.refs_1_, bf16[704,512]{1,0:T(8,128)(2,1)} %refs_2_, bf16[704,512]{1,0:T(8,128)(2,1)} %collective-permute-done.26.refs_5_.refs_3_, bf16[704,512]{1,0:T(8,128)(2,1)} %collective-permute-done.27.refs_6_.refs_4_, ...), custom_call_target="tpu_custom_call" | custom-call | flops 2952790016 | bytes 4325376 | tf_op jit(solution)/shard_map/down/pallas_call | solution.py:368
  303.2 18.1 %collective-permute-done.39 = bf16[2,704,512]{2,1,0:T(8,128)(2,1)} collective-permute-done((bf16[2,704,512]{2,1,0:T(8,128)(2,1)}, bf16[2,704,512]{2,1,0:T(8,128)(2,1)}, u32[]{:S(2)}, u32[]{:S(2)}) %collective-permute-start.39) | collective-permute-done | bytes 1441824 | tf_op jit(solution)/shard_map/ppermute | solution.py:43
  324.1 6.6 %all-gather.12.cloned.1.call-done = bf16[1024,2048]{1,0:T(8,128)(2,1)} async-done(((bf16[128,2048]{1,0:T(8,128)(2,1)}), bf16[1024,2048]{1,0:T(8,128)(2,1)}) %all-gather.12.cloned.1.call-update) | async-done | bytes 4194320 | tf_op jit(solution)/shard_map/all_gather | solution.py:187
  333.4 4.3 convolution_convert_fusion.4.g_ref
  337.7 15.5 %attend_back.1 = (bf16[1024,768]{1,0:T(8,128)(2,1)}, f32[1,768]{1,0:T(1,128)}) custom-call(bf16[1024,256]{1,0:T(8,128)(2,1)} %get-tuple-element.157.q_ref, bf16[1024,256]{1,0:T(8,128)(2,1)} %get-tuple-element.158.k_ref, bf16[1024,256]{1,0:T(8,128)(2,1)} %get-tuple-element.159.v_ref, bf16[1024,256]{1,0:T(8,128)(2,1)} %convolution_convert_fusion.4.g_ref, ...), custom_call_target="tpu_custom_call" | custom-call | flops 8589934592 | bytes 4194304 | tf_op jit(solution)/shard_map/attend_back/pallas_call | solution.py:625
  353.2 6.5 %convolution_convert_fusion.1 = bf16[1024,2048]{1,0:T(8,128)(2,1)} fusion(bf16[1024,768]{1,0:T(8,128)(2,1)} %get-tuple-element.219.grad_ref, bf16[2048,768]{1,0:T(8,128)(2,1)S(1)} %copy-done.4), kind=kOutput, calls=%fused_computation.3 | convolution fusion | flops 3223322624 | bytes 8912896 | tf_op jit(solution)/shard_map/dot_general | solution.py:35
  360.7 3.5 convolution_convert_fusion.3
  366.2 9.3 %weights_back.1 = bf16[32,72,768]{2,1,0:T(8,128)(2,1)} custom-call(bf16[1024,2048]{1,0:T(8,128)(2,1)} %get-tuple-element.218.hat_ref, bf16[1024,768]{1,0:T(8,128)(2,1)} %get-tuple-element.219.grad_ref, bf16[2048,768]{1,0:T(8,128)(2,1)} %get-tuple-element.216.w_ref, f32[4,2048]{1,0:T(4,128)} %get-tuple-element.173.norms_ref, ...), custom_call_target="tpu_custom_call" | custom-call | flops 3221225472 | bytes 8388608 | tf_op jit(solution)/shard_map/weights_back/pallas_call | solution.py:671
  383.1 4.1 collective-permute-done.42
  396.4 4.6 fusion.13
  401.0 5.8 %fusion.6 = (f32[2,512,704]{1,2,0:T(8,128)}, f32[2,512,704]{1,2,0:T(8,128)}) fusion(bf16[2,512,704]{1,2,0:T(8,128)(2,1)S(1)} %copy-done.2, f32[2,2,512,704]{2,3,1,0:T(8,128)S(1)} %bitcast.95, f32[]{:T(128)} %bitcast.34, bf16[2,704,512]{2,1,0:T(8,128)(2,1)} %collective-permute-done.39, bf16[2,704,512]{2,1,0:T(8,128)(2,1)} %collective-permute-done.38, ...), kind=kLoop, calls=%fused_computation.10 | loop fusion | flops 14417920 | bytes 17301512 | tf_op jit(solution)/shard_map/add | solution.py:780
  406.8 3.9 collective-permute-done.45
  414.8 4.1 collective-permute-start.46
  429.6 15.0 %collective-permute-done.48 = bf16[1,72,768]{2,1,0:T(8,128)(2,1)S(1)} collective-permute-done((bf16[1,72,768]{2,1,0:T(8,128)(2,1)S(1)}, bf16[1,72,768]{2,1,0:T(8,128)(2,1)S(1)}, u32[]{:S(2)}, u32[]{:S(2)}) %collective-permute-start.48) | collective-permute-done | bytes 110624 | tf_op jit(solution)/shard_map/ppermute | solution.py:169
  451.0 5.4 %finish.1 = (f32[64,6144]{1,0:T(8,128)}, f32[64,6144]{1,0:T(8,128)}) custom-call(bf16[8,72,768]{2,1,0:T(8,128)(2,1)} %copy-done.3, bf16[64,6144]{1,0:T(8,128)(2,1)} %w_ref.3, f32[2,64,6144]{2,1,0:T(8,128)} %moment_ref.1), custom_call_target="tpu_custom_call" | custom-call | tf_op jit(solution)/shard_map/finish/pallas_call | solution.py:811
  (281 shorter events, 150.8 us)
Async XLA Ops:
  7.2 80.2 %all-gather.8.cloned.1.call-start = ((), (), s32[]{:S(2)}) async-start(), calls=%async_computation.3 | async-start | bytes 4718592 | tf_op jit(solution)/shard_map/all_gather | solution.py:187
  12.8 21.2 %collective-permute-start.3 = (bf16[704,512]{1,0:T(8,128)(2,1)S(1)}, bf16[704,512]{1,0:T(8,128)(2,1)S(1)}, u32[]{:S(2)}, u32[]{:S(2)}) collective-permute-start(bf16[704,512]{1,0:T(8,128)(2,1)S(1)} %get-tuple-element.128.refs_2_.refs_9_), channel_id=1, source_target_pairs={{0,8},{8,0},{16,24},{24,16},{1,9},{9,1},{17,25},{25,17},{2,10},{10... | collective-permute-start | bytes 2162696 | tf_op jit(solution)/shard_map/ppermute | solution.py:43
  14.0 21.8 %collective-permute-start.4 = (bf16[704,512]{1,0:T(8,128)(2,1)S(1)}, bf16[704,512]{1,0:T(8,128)(2,1)S(1)}, u32[]{:S(2)}, u32[]{:S(2)}) collective-permute-start(bf16[704,512]{1,0:T(8,128)(2,1)S(1)} %get-tuple-element.128.refs_2_.refs_9_), channel_id=1, source_target_pairs={{0,16},{8,24},{16,0},{24,8},{1,17},{9,25},{17,1},{25,9},{2,18},{10... | collective-permute-start | bytes 2162696 | tf_op jit(solution)/shard_map/ppermute | solution.py:43
  40.8 77.6 %all-gather.14.cloned.1.call-start = ((), (), s32[]{:S(2)}) async-start(), calls=%async_computation.9 | async-start | bytes 2359296 | tf_op jit(solution)/shard_map/all_gather | solution.py:870
  40.8 21.3 %collective-permute-start.10 = (bf16[8,72,768]{2,1,0:T(8,128)(2,1)S(1)}, bf16[8,72,768]{2,1,0:T(8,128)(2,1)S(1)}, u32[]{:S(2)}, u32[]{:S(2)}) collective-permute-start(bf16[8,72,768]{2,1,0:T(8,128)(2,1)S(1)} %constant_dynamic-update-slice_fusion.7.refs_5_), channel_id=1, source_target_pairs={{0,16},{8,24},{16,0},{24,8},{1,17},{9,25},{17,1},{25,9},{2,18},{10... | collective-permute-start | bytes 2654216 | tf_op jit(solution)/shard_map/ppermute | solution.py:43
  41.1 21.5 %collective-permute-start.9 = (bf16[8,72,768]{2,1,0:T(8,128)(2,1)S(1)}, bf16[8,72,768]{2,1,0:T(8,128)(2,1)S(1)}, u32[]{:S(2)}, u32[]{:S(2)}) collective-permute-start(bf16[8,72,768]{2,1,0:T(8,128)(2,1)S(1)} %constant_dynamic-update-slice_fusion.7.refs_5_), channel_id=1, source_target_pairs={{0,8},{8,0},{16,24},{24,16},{1,9},{9,1},{17,25},{25,17},{2,10},{10... | collective-permute-start | bytes 2654216 | tf_op jit(solution)/shard_map/ppermute | solution.py:43
  87.4 77.7 %all-gather.16.cloned.1.call-start = ((), (), s32[]{:S(2)}) async-start(), calls=%async_computation.10 | async-start | bytes 4718592 | tf_op jit(solution)/shard_map/all_gather | solution.py:876
  87.6 24.5 %collective-permute-start.13 = (bf16[704,512]{1,0:T(8,128)(2,1)S(1)}, bf16[704,512]{1,0:T(8,128)(2,1)}, u32[]{:S(2)}, u32[]{:S(2)}) collective-permute-start(bf16[704,512]{1,0:T(8,128)(2,1)S(1)} %get-tuple-element.147.refs_7_.refs_14_), channel_id=1, source_target_pairs={{0,8},{8,0},{16,24},{24,16},{1,9},{9,1},{17,25},{25,17},{2,10},{10... | collective-permute-start | bytes 2162696 | tf_op jit(solution)/shard_map/ppermute | solution.py:43
  88.9 23.2 %collective-permute-start.14 = (bf16[704,512]{1,0:T(8,128)(2,1)S(1)}, bf16[704,512]{1,0:T(8,128)(2,1)}, u32[]{:S(2)}, u32[]{:S(2)}) collective-permute-start(bf16[704,512]{1,0:T(8,128)(2,1)S(1)} %get-tuple-element.147.refs_7_.refs_14_), channel_id=1, source_target_pairs={{0,16},{8,24},{16,0},{24,8},{1,17},{9,25},{17,1},{25,9},{2,18},{10... | collective-permute-start | bytes 2162696 | tf_op jit(solution)/shard_map/ppermute | solution.py:43
  90.7 23.2 %collective-permute-start.15 = (bf16[704,256]{1,0:T(8,128)(2,1)S(1)}, bf16[704,256]{1,0:T(8,128)(2,1)}, u32[]{:S(2)}, u32[]{:S(2)}) collective-permute-start(bf16[704,256]{1,0:T(8,128)(2,1)S(1)} %slice.163), channel_id=1, source_target_pairs={{0,16},{8,24},{16,0},{24,8},{1,17},{9,25},{17,1},{25,9},{2,18},{10... | collective-permute-start | bytes 1081352 | tf_op jit(solution)/shard_map/ppermute | solution.py:43
  90.9 22.9 %collective-permute-start.16 = (bf16[704,256]{1,0:T(8,128)(2,1)S(1)}, bf16[704,256]{1,0:T(8,128)(2,1)}, u32[]{:S(2)}, u32[]{:S(2)}) collective-permute-start(bf16[704,256]{1,0:T(8,128)(2,1)S(1)} %slice.164), channel_id=1, source_target_pairs={{0,8},{8,0},{16,24},{24,16},{1,9},{9,1},{17,25},{25,17},{2,10},{10... | collective-permute-start | bytes 1081352 | tf_op jit(solution)/shard_map/ppermute | solution.py:43
  118.4 94.1 %all-gather.10.cloned.1.call-start = ((), (), s32[]{:S(2)}) async-start(), calls=%async_computation.4 | async-start | bytes 4718592 | tf_op jit(solution)/shard_map/all_gather | solution.py:187
  119.8 24.7 %collective-permute-start.17 = (bf16[256,2048]{1,0:T(8,128)(2,1)S(1)}, bf16[256,2048]{1,0:T(8,128)(2,1)S(1)}, u32[]{:S(2)}, u32[]{:S(2)}) collective-permute-start(bf16[256,2048]{1,0:T(8,128)(2,1)S(1)} %bitcast.102), channel_id=1, source_target_pairs={{0,8},{8,0},{16,24},{24,16},{1,9},{9,1},{17,25},{25,17},{2,10},{10... | collective-permute-start | bytes 3145736 | tf_op jit(solution)/shard_map/ppermute | solution.py:43
  121.1 24.7 %collective-permute-start.19 = (bf16[256,2048]{1,0:T(8,128)(2,1)S(1)}, bf16[256,2048]{1,0:T(8,128)(2,1)}, u32[]{:S(2)}, u32[]{:S(2)}) collective-permute-start(bf16[256,2048]{1,0:T(8,128)(2,1)S(1)} %bitcast.103), channel_id=1, source_target_pairs={{0,16},{8,24},{16,0},{24,8},{1,17},{9,25},{17,1},{25,9},{2,18},{10... | collective-permute-start | bytes 3145736 | tf_op jit(solution)/shard_map/ppermute | solution.py:43
  165.1 116.6 %reduce-scatter.4.cloned.1.call-start = ((), (), s32[]{:S(2)}) async-start(), calls=%async_computation.5 | async-start | bytes 4718592 | tf_op jit(solution)/shard_map/reduce_scatter | solution.py:191
  167.4 21.9 %collective-permute-start.26 = (bf16[704,512]{1,0:T(8,128)(2,1)S(1)}, bf16[704,512]{1,0:T(8,128)(2,1)}, u32[]{:S(2)}, u32[]{:S(2)}) collective-permute-start(bf16[704,512]{1,0:T(8,128)(2,1)S(1)} %copy-done.16), channel_id=1, source_target_pairs={{0,8},{8,0},{16,24},{24,16},{1,9},{9,1},{17,25},{25,17},{2,10},{10... | collective-permute-start | bytes 2162696 | tf_op jit(solution)/shard_map/ppermute | solution.py:43
  169.8 24.0 %collective-permute-start.28 = (bf16[704,256]{1,0:T(8,128)(2,1)S(1)}, bf16[704,256]{1,0:T(8,128)(2,1)}, u32[]{:S(2)}, u32[]{:S(2)}) collective-permute-start(bf16[704,256]{1,0:T(8,128)(2,1)S(1)} %slice.167), channel_id=1, source_target_pairs={{0,16},{8,24},{16,0},{24,8},{1,17},{9,25},{17,1},{25,9},{2,18},{10... | collective-permute-start | bytes 1081352 | tf_op jit(solution)/shard_map/ppermute | solution.py:43
  170.0 23.8 %collective-permute-start.29 = (bf16[704,256]{1,0:T(8,128)(2,1)S(1)}, bf16[704,256]{1,0:T(8,128)(2,1)}, u32[]{:S(2)}, u32[]{:S(2)}) collective-permute-start(bf16[704,256]{1,0:T(8,128)(2,1)S(1)} %slice.168), channel_id=1, source_target_pairs={{0,8},{8,0},{16,24},{24,16},{1,9},{9,1},{17,25},{25,17},{2,10},{10... | collective-permute-start | bytes 1081352 | tf_op jit(solution)/shard_map/ppermute | solution.py:43
  233.2 97.5 %all-gather.12.cloned.1.call-start = ((), (), s32[]{:S(2)}) async-start(), calls=%async_computation.6 | async-start | bytes 4718592 | tf_op jit(solution)/shard_map/all_gather | solution.py:187
  248.0 33.7 %collective-permute-start.36 = (bf16[1,704,512]{2,1,0:T(8,128)(2,1)}, bf16[1,704,512]{2,1,0:T(8,128)(2,1)}, u32[]{:S(2)}, u32[]{:S(2)}) collective-permute-start(bf16[1,704,512]{2,1,0:T(8,128)(2,1)} %get-tuple-element.249), channel_id=1, source_target_pairs={{0,8},{8,0},{16,24},{24,16},{1,9},{9,1},{17,25},{25,17},{2,10},{10... | collective-permute-start | bytes 2162696 | tf_op jit(solution)/shard_map/ppermute | solution.py:43
  249.2 32.5 %collective-permute-start.37 = (bf16[1,704,512]{2,1,0:T(8,128)(2,1)}, bf16[1,704,512]{2,1,0:T(8,128)(2,1)}, u32[]{:S(2)}, u32[]{:S(2)}) collective-permute-start(bf16[1,704,512]{2,1,0:T(8,128)(2,1)} %get-tuple-element.250), channel_id=1, source_target_pairs={{0,16},{8,24},{16,0},{24,8},{1,17},{9,25},{17,1},{25,9},{2,18},{10... | collective-permute-start | bytes 2162696 | tf_op jit(solution)/shard_map/ppermute | solution.py:43
  284.9 127.9 %reduce-scatter.6.cloned.1.call-start = ((), (), s32[]{:S(2)}) async-start(), calls=%async_computation.7 | async-start | bytes 4718592 | tf_op jit(solution)/shard_map/reduce_scatter | solution.py:191
  288.5 32.8 %collective-permute-start.39 = (bf16[2,704,512]{2,1,0:T(8,128)(2,1)}, bf16[2,704,512]{2,1,0:T(8,128)(2,1)}, u32[]{:S(2)}, u32[]{:S(2)}) collective-permute-start(bf16[2,704,512]{2,1,0:T(8,128)(2,1)} %pad_maximum_fusion.1), channel_id=1, source_target_pairs={{0,8},{8,0},{16,24},{24,16},{1,9},{9,1},{17,25},{25,17},{2,10},{10... | collective-permute-start | bytes 4325384 | tf_op jit(solution)/shard_map/ppermute | solution.py:43
  290.9 33.2 %collective-permute-start.38 = (bf16[2,704,512]{2,1,0:T(8,128)(2,1)}, bf16[2,704,512]{2,1,0:T(8,128)(2,1)}, u32[]{:S(2)}, u32[]{:S(2)}) collective-permute-start(bf16[2,704,512]{2,1,0:T(8,128)(2,1)} %pad_maximum_fusion), channel_id=1, source_target_pairs={{0,16},{8,24},{16,0},{24,8},{1,17},{9,25},{17,1},{25,9},{2,18},{10... | collective-permute-start | bytes 4325384 | tf_op jit(solution)/shard_map/ppermute | solution.py:43
  330.8 126.7 %reduce-scatter.8.cloned.1.call-start = ((), (), s32[]{:S(2)}) async-start(), calls=%async_computation.8 | async-start | bytes 4718592 | tf_op jit(solution)/shard_map/reduce_scatter | solution.py:191
  331.0 22.2 %collective-permute-start.35 = (bf16[704,512]{1,0:T(8,128)(2,1)}, bf16[704,512]{1,0:T(8,128)(2,1)}, u32[]{:S(2)}, u32[]{:S(2)}) collective-permute-start(bf16[704,512]{1,0:T(8,128)(2,1)} %pad_maximum_fusion.5), channel_id=1, source_target_pairs={{0,8},{8,0},{16,24},{24,16},{1,9},{9,1},{17,25},{25,17},{2,10},{10... | collective-permute-start | bytes 2162696 | tf_op jit(solution)/shard_map/ppermute | solution.py:43
  389.6 21.2 %collective-permute-start.45 = (bf16[8,72,768]{2,1,0:T(8,128)(2,1)S(1)}, bf16[8,72,768]{2,1,0:T(8,128)(2,1)S(1)}, u32[]{:S(2)}, u32[]{:S(2)}) collective-permute-start(bf16[8,72,768]{2,1,0:T(8,128)(2,1)S(1)} %pad_maximum_fusion.3), channel_id=1, source_target_pairs={{0,8},{8,0},{16,24},{24,16},{1,9},{9,1},{17,25},{25,17},{2,10},{10... | collective-permute-start | bytes 2654216 | tf_op jit(solution)/shard_map/ppermute | solution.py:43
  390.0 22.7 %collective-permute-start.43 = (bf16[8,72,768]{2,1,0:T(8,128)(2,1)S(1)}, bf16[8,72,768]{2,1,0:T(8,128)(2,1)}, u32[]{:S(2)}, u32[]{:S(2)}) collective-permute-start(bf16[8,72,768]{2,1,0:T(8,128)(2,1)S(1)} %pad_maximum_fusion.2), channel_id=1, source_target_pairs={{0,16},{8,24},{16,0},{24,8},{1,17},{9,25},{17,1},{25,9},{2,18},{10... | collective-permute-start | bytes 2654216 | tf_op jit(solution)/shard_map/ppermute | solution.py:43
  419.1 25.6 %collective-permute-start.48 = (bf16[1,72,768]{2,1,0:T(8,128)(2,1)S(1)}, bf16[1,72,768]{2,1,0:T(8,128)(2,1)S(1)}, u32[]{:S(2)}, u32[]{:S(2)}) collective-permute-start(bf16[1,72,768]{2,1,0:T(8,128)(2,1)S(1)} %get-tuple-element.278), channel_id=1, source_target_pairs={{0,3},{1,4},{2,5},{3,6},{4,7},{5,0},{6,1},{7,2},{8,11},{9,12},{10,... | collective-permute-start | bytes 331784 | tf_op jit(solution)/shard_map/ppermute | solution.py:169
  422.0 25.9 %collective-permute-start.49 = (bf16[1,72,768]{2,1,0:T(8,128)(2,1)S(1)}, bf16[1,72,768]{2,1,0:T(8,128)(2,1)S(1)}, u32[]{:S(2)}, u32[]{:S(2)}) collective-permute-start(bf16[1,72,768]{2,1,0:T(8,128)(2,1)S(1)} %get-tuple-element.277), channel_id=1, source_target_pairs={{0,4},{1,5},{2,6},{3,7},{4,0},{5,1},{6,2},{7,3},{8,12},{9,13},{10,... | collective-permute-start | bytes 331784 | tf_op jit(solution)/shard_map/ppermute | solution.py:169
  422.0 25.9 %collective-permute-start.50 = (bf16[1,72,768]{2,1,0:T(8,128)(2,1)S(1)}, bf16[1,72,768]{2,1,0:T(8,128)(2,1)S(1)}, u32[]{:S(2)}, u32[]{:S(2)}) collective-permute-start(bf16[1,72,768]{2,1,0:T(8,128)(2,1)S(1)} %get-tuple-element.276), channel_id=1, source_target_pairs={{0,5},{1,6},{2,7},{3,0},{4,1},{5,2},{6,3},{7,4},{8,13},{9,14},{10,... | collective-permute-start | bytes 331784 | tf_op jit(solution)/shard_map/ppermute | solution.py:169
  425.8 24.2 %collective-permute-start.51 = (bf16[1,72,768]{2,1,0:T(8,128)(2,1)S(1)}, bf16[1,72,768]{2,1,0:T(8,128)(2,1)S(1)}, u32[]{:S(2)}, u32[]{:S(2)}) collective-permute-start(bf16[1,72,768]{2,1,0:T(8,128)(2,1)S(1)} %get-tuple-element.275), channel_id=1, source_target_pairs={{0,6},{1,7},{2,0},{3,1},{4,2},{5,3},{6,4},{7,5},{8,14},{9,15},{10,... | collective-permute-start | bytes 331784 | tf_op jit(solution)/shard_map/ppermute | solution.py:169
  (75 other events, 983.2 us)
Sparse Core Ops, SparseCore 0:
  40.9 46.4 all-gather.7
  89.0 29.3 all-gather.13
  119.9 45.1 all-gather.15
  166.5 45.8 all-gather.9
  233.3 48.3 reduce-scatter.3
  285.0 45.6 all-gather.11
  333.0 48.3 reduce-scatter.5
  383.7 65.6 reduce-scatter.7
